TPU v7x, 32 devices: a whole 2x2x4 slice. The times are simulated.
32 devices in a mesh: dp: 2 (over x), ctx: 4 (over y, core), tensor: 4 (over z).
Axes of the slice: x: 2, y: 2, z: 4, core: 2. Of those that a mesh axis runs over, the one named last changes fastest.
Arguments:
- tokens: bfloat16 [2, 4096, 768], P('dp', 'ctx'), may hold values from -6 to 6
- cotangent: bfloat16 [2, 4096, 768], P('dp', 'ctx'), may hold values from -6 to 6
- segments: int32 [2, 2048], P('dp'), may hold values from 0 to 11, never falling along the last dimension, each value on 1 to 256 neighbouring positions
- pairing: int32 [12, 2], replicated, may hold values from 0 to 1, each once within a row
- project: bfloat16 [768, 3, 768], P('dp', None, 'tensor'), may hold values from -0.21875 to 0.21875
- offsets: bfloat16 [2, 768], P(None, ('tensor', 'dp')), may hold values from -3 to 3
- combine: bfloat16 [768, 768], P('tensor', 'dp'), may hold values from -6 to 6
- baseline: bfloat16 [768], P('dp'), may hold values from -3 to 3
- scaling: bfloat16 [768], P('dp'), may hold values from 0.25 to 1.75
- shifting: bfloat16 [768], P('dp'), may hold values from -3 to 3
- expand: bfloat16 [768, 3072], P('dp', 'tensor'), may hold values from -0.21875 to 0.21875
- thresholds: bfloat16 [3072], P(('tensor', 'dp')), may hold values from -3 to 3
- shrink: bfloat16 [3072, 768], P('tensor', 'dp'), may hold values from -0.109375 to 0.109375
- settling: bfloat16 [768], P('dp'), may hold values from -3 to 3
- rescaling: bfloat16 [768], P('dp'), may hold values from 0.25 to 1.75
- reshifting: bfloat16 [768], P('dp'), may hold values from -3 to 3
Outputs:
- layer_out: bfloat16 [2, 4096, 768], P('dp', 'ctx')
- grad_tokens: float32 [2, 4096, 768], P('dp', 'ctx')
- grad_project: float32 [768, 3, 768], P('dp', None, 'tensor')
- grad_offsets: float32 [2, 768], P(None, ('tensor', 'dp'))
- grad_combine: float32 [768, 768], P('tensor', 'dp')
- grad_baseline: float32 [768], P('dp')
- grad_scaling: float32 [768], P('dp')
- grad_shifting: float32 [768], P('dp')
- grad_expand: float32 [768, 3072], P('dp', 'tensor')
- grad_thresholds: float32 [3072], P(('tensor', 'dp'))
- grad_shrink: float32 [3072, 768], P('tensor', 'dp')
- grad_settling: float32 [768], P('dp')
- grad_rescaling: float32 [768], P('dp')
- grad_reshifting: float32 [768], P('dp')
Inputs may be any that keep to these rules, and one draw needn't show every extreme that they name: `segments`: along a group's row the numbers never fall, every number of 0 to 11 appears, each continuation has 1 to 256 tokens and one has exactly 256. `pairing`: each row is a permutation of 0 and 1.
All inputs are finite; a program needn't handle non-finite values.
Results may differ from a plain program's by a relative error of at most 0.018.
Values may be sent and summed in bfloat16 or wider, within the bound.
No kernel may reach another device: no remote copies, remote signals or barrier semaphores. Data moves between devices by JAX's collectives and lax.ppermute only.
A program may use at most 192 MiB of HBM per device.

v0:
```python
import jax
import jax.numpy as jnp
from jax import lax
from jax.sharding import PartitionSpec as P

P_SIZE = 2048
LMAX = 256
CT = 2048
QB = 512
B = 1152
WIN = 1024


EPS = 1e-06
NEG = -1e30


def layer_norm(value, gain, shift):
    mean = jnp.mean(value, axis=-1, keepdims=True)
    centred = value - mean
    spread = jnp.mean(centred * centred, axis=-1, keepdims=True)
    return centred * lax.rsqrt(spread + EPS) * gain + shift


def exact_gelu(value):
    return jax.nn.gelu(value, approximate=False)


def contract_rows(left, right):
    return lax.dot_general(
        left, right, (((0,), (0,)), ((), ())), preferred_element_type=jnp.float32
    )


def contract_cols(left, right):
    return lax.dot_general(
        left, right, (((1,), (1,)), ((), ())), preferred_element_type=jnp.float32
    )


def padded_segments(seg_row):
    return jnp.concatenate(
        [
            jnp.full((LMAX,), -3, jnp.int32),
            jnp.full((P_SIZE,), -1, jnp.int32),
            seg_row,
            jnp.full((LMAX,), -2, jnp.int32),
        ]
    )


def prompt_mask(start, pair_local):
    positions = start + jnp.arange(QB, dtype=jnp.int32)
    later = (positions >= B).astype(jnp.int32)
    paired = jnp.where(later[None, :] == 1, pair_local[:, 1:2], pair_local[:, 0:1])
    key_blocks = (jnp.arange(P_SIZE, dtype=jnp.int32) >= B).astype(jnp.int32)
    return key_blocks[None, None, :] == paired[:, :, None]


def near_mask(start, seg_pad, window_global, pair_local):
    own_segs = lax.dynamic_slice_in_dim(seg_pad, start + LMAX, QB, 0)
    window_segs = lax.dynamic_slice_in_dim(seg_pad, window_global + LMAX, WIN, 0)
    same = own_segs[:, None] == window_segs[None, :]
    return same[None, :, :] & (pair_local[:, 1] == 1)[:, None, None]


def window_place(start):
    window_local = jnp.clip(start - P_SIZE - LMAX, 0, CT - WIN)
    return (window_local, P_SIZE + window_local)


def split_pairs(pairs, heads):
    count, _, width = pairs.shape
    both = pairs.reshape(count, 2, heads, width // heads)
    return (both[:, 0], both[:, 1])


def tile_forward(query_tile, keys, values, mask):
    scale = query_tile.shape[2] ** (-0.5)
    raw = jnp.einsum("qhd,khd->hqk", query_tile, keys, preferred_element_type=jnp.float32) * scale
    scores = jnp.where(mask, raw, NEG)
    peak = jnp.max(scores, axis=2, keepdims=True)
    expo = jnp.exp(scores - peak)
    total = jnp.sum(expo, axis=2, keepdims=True)
    weights = (expo / total).astype(jnp.bfloat16)
    mixed = jnp.einsum("hqk,khd->qhd", weights, values, preferred_element_type=jnp.float32)
    return (mixed, peak[:, :, 0] + jnp.log(total[:, :, 0]))


def tile_backward(query_tile, keys, values, mask, logsum, grad_tile):
    scale = query_tile.shape[2] ** (-0.5)
    raw = jnp.einsum("qhd,khd->hqk", query_tile, keys, preferred_element_type=jnp.float32) * scale
    scores = jnp.where(mask, raw, NEG)
    probs = jnp.exp(scores - logsum[:, :, None])
    prob_grads = jnp.einsum("qhd,khd->hqk", grad_tile, values, preferred_element_type=jnp.float32)
    score_grads = (
        probs * (prob_grads - jnp.sum(probs * prob_grads, axis=2, keepdims=True))
    ).astype(jnp.bfloat16)
    query_grad = (
        jnp.einsum("hqk,khd->qhd", score_grads, keys, preferred_element_type=jnp.float32) * scale
    )
    key_grad = (
        jnp.einsum("hqk,qhd->khd", score_grads, query_tile, preferred_element_type=jnp.float32)
        * scale
    )
    value_grad = jnp.einsum(
        "hqk,qhd->khd", probs.astype(jnp.bfloat16), grad_tile, preferred_element_type=jnp.float32
    )
    return (query_grad, key_grad, value_grad)


def attend_forward(query_group, prompt_pairs, window_source, seg_pad, pair_local, offset):
    rows, width = query_group.shape
    heads = pair_local.shape[0]
    prompt_keys, prompt_values = split_pairs(prompt_pairs, heads)

    def one_tile(index):
        start = offset + index * QB
        query_tile = lax.dynamic_slice_in_dim(query_group, index * QB, QB, 0).reshape(
            QB, heads, width // heads
        )
        first_mask = prompt_mask(start, pair_local)
        window_local, window_global = window_place(start)

        def prompt_part():
            return tile_forward(query_tile, prompt_keys, prompt_values, first_mask)

        def joint_part():
            near_keys, near_values = split_pairs(
                lax.dynamic_slice_in_dim(window_source, window_local, WIN, 0), heads
            )
            mask = jnp.concatenate(
                [first_mask, near_mask(start, seg_pad, window_global, pair_local)], axis=2
            )
            return tile_forward(
                query_tile,
                jnp.concatenate([prompt_keys, near_keys]),
                jnp.concatenate([prompt_values, near_values]),
                mask,
            )

        mixed, logsum = lax.cond(start + QB <= P_SIZE, prompt_part, joint_part)
        return (mixed.reshape(QB, width), logsum)

    mixed, logsum = lax.map(one_tile, jnp.arange(rows // QB, dtype=jnp.int32))
    return (mixed.reshape(rows, width), logsum)


def attend_backward(
    query_group, prompt_pairs, window_source, seg_pad, logsum, grad_group, pair_local, offset
):
    rows, width = query_group.shape
    heads = pair_local.shape[0]
    prompt_keys, prompt_values = split_pairs(prompt_pairs, heads)

    def one_tile(carry, index):
        prompt_acc, window_acc = carry
        start = offset + index * QB
        query_tile = lax.dynamic_slice_in_dim(query_group, index * QB, QB, 0).reshape(
            QB, heads, width // heads
        )
        grad_tile = lax.dynamic_slice_in_dim(grad_group, index * QB, QB, 0).reshape(
            QB, heads, width // heads
        )
        first_mask = prompt_mask(start, pair_local)
        window_local, window_global = window_place(start)

        def prompt_part():
            query_grad, key_grad, value_grad = tile_backward(
                query_tile, prompt_keys, prompt_values, first_mask, logsum[index], grad_tile
            )
            both = jnp.stack([key_grad, value_grad], axis=1).reshape(P_SIZE, 2, width)
            return (query_grad, both, jnp.zeros((WIN, 2, width), jnp.float32))

        def joint_part():
            near_keys, near_values = split_pairs(
                lax.dynamic_slice_in_dim(window_source, window_local, WIN, 0), heads
            )
            mask = jnp.concatenate(
                [first_mask, near_mask(start, seg_pad, window_global, pair_local)], axis=2
            )
            query_grad, key_grad, value_grad = tile_backward(
                query_tile,
                jnp.concatenate([prompt_keys, near_keys]),
                jnp.concatenate([prompt_values, near_values]),
                mask,
                logsum[index],
                grad_tile,
            )
            both = jnp.stack([key_grad, value_grad], axis=1).reshape(P_SIZE + WIN, 2, width)
            return (query_grad, both[:P_SIZE], both[P_SIZE:])

        query_grad, prompt_grad, near_grad = lax.cond(start + QB <= P_SIZE, prompt_part, joint_part)
        prompt_acc = prompt_acc + prompt_grad
        current = lax.dynamic_slice_in_dim(window_acc, window_local, WIN, 0)
        window_acc = lax.dynamic_update_slice_in_dim(
            window_acc, current + near_grad, window_local, 0
        )
        return ((prompt_acc, window_acc), query_grad.reshape(QB, width))

    start_carry = (
        jnp.zeros((P_SIZE, 2, width), jnp.float32),
        jnp.zeros((window_source.shape[0], 2, width), jnp.float32),
    )
    (prompt_acc, window_acc), query_grads = lax.scan(
        one_tile, start_carry, jnp.arange(rows // QB, dtype=jnp.int32)
    )
    return (query_grads.reshape(rows, width), prompt_acc, window_acc)


def on_device(
    tokens,
    cotangent,
    segments,
    pairing,
    project,
    offsets,
    combine,
    baseline,
    scaling,
    shifting,
    expand,
    thresholds,
    shrink,
    settling,
    rescaling,
    reshifting,
):
    groups, rows, width = tokens.shape
    heads_local = pairing.shape[0] // lax.axis_size("tensor")
    pair_local = lax.dynamic_slice_in_dim(
        pairing, lax.axis_index("tensor") * heads_local, heads_local, 0
    )
    offset = lax.axis_index("ctx") * rows
    gathered = (
        lax.all_gather(project, "dp", axis=0, tiled=True),
        lax.all_gather(offsets, "dp", axis=1, tiled=True),
        lax.all_gather(combine, "dp", axis=1, tiled=True),
        lax.all_gather(baseline, "dp", axis=0, tiled=True),
        lax.all_gather(scaling, "dp", axis=0, tiled=True),
        lax.all_gather(shifting, "dp", axis=0, tiled=True),
        lax.all_gather(expand, "dp", axis=0, tiled=True),
        lax.all_gather(thresholds, "dp", axis=0, tiled=True),
        lax.all_gather(shrink, "dp", axis=1, tiled=True),
        lax.all_gather(settling, "dp", axis=0, tiled=True),
        lax.all_gather(rescaling, "dp", axis=0, tiled=True),
        lax.all_gather(reshifting, "dp", axis=0, tiled=True),
    )
    (
        project_all,
        offsets_all,
        combine_all,
        baseline_all,
        scaling_all,
        shifting_all,
        expand_all,
        thresholds_all,
        shrink_all,
        settling_all,
        rescaling_all,
        reshifting_all,
    ) = gathered
    local_width = project_all.shape[2]
    tokens_flat = tokens.reshape(groups * rows, width)
    project_flat = project_all.reshape(width, 3 * local_width)
    joined = jnp.dot(tokens_flat, project_flat, preferred_element_type=jnp.float32).reshape(
        groups, rows, 3, local_width
    )
    shifts = offsets_all.astype(jnp.float32)
    queries = (joined[:, :, 0] + shifts[0]).astype(jnp.bfloat16)
    pairs = jnp.stack([joined[:, :, 1], joined[:, :, 2] + shifts[1]], axis=2).astype(jnp.bfloat16)
    seg_pads = jax.vmap(padded_segments)(segments)
    context = lax.all_gather(pairs, "ctx", axis=1, tiled=True)
    prompt_pairs = context[:, :P_SIZE]
    window_source = context[:, P_SIZE:]

    def forward_group(item):
        return attend_forward(item[0], item[1], item[2], item[3], pair_local, offset)

    mixed, logsum = lax.map(forward_group, (queries, prompt_pairs, window_source, seg_pads))
    mixed_low = mixed.reshape(groups * rows, local_width).astype(jnp.bfloat16)
    attended = lax.psum(
        jnp.dot(mixed_low, combine_all, preferred_element_type=jnp.float32), "tensor"
    )
    first = tokens_flat.astype(jnp.float32) + attended + baseline_all.astype(jnp.float32)
    normed, first_back = jax.vjp(
        layer_norm, first, scaling_all.astype(jnp.float32), shifting_all.astype(jnp.float32)
    )
    normed_low = normed.astype(jnp.bfloat16)
    inner = jnp.dot(
        normed_low, expand_all, preferred_element_type=jnp.float32
    ) + thresholds_all.astype(jnp.float32)
    active, gelu_back = jax.vjp(exact_gelu, inner)
    active_low = active.astype(jnp.bfloat16)
    feed = lax.psum(jnp.dot(active_low, shrink_all, preferred_element_type=jnp.float32), "tensor")
    second = normed + feed + settling_all.astype(jnp.float32)
    result, second_back = jax.vjp(
        layer_norm, second, rescaling_all.astype(jnp.float32), reshifting_all.astype(jnp.float32)
    )
    grad_second, grad_rescaling, grad_reshifting = second_back(
        cotangent.reshape(groups * rows, width).astype(jnp.float32)
    )
    grad_settling = jnp.sum(grad_second, axis=0)
    feed_back = grad_second.astype(jnp.bfloat16)
    grad_shrink = contract_rows(active_low, feed_back)
    inner_back = gelu_back(contract_cols(feed_back, shrink_all))[0].astype(jnp.bfloat16)
    grad_thresholds = jnp.sum(inner_back.astype(jnp.float32), axis=0)
    grad_expand = contract_rows(normed_low, inner_back)
    grad_normed = grad_second + lax.psum(contract_cols(inner_back, expand_all), "tensor")
    grad_first, grad_scaling, grad_shifting = first_back(grad_normed)
    grad_baseline = jnp.sum(grad_first, axis=0)
    attended_back = grad_first.astype(jnp.bfloat16)
    grad_combine = contract_rows(mixed_low, attended_back)
    mixed_back = (
        contract_cols(attended_back, combine_all)
        .astype(jnp.bfloat16)
        .reshape(groups, rows, local_width)
    )

    def backward_group(item):
        return attend_backward(
            item[0], item[1], item[2], item[3], item[4], item[5], pair_local, offset
        )

    query_grads, prompt_grads, window_grads = lax.map(
        backward_group, (queries, prompt_pairs, window_source, seg_pads, logsum, mixed_back)
    )
    pair_grads = lax.psum_scatter(
        jnp.concatenate([prompt_grads, window_grads], axis=1).astype(jnp.bfloat16),
        "ctx",
        scatter_dimension=1,
        tiled=True,
    )
    query_back = query_grads.astype(jnp.bfloat16)
    grad_offsets = jnp.stack(
        [
            jnp.sum(query_back.astype(jnp.float32), axis=(0, 1)),
            jnp.sum(pair_grads[:, :, 1].astype(jnp.float32), axis=(0, 1)),
        ]
    )
    joined_back = jnp.concatenate([query_back[:, :, None], pair_grads], axis=2).reshape(
        groups * rows, 3 * local_width
    )
    grad_project = contract_rows(tokens_flat, joined_back).reshape(width, 3, local_width)
    input_back = lax.psum(
        contract_cols(joined_back, project_flat).astype(jnp.bfloat16), "tensor"
    ).astype(jnp.float32)
    grad_tokens = (grad_first + input_back).reshape(groups, rows, width)
    summed = (
        lax.psum(grad_project.astype(jnp.bfloat16), "ctx").astype(jnp.float32),
        lax.psum(grad_offsets.astype(jnp.bfloat16), "ctx").astype(jnp.float32),
        lax.psum(grad_combine.astype(jnp.bfloat16), "ctx").astype(jnp.float32),
        lax.psum(grad_baseline.astype(jnp.bfloat16), "ctx").astype(jnp.float32),
        lax.psum(grad_scaling.astype(jnp.bfloat16), "ctx").astype(jnp.float32),
        lax.psum(grad_shifting.astype(jnp.bfloat16), "ctx").astype(jnp.float32),
        lax.psum(grad_expand.astype(jnp.bfloat16), "ctx").astype(jnp.float32),
        lax.psum(grad_thresholds.astype(jnp.bfloat16), "ctx").astype(jnp.float32),
        lax.psum(grad_shrink.astype(jnp.bfloat16), "ctx").astype(jnp.float32),
        lax.psum(grad_settling.astype(jnp.bfloat16), "ctx").astype(jnp.float32),
        lax.psum(grad_rescaling.astype(jnp.bfloat16), "ctx").astype(jnp.float32),
        lax.psum(grad_reshifting.astype(jnp.bfloat16), "ctx").astype(jnp.float32),
    )
    shares = (
        lax.psum_scatter(
            summed[0].astype(jnp.bfloat16), "dp", scatter_dimension=0, tiled=True
        ).astype(jnp.float32),
        lax.psum_scatter(
            summed[1].astype(jnp.bfloat16), "dp", scatter_dimension=1, tiled=True
        ).astype(jnp.float32),
        lax.psum_scatter(
            summed[2].astype(jnp.bfloat16), "dp", scatter_dimension=1, tiled=True
        ).astype(jnp.float32),
        lax.psum_scatter(
            summed[3].astype(jnp.bfloat16), "dp", scatter_dimension=0, tiled=True
        ).astype(jnp.float32),
        lax.psum_scatter(
            summed[4].astype(jnp.bfloat16), "dp", scatter_dimension=0, tiled=True
        ).astype(jnp.float32),
        lax.psum_scatter(
            summed[5].astype(jnp.bfloat16), "dp", scatter_dimension=0, tiled=True
        ).astype(jnp.float32),
        lax.psum_scatter(
            summed[6].astype(jnp.bfloat16), "dp", scatter_dimension=0, tiled=True
        ).astype(jnp.float32),
        lax.psum_scatter(
            summed[7].astype(jnp.bfloat16), "dp", scatter_dimension=0, tiled=True
        ).astype(jnp.float32),
        lax.psum_scatter(
            summed[8].astype(jnp.bfloat16), "dp", scatter_dimension=1, tiled=True
        ).astype(jnp.float32),
        lax.psum_scatter(
            summed[9].astype(jnp.bfloat16), "dp", scatter_dimension=0, tiled=True
        ).astype(jnp.float32),
        lax.psum_scatter(
            summed[10].astype(jnp.bfloat16), "dp", scatter_dimension=0, tiled=True
        ).astype(jnp.float32),
        lax.psum_scatter(
            summed[11].astype(jnp.bfloat16), "dp", scatter_dimension=0, tiled=True
        ).astype(jnp.float32),
    )
    layer_out = result.reshape(groups, rows, width).astype(jnp.bfloat16)
    return (
        layer_out,
        grad_tokens,
        shares[0],
        shares[1],
        shares[2],
        shares[3],
        shares[4],
        shares[5],
        shares[6],
        shares[7],
        shares[8],
        shares[9],
        shares[10],
        shares[11],
    )


def solution(mesh):
    in_specs = (
        P("dp", "ctx", None),
        P("dp", "ctx", None),
        P("dp", None),
        P(),
        P("dp", None, "tensor"),
        P(None, ("tensor", "dp")),
        P("tensor", "dp"),
        P("dp"),
        P("dp"),
        P("dp"),
        P("dp", "tensor"),
        P(("tensor", "dp")),
        P("tensor", "dp"),
        P("dp"),
        P("dp"),
        P("dp"),
    )
    out_specs = (
        P("dp", "ctx", None),
        P("dp", "ctx", None),
        P("dp", None, "tensor"),
        P(None, ("tensor", "dp")),
        P("tensor", "dp"),
        P("dp"),
        P("dp"),
        P("dp"),
        P("dp", "tensor"),
        P(("tensor", "dp")),
        P("tensor", "dp"),
        P("dp"),
        P("dp"),
        P("dp"),
    )
    return jax.shard_map(
        on_device, mesh=mesh, in_specs=in_specs, out_specs=out_specs, check_vma=False
    )
```

profile of v0, /device:TPU:0, one launch (start us, length us, event | category | flops | bytes accessed | tf_op | source)
XLA Modules:
  0.0 1042.8 jit_solution(5760663091211315352)
XLA Ops:
  13.5 11.9 %all_gather.39 = bf16[768,3,192]{0,2,1:T(8,128)(2,1)S(1)} all-gather(bf16[384,3,192]{0,2,1:T(8,128)(2,1)} %param.28), channel_id=1, replica_groups=mesh['dp'=2,'ctx'=4,'tensor'=4] {'dp'}, dimensions={0}, use_global_device_ids=true | all-gather | bytes 1327104 | tf_op jit(solution)/shard_map/all_gather | solution.py:236
  37.1 22.5 %all-gather.12.cloned.1.call-done = bf16[1,4096,2,192]{1,3,2,0:T(8,128)(2,1)} async-done(((bf16[1,1024,2,192]{1,3,2,0:T(8,128)(2,1)}), bf16[1,4096,2,192]{1,3,2,0:T(8,128)(2,1)}) %all-gather.12.cloned.1.call-update) | async-done | bytes 3145744 | tf_op jit(solution)/shard_map/all_gather | solution.py:273
  65.6 36.7 %while.53 = (s32[]{:T(128)}, bf16[2,512,192]{1,2,0:T(8,128)(2,1)}, f32[2,3,512]{2,1,0:T(4,128)}, s32[2]{0:T(128)}, s32[]{:T(128)}, /*index=5*/s32[3,2]{0,1:T(2,1...) while((s32[]{:T(128)}, bf16[2,512,192]{1,2,0:T(8,128)(2,1)}, ...), condition=%wide.region_7.8_spmd, body=%wide.region_0.7_spmd.sunk | while | flops 1260394496 | bytes 88061616 | solution.py:145
  70.6 12.0 %conditional.5 = (bf16[1,512,192]{1,2,0:T(8,128)(2,1)S(1)}, f32[1,3,512]{2,1,0:T(4,128)S(1)}) conditional(s32[]{:T(128)} %convert_element_type.429, (s32[]{:T(128)}, bf16[2048,2,192]{0,2,1:T(8,128)(2,1)}, bf16[2048,3,64]{0,2,1:T(8,128)(2,1)}, s32[4608]{0:T(1024)}, s32[3,2]{0,1:T(2,128)S(1)}, /*index=5*/pred[3,512,2048]{2,1,0:T(32,128)(4,1)S(1)}, ...), branch_computations={%region_1.3_spmd, %region_4.6_spmd} | conditional | flops 1257241088 | bytes 84084992 | solution.py:142
  88.9 12.0 %conditional.5 = (bf16[1,512,192]{1,2,0:T(8,128)(2,1)S(1)}, f32[1,3,512]{2,1,0:T(4,128)S(1)}) conditional(s32[]{:T(128)} %convert_element_type.429, (s32[]{:T(128)}, bf16[2048,2,192]{0,2,1:T(8,128)(2,1)}, bf16[2048,3,64]{0,2,1:T(8,128)(2,1)}, s32[4608]{0:T(1024)}, s32[3,2]{0,1:T(2,128)S(1)}, /*index=5*/pred[3,512,2048]{2,1,0:T(32,128)(4,1)S(1)}, ...), branch_computations={%region_1.3_spmd, %region_4.6_spmd} | conditional | flops 1257241088 | bytes 84084992 | solution.py:142
  126.3 152.2 %all-reduce.16.cloned.1.call-done = f32[1024,768]{1,0:T(8,128)} async-done(((f32[1024,768]{1,0:T(8,128)}), f32[1024,768]{1,0:T(8,128)}) %all-reduce.16.cloned.1.call-update) | async-done | bytes 3145744 | tf_op jit(solution)/shard_map/psum | solution.py:282
  283.6 11.1 %multiply_convert_fusion.1 = (bf16[1024,768]{1,0:T(8,128)(2,1)}, f32[1024,768]{1,0:T(8,128)}, f32[1024,768]{1,0:T(8,128)}) fusion(f32[768]{0:T(1024)S(1)} %reshape.580, bf16[1024,768]{1,0:T(8,128)(2,1)} %fusion.48, bf16[768,768]{1,0:T(8,128)(2,1)} %all-gather.14.cloned.1.call-done), kind=kOutput, calls=%fused_computation.113 | convolution fusion | flops 1259864064 | bytes 10619904 | tf_op jit(solution)/shard_map/dot_general | solution.py:290
  313.4 106.5 %all-reduce.18.cloned.1.call-done = f32[1024,768]{1,0:T(8,128)} async-done(((f32[1024,768]{1,0:T(8,128)}), f32[1024,768]{1,0:T(8,128)}) %all-reduce.18.cloned.1.call-update) | async-done | bytes 3145744 | tf_op jit(solution)/shard_map/psum | solution.py:295
  437.2 120.2 %all-reduce.20.cloned.1.call-done = f32[1024,768]{1,0:T(8,128)} async-done(((f32[1024,768]{1,0:T(8,128)}), f32[1024,768]{1,0:T(8,128)}) %all-reduce.20.cloned.1.call-update) | async-done | bytes 3145744 | tf_op jit(solution)/shard_map/psum | solution.py:309
  568.4 90.9 %while.54 = (s32[]{:T(128)}, f32[2048,2,192]{0,2,1:T(8,128)}, f32[2048,2,192]{0,2,1:T(8,128)}, bf16[2,512,192]{1,2,0:T(8,128)(2,1)}, s32[2]{0:T(128)}, /*index=5...) while((s32[]{:T(128)}, f32[2048,2,192]{0,2,1:T(8,128)}, ...), condition=%wide.region_24.25_spmd.clone, body=%wide.region_19.24_spmd.clone.sunk | while | flops 3083343872 | bytes 277362656 | solution.py:205
  573.7 25.1 %conditional.6 = (f32[2048,2,192]{0,2,1:T(8,128)}, f32[1024,2,192]{0,2,1:T(8,128)}, bf16[1,512,192]{1,2,0:T(8,128)(2,1)S(1)}) conditional(s32[]{:T(128)} %convert_element_type.432, (s32[]{:T(128)}, s32[4608]{0:T(1024)}, s32[]{:T(128)}, s32[3,2]{0,1:T(2,128)S(1)}, pred[3,512,2048]{2,1,0:T(32,128)(4,1)S(1)}, ...), branch_computations={%region_20.21_spmd, %region_22.23_spmd} | conditional | flops 3078224384 | bytes 239976800 | solution.py:193
  579.2 6.5 multiply_reduce_fusion
  605.3 8.0 dynamic_update_slice.57
  618.4 25.1 %conditional.6 = (f32[2048,2,192]{0,2,1:T(8,128)}, f32[1024,2,192]{0,2,1:T(8,128)}, bf16[1,512,192]{1,2,0:T(8,128)(2,1)S(1)}) conditional(s32[]{:T(128)} %convert_element_type.432, (s32[]{:T(128)}, s32[4608]{0:T(1024)}, s32[]{:T(128)}, s32[3,2]{0,1:T(2,128)S(1)}, pred[3,512,2048]{2,1,0:T(32,128)(4,1)S(1)}, ...), branch_computations={%region_20.21_spmd, %region_22.23_spmd} | conditional | flops 3078224384 | bytes 239976800 | solution.py:193
  651.1 8.0 dynamic_update_slice.57
  680.0 128.1 %reduce-scatter.15.cloned.1.call-done = bf16[1,1024,2,192]{1,3,2,0:T(8,128)(2,1)} async-done(((bf16[1,4096,2,192]{1,3,2,0:T(8,128)(2,1)}), bf16[1,1024,2,192]{1,3,2,0:T(8,128)(2,1)}) %reduce-scatter.15.cloned.1.call-update) | async-done | bytes 786448 | tf_op jit(solution)/shard_map/reduce_scatter | solution.py:328
  834.1 13.3 %reduce-scatter.23.cloned.1.call-done = bf16[384,192]{1,0:T(8,128)(2,1)} async-done(((bf16[768,192]{1,0:T(8,128)(2,1)}), bf16[384,192]{1,0:T(8,128)(2,1)}) %reduce-scatter.23.cloned.1.call-update) | async-done | bytes 147472
  849.1 20.3 %reduce-scatter.19.cloned.1.call-done = bf16[384,576]{1,0:T(8,128)(2,1)} async-done(((bf16[768,576]{1,0:T(8,128)(2,1)}), bf16[384,576]{1,0:T(8,128)(2,1)}) %reduce-scatter.19.cloned.1.call-update) | async-done | bytes 442384
  871.4 22.6 %reduce-scatter.17.cloned.1.call-done = bf16[384,768]{1,0:T(8,128)(2,1)} async-done(((bf16[768,768]{1,0:T(8,128)(2,1)}), bf16[384,768]{1,0:T(8,128)(2,1)}) %reduce-scatter.17.cloned.1.call-update) | async-done | bytes 589840 | tf_op jit(solution)/shard_map/reduce_scatter | solution.py:382
  897.0 9.0 reduce-scatter.21.cloned.1.call-done
  906.9 71.4 %all-reduce.22.cloned.1.call-done = bf16[1024,768]{1,0:T(8,128)(2,1)} async-done(((bf16[1024,768]{1,0:T(8,128)(2,1)}), bf16[1024,768]{1,0:T(8,128)(2,1)}) %all-reduce.22.cloned.1.call-update) | async-done | bytes 1572880 | tf_op jit(solution)/shard_map/psum | solution.py:345
  981.9 8.1 all-reduce.9
  990.5 6.8 all-reduce.7
  1001.9 26.1 %all-reduce.24.cloned.1.call-done = (bf16[384,3,192]{0,2,1:T(8,128)(2,1)}, bf16[192,384]{1,0:T(8,128)(2,1)}, bf16[384,768]{1,0:T(8,128)(2,1)}, bf16[768,384]{1,0:T(8,128)(2,1)}) async-done(((bf16[384,3,192]{0,2,1:T(8,128)(2,1)}, bf16[192,384]{1,0:T(8,128)(2,1)}, bf16[384,768]{1,0:T(8,128)(2,1)}, bf16[768,384]{1,0:T(8,128)(2,1)}), (bf16[384,3,192]{0,2,1:T(8,128)(2,1)}, bf16[192,384]{1,0:T(8,128)(2,1)}, ...) | async-done | bytes 1769488 | tf_op jit(solution)/shard_map/psum | solution.py:350
  (321 shorter events, 265.6 us)
Async XLA Ops:
  8.0 28.2 %copy-start = (s32[12,2]{0,1:T(2,128)S(1)}, s32[12,2]{0,1:T(2,128)}, u32[]{:S(2)}) copy-start(s32[12,2]{0,1:T(2,128)} %param.27) | copy-start | bytes 292
  8.0 51.6 %all-gather.12.cloned.1.call-start = ((), (), s32[]{:S(2)}) async-start(), calls=%async_computation.6 | async-start | bytes 3932160 | tf_op jit(solution)/shard_map/all_gather | solution.py:273
  29.4 249.1 %all-reduce.16.cloned.1.call-start = ((), (), s32[]{:S(2)}) async-start(), calls=%async_computation.7 | async-start | bytes 6291456 | tf_op jit(solution)/shard_map/psum | solution.py:282
  107.5 14.4 %copy-start.43 = (bf16[384]{0:T(512)(128)(2,1)S(1)}, bf16[384]{0:T(512)(128)(2,1)}, u32[]{:S(2)}) copy-start(bf16[384]{0:T(512)(128)(2,1)} %param.35) | copy-start | bytes 2308
  107.5 176.1 %all-gather.14.cloned.1.call-start = ((), (), s32[]{:S(2)}) async-start(), calls=%async_computation.8 | async-start | bytes 1769472 | tf_op jit(solution)/shard_map/all_gather | solution.py:242
  108.1 186.6 %all-gather.16.cloned.1.call-start = ((), (), s32[]{:S(2)}) async-start(), calls=%async_computation.9 | async-start | bytes 1769472 | tf_op jit(solution)/shard_map/all_gather | solution.py:244
  108.7 311.2 %all-reduce.18.cloned.1.call-start = ((), (), s32[]{:S(2)}) async-start(), calls=%async_computation.10 | async-start | bytes 6291456 | tf_op jit(solution)/shard_map/psum | solution.py:295
  299.6 257.8 %all-reduce.20.cloned.1.call-start = ((), (), s32[]{:S(2)}) async-start(), calls=%async_computation.11 | async-start | bytes 6291456 | tf_op jit(solution)/shard_map/psum | solution.py:309
  429.0 128.4 %copy-start.32 = (f32[1024]{0:T(1024)}, f32[1024]{0:T(1024)S(1)}, u32[]{:S(2)}) copy-start(f32[1024]{0:T(1024)S(1)} %negate_multiply_fusion.2) | copy-start | bytes 12292
  437.1 370.9 %reduce-scatter.15.cloned.1.call-start = ((), (), s32[]{:S(2)}) async-start(), calls=%async_computation.12 | async-start | bytes 3932160 | tf_op jit(solution)/shard_map/reduce_scatter | solution.py:328
  664.7 167.3 %reduce-scatter.25.cloned.1.call-start = ((), (), s32[]{:S(2)}) async-start(), calls=%async_computation.18 | async-start | bytes 1769472
  673.2 174.2 %reduce-scatter.23.cloned.1.call-start = ((), (), s32[]{:S(2)}) async-start(), calls=%async_computation.17 | async-start | bytes 589824
  676.5 192.9 %reduce-scatter.19.cloned.1.call-start = ((), (), s32[]{:S(2)}) async-start(), calls=%async_computation.15 | async-start | bytes 1474560
  816.0 78.1 %reduce-scatter.17.cloned.1.call-start = ((), (), s32[]{:S(2)}) async-start(), calls=%async_computation.14 | async-start | bytes 1769472 | tf_op jit(solution)/shard_map/reduce_scatter | solution.py:382
  820.5 85.5 %reduce-scatter.21.cloned.1.call-start = ((), (), s32[]{:S(2)}) async-start(), calls=%async_computation.16 | async-start | bytes 73728
  822.6 155.6 %all-reduce.22.cloned.1.call-start = ((), (), s32[]{:S(2)}) async-start(), calls=%async_computation.13 | async-start | bytes 3145728 | tf_op jit(solution)/shard_map/psum | solution.py:345
  826.8 68.9 %copy-start.49 = (u32[32]{0:T(128)S(1)}, u32[32]{0:T(128)}, u32[]{:S(2)}) copy-start(u32[32]{0:T(128)} %constant.349) | copy-start | bytes 388
  826.8 201.2 %all-reduce.24.cloned.1.call-start = ((), (), s32[]{:S(2)}) async-start(), calls=%async_computation.19 | async-start | bytes 3538944 | tf_op jit(solution)/shard_map/psum | solution.py:350
  906.8 75.1 %copy-start.34 = (bf16[768]{0:T(1024)(128)(2,1)S(1)}, bf16[768]{0:T(1024)(128)(2,1)}, u32[]{:S(2)}) copy-start(bf16[768]{0:T(1024)(128)(2,1)} %get-tuple-element.757) | copy-start | bytes 4612
  906.8 75.1 %copy-start.35 = (bf16[768]{0:T(1024)(128)(2,1)S(1)}, bf16[768]{0:T(1024)(128)(2,1)}, u32[]{:S(2)}) copy-start(bf16[768]{0:T(1024)(128)(2,1)} %get-tuple-element.755) | copy-start | bytes 4612
  906.8 75.1 %copy-start.36 = (bf16[768]{0:T(1024)(128)(2,1)S(1)}, bf16[768]{0:T(1024)(128)(2,1)}, u32[]{:S(2)}) copy-start(bf16[768]{0:T(1024)(128)(2,1)} %get-tuple-element.759) | copy-start | bytes 4612
  906.9 75.0 %copy-start.37 = (bf16[768]{0:T(1024)(128)(2,1)S(1)}, bf16[768]{0:T(1024)(128)(2,1)}, u32[]{:S(2)}) copy-start(bf16[768]{0:T(1024)(128)(2,1)} %get-tuple-element.859) | copy-start | bytes 4612
  906.9 75.0 %copy-start.39 = (bf16[768]{0:T(1024)(128)(2,1)S(1)}, bf16[768]{0:T(1024)(128)(2,1)}, u32[]{:S(2)}) copy-start(bf16[768]{0:T(1024)(128)(2,1)} %get-tuple-element.869) | copy-start | bytes 4612
  978.3 56.7 %copy-start.1 = (s32[12,2]{0,1:T(2,128)S(1)}, s32[12,2]{0,1:T(2,128)}, u32[]{:S(2)}) copy-start(s32[12,2]{0,1:T(2,128)} %param.27) | copy-start | bytes 292
  (42 other events, 168.5 us)
Sparse Core Ops, SparseCore 0:
  29.6 29.9 all-gather.11
  107.6 170.8 all-reduce.15
  299.7 120.0 all-reduce.17
  437.3 120.0 all-reduce.19
  664.8 143.1 reduce-scatter.14
  810.2 21.7 reduce-scatter.24
  834.3 13.1 reduce-scatter.22
  849.8 19.5 reduce-scatter.18
  872.2 21.7 reduce-scatter.16
  896.1 9.8 reduce-scatter.20
  909.1 69.1 all-reduce.21
  982.1 45.9 all-reduce.23
Sparse Core Ops, SparseCore 1:
  109.5 72.3 all-gather.13
  183.3 22.7 all-gather.15
where the time goes:
time: 1060 us; the launch traced here: 1040 us
  waiting for transfers between devices  699 us (66%)
  matrix products  92 us (9%)
  other arithmetic  87.1 us (8%)
  local copies, waits for them, and re-layouts  71.7 us (7%)
  blocking collectives  68.3 us (6%)
  between operations  17.3 us (2%)
    psum x1, waiting for transfers between devices, on_device(): lax.psum(jnp.dot(mixed_low, combine_all, preferred_element_type=jnp.float...  152 us
    reduce_scatter x1, waiting for transfers between devices, on_device(): lax.psum_scatter(jnp.concatenate([prompt_grads, window_grads], axis=1).as...  128 us
    psum x1, waiting for transfers between devices, on_device(): lax.psum(contract_cols(inner_back, expand_all), 'tensor')  120 us
    psum x1, waiting for transfers between devices, on_device(): lax.psum(jnp.dot(active_low, shrink_all, preferred_element_type=jnp.float...  106 us
    psum x1, waiting for transfers between devices, on_device(): lax.psum(contract_cols(joined_back, project_flat).astype(jnp.bfloat16), '...  71.4 us
    unnamed x18, waiting for transfers between devices  49 us
    psum x1, waiting for transfers between devices, on_device(): lax.psum(grad_project.astype(jnp.bfloat16), 'ctx').astype(jnp.float32)  26.1 us
    reduce_scatter x1, waiting for transfers between devices, on_device(): lax.psum_scatter(summed[6].astype(jnp.bfloat16), 'dp', scatter_dimension=...  22.6 us
  transfers between devices with their start and end apart: 14, of which 12 were waited for; matrix products, arithmetic and copies ran while one was open for 6% of the time, Pallas kernels for 0%

commit v1 on v0

v1 whole, which is shorter than its diff:
```python
import functools
import math

import jax
import jax.numpy as jnp
from jax import lax
from jax.experimental import pallas as pl
from jax.experimental.pallas import tpu as pltpu
from jax.sharding import PartitionSpec as P

P_SIZE = 2048
LMAX = 256
B = 1152
HD = 64
EPS = 1e-06
NEG = -1e30

BF = jnp.bfloat16
F32 = jnp.float32

VM = pl.BlockSpec(memory_space=pltpu.VMEM)
ANY = pl.BlockSpec(memory_space=pl.ANY)
SM = pl.BlockSpec(memory_space=pltpu.SMEM)
LIMIT = 60 << 20


def call(body, outs, scratch=(), ins=None, cost=None):
    out_specs = tuple([VM] * len(outs)) if isinstance(outs, tuple) else VM
    return pl.pallas_call(
        body,
        out_shape=outs,
        in_specs=ins,
        out_specs=out_specs,
        scratch_shapes=scratch,
        cost_estimate=cost,
        compiler_params=pltpu.CompilerParams(vmem_limit_bytes=LIMIT),
    )


def sds(shape, dtype):
    return jax.ShapeDtypeStruct(shape, dtype)


def cost(flops, nbytes, trans=0):
    return pl.CostEstimate(flops=int(flops), bytes_accessed=int(nbytes), transcendentals=int(trans))


def dot(a, b):
    return lax.dot_general(a, b, (((1,), (0,)), ((), ())), preferred_element_type=F32)


def dot_t(a, b):
    return lax.dot_general(a, b, (((1,), (1,)), ((), ())), preferred_element_type=F32)


def tdot(a, b):
    return lax.dot_general(a, b, (((0,), (0,)), ((), ())), preferred_element_type=F32)


def mult(value, by):
    return pl.multiple_of(value * by, by)


CTX, Z, X, C, Y, PAIR = 0, 1, 2, 3, 4, 8


def qkv_body(sc, x_ref, w0_ref, w1_ref, bias_ref, q_ref, kv_ref):
    half = w0_ref.shape[1]
    wide = q_ref.shape[0]
    acc = bias_ref[...].astype(F32)
    a0 = x_ref[:, pl.ds(mult(sc[X], half), half)]
    a1 = x_ref[:, pl.ds(mult(1 - sc[X], half), half)]
    out = dot_t(w0_ref[...], a0) + dot_t(w1_ref[...], a1) + acc
    low = out.astype(BF)
    q_ref[...] = low[:wide] * jnp.asarray(HD**-0.5, BF)
    kv_ref[...] = low[wide:]


def load_pairs(sc, own, par, ra, rb, pbuf, cbuf, sems):
    rows = own.shape[1]
    here = pl.ds(mult(sc[C], rows), rows)
    there = pl.ds(mult(1 - sc[C], rows), rows)

    def run(moves):
        copies = [
            pltpu.make_async_copy(src, dst, sems.at[i]) for i, (src, dst) in enumerate(moves)
        ]
        for copy in copies:
            copy.start()
        for copy in copies:
            copy.wait()

    @pl.when(sc[Y] == 0)
    def _():
        run([(own, pbuf.at[:, here]), (par, pbuf.at[:, there])])

    @pl.when(sc[Y] == 1)
    def _():
        run(
            [
                (ra, pbuf.at[:, here]),
                (rb, pbuf.at[:, there]),
                (own, cbuf.at[:, here]),
                (par, cbuf.at[:, there]),
            ]
        )


def prompt_pass(sc, h, index, start, tile):
    first = jnp.where(start >= B, 1, 0)
    last = jnp.where(start + tile // 2 >= B, 1, 0)
    mixed = jnp.where(first != last, 1, 0)
    blk = jnp.where(index == 0, first, last)
    paired = sc[PAIR + 2 * h + blk]
    lane = lax.broadcasted_iota(jnp.int32, (1, tile), 1)
    wanted = jnp.where(lane >= tile // 2, last, first)
    mine = jnp.where(wanted == blk, 1, 0)
    low = mine * (paired * B)
    high = mine * (B + paired * (P_SIZE - B))
    key_start = pl.multiple_of(paired * (P_SIZE - B), 128)
    return mixed, key_start, low, high


def window_start(sc, t, rows, tile):
    local = sc[C] * rows + t * tile
    return pl.multiple_of(jnp.clip(local - LMAX, 0, 2 * rows - tile - 2 * LMAX), 128)


CHUNK = 384


def fwd_body(k, sc, q_ref, span_ref, own, par, ra, rb, o_ref, lse_ref, pbuf, cbuf, s_buf, sems):
    load_pairs(sc, own, par, ra, rb, pbuf, cbuf, sems)
    rows = own.shape[1]
    wide, tile = o_ref.shape
    heads = wide // HD
    t = sc[Z] ^ k
    start = sc[CTX] * rows + t * tile
    cols = pl.ds(mult(t, tile), tile)

    def one_pass(src, key_start, size, low, high, q_h, h, carry):
        peak, total, acc = carry
        k_rows = pl.ds(mult(h, HD), HD)
        v_rows = pl.ds(mult(h, HD) + wide, HD)
        new_peak = peak
        for j in range(size // CHUNK):
            keys = src[k_rows, pl.ds(key_start + j * CHUNK, CHUNK)]
            s = tdot(keys, q_h)
            pos = lax.broadcasted_iota(jnp.int32, s.shape, 0) + (key_start + j * CHUNK)
            s = jnp.where((pos >= low) & (pos < high), s, NEG)
            s_buf[j * CHUNK : (j + 1) * CHUNK, :] = s
            new_peak = jnp.maximum(new_peak, jnp.max(s, axis=0, keepdims=True))
        alpha = jnp.exp(peak - new_peak)
        total = total * alpha
        acc = acc * alpha
        for j in range(size // CHUNK):
            e = jnp.exp(s_buf[j * CHUNK : (j + 1) * CHUNK, :] - new_peak)
            total = total + jnp.sum(e, axis=0, keepdims=True)
            vals = src[v_rows, pl.ds(key_start + j * CHUNK, CHUNK)]
            acc = acc + dot(vals, e.astype(BF))
        return new_peak, total, acc

    def one_head(h, _):
        q_h = q_ref[pl.ds(mult(h, HD), HD), cols]

        def prompt(index, carry):
            _, key_start, low, high = prompt_pass(sc, h, index, start, tile)
            return one_pass(pbuf, key_start, B, low, high, q_h, h, carry)

        def window(index, carry):
            first = window_start(sc, t, rows, tile)
            low = span_ref[0:1, cols]
            high = span_ref[1:2, cols]
            return one_pass(cbuf, first, tile + 2 * LMAX, low, high, q_h, h, carry)

        mixed = prompt_pass(sc, h, 0, start, tile)[0]
        carry = (
            jnp.full((1, tile), NEG, F32),
            jnp.zeros((1, tile), F32),
            jnp.zeros((HD, tile), F32),
        )
        carry = lax.fori_loop(0, 1 + mixed, prompt, carry)
        near = jnp.where((sc[Y] == 1) & (sc[PAIR + 2 * h + 1] == 1), 1, 0)
        peak, total, acc = lax.fori_loop(0, near, window, carry)
        o_ref[pl.ds(mult(h, HD), HD), :] = (acc / total).astype(BF)
        lse_ref[pl.ds(mult(h, 8), 8), :] = jnp.broadcast_to(peak + jnp.log(total), (8, tile))
        return 0

    lax.fori_loop(0, heads, one_head, 0)


def bwd_body(
    sc,
    q_ref,
    span_ref,
    own,
    par,
    ra,
    rb,
    *refs,
):
    o_in = refs[0:4]
    lse_in = refs[4:8]
    g_in = refs[8:12]
    dq_ref, d_own, d_par, d_r0, d_r1 = refs[12:17]
    pbuf, cbuf, o_s, lse_s, g_s, acc_p, acc_c, sems = refs[17:]
    load_pairs(sc, own, par, ra, rb, pbuf, cbuf, sems)
    rows = own.shape[1]
    wide, tile = o_in[0].shape
    heads = wide // HD
    for k in range(4):
        o_s[k] = o_in[k][...]
        lse_s[k] = lse_in[k][...]
        g_s[k] = g_in[k][...]

    def one_pass(src, acc_ref, key_start, size, low, high, q_h, g_h, lse, delta, h, dq):
        k_rows = pl.ds(mult(h, HD), HD)
        v_rows = pl.ds(mult(h, HD) + wide, HD)
        zero = jnp.zeros_like(q_h)
        both = jnp.concatenate(
            [jnp.concatenate([q_h, zero], axis=1), jnp.concatenate([zero, g_h], axis=1)], axis=0
        )
        for j in range(size // CHUNK):
            place = pl.ds(key_start + j * CHUNK, CHUNK)
            keys = src[k_rows, place]
            vals = src[v_rows, place]
            s = tdot(keys, q_h)
            pos = lax.broadcasted_iota(jnp.int32, s.shape, 0) + (key_start + j * CHUNK)
            s = jnp.where((pos >= low) & (pos < high), s, NEG)
            probs = jnp.exp(s - lse)
            ds = probs * (tdot(vals, g_h) - delta)
            ds = ds.astype(BF)
            dq = dq + dot(keys, ds)
            acc_ref[place, :] += dot_t(jnp.concatenate([ds, probs.astype(BF)], axis=1), both)
        return dq

    def one_head(h, _):
        acc_p[...] = jnp.zeros_like(acc_p)
        acc_c[...] = jnp.zeros_like(acc_c)
        h_rows = pl.ds(mult(h, HD), HD)

        def one_tile(k, _):
            t = sc[Z] ^ k
            start = sc[CTX] * rows + t * tile
            cols = pl.ds(mult(t, tile), tile)
            q_h = q_ref[h_rows, cols]
            g_h = g_s[k, h_rows, :]
            o_h = o_s[k, h_rows, :]
            lse = lse_s[k, pl.ds(mult(h, 8), 8), :][0:1]
            delta = jnp.sum(o_h.astype(F32) * g_h.astype(F32), axis=0, keepdims=True)

            def prompt(index, dq):
                _, key_start, low, high = prompt_pass(sc, h, index, start, tile)
                return one_pass(
                    pbuf, acc_p, key_start, B, low, high, q_h, g_h, lse, delta, h, dq
                )

            def window(index, dq):
                first = window_start(sc, t, rows, tile)
                low = span_ref[0:1, cols]
                high = span_ref[1:2, cols]
                return one_pass(
                    cbuf, acc_c, first, tile + 2 * LMAX, low, high, q_h, g_h, lse, delta, h, dq
                )

            mixed = prompt_pass(sc, h, 0, start, tile)[0]
            dq = lax.fori_loop(0, 1 + mixed, prompt, jnp.zeros((HD, tile), F32))
            near = jnp.where((sc[Y] == 1) & (sc[PAIR + 2 * h + 1] == 1), 1, 0)
            dq = lax.fori_loop(0, near, window, dq)
            dq_ref[k, h_rows, :] = (dq * HD**-0.5).astype(BF)
            return 0

        lax.fori_loop(0, 4, one_tile, 0)

        def give(acc, row, out):
            turned = acc[pl.ds(mult(row, rows), rows), :].T.astype(BF)
            out[h_rows, :] = turned[:HD]
            out[pl.ds(mult(h, HD) + wide, HD), :] = turned[HD:]

        @pl.when(sc[Y] == 0)
        def _():
            give(acc_p, sc[C], d_own)
            give(acc_p, 1 - sc[C], d_par)

        @pl.when(sc[Y] == 1)
        def _():
            give(acc_c, sc[C], d_own)
            give(acc_c, 1 - sc[C], d_par)
            give(acc_p, sc[C], d_r0)
            give(acc_p, 1 - sc[C], d_r1)

        return 0

    lax.fori_loop(0, heads, one_head, 0)


def norm(value):
    mean = jnp.mean(value, axis=-1, keepdims=True)
    centred = value - mean
    inv = lax.rsqrt(jnp.mean(centred * centred, axis=-1, keepdims=True) + EPS)
    return centred * inv, inv


def norm_back(e, n, inv):
    return (
        e - jnp.mean(e, axis=-1, keepdims=True) - n * jnp.mean(e * n, axis=-1, keepdims=True)
    ) * inv


def mid_body(sc, *refs):
    mixed = refs[0:4]
    x_ref, cot_ref = refs[4:6]
    packs = refs[6:14]
    pieces = refs[14:30]
    (
        out_ref,
        mb0,
        mb1,
        mb2,
        mb3,
        nl_ref,
        fb_ref,
        ab_ref,
        act_own,
        act_oth,
        ib_own,
        ib_oth,
        mix_own,
        mix_oth,
        gf_ref,
        small_ref,
    ) = refs[30:46]
    we, ws, wc, mix_s, act_s, gp_s, ib_s, vec_s, thr_s, mb_s, sems, osems = refs[46:]
    wide, tile = mixed[0].shape
    width = x_ref.shape[1]
    half = width // 2
    hidden = we.shape[1]
    block = hidden // 4
    hb = block // 2
    hw = wide // 2
    c = sc[C]

    stages = [[], [], []]
    for k in range(4):
        z = sc[Z] ^ k
        for j in range(2):
            xc = pl.ds(mult(sc[X] ^ j, half), half)
            for i in range(2):
                cc = c ^ i
                piece = pieces[k * 4 + j * 2 + i]
                n = len(stages[0])
                stages[0].append(
                    pltpu.make_async_copy(
                        piece.at[pl.ds(half + hb, hw), :],
                        wc.at[pl.ds(pl.multiple_of(z * wide + cc * hw, hw), hw), xc],
                        sems.at[0, n],
                    )
                )
                stages[1].append(
                    pltpu.make_async_copy(
                        piece.at[pl.ds(0, half), :],
                        we.at[xc, pl.ds(pl.multiple_of(z * block + cc * hb, hb), hb)],
                        sems.at[1, n],
                    )
                )
                stages[2].append(
                    pltpu.make_async_copy(
                        piece.at[pl.ds(half, hb), :],
                        ws.at[pl.ds(pl.multiple_of(z * block + cc * hb, hb), hb), xc],
                        sems.at[2, n],
                    )
                )
    for stage in stages:
        for copy in stage:
            copy.start()

    for k in range(4):
        mix_s[pl.ds(mult(sc[Z] ^ k, wide), wide), :] = mixed[k][...]
        for j in range(2):
            pack = packs[k * 2 + j]
            at = pl.multiple_of((sc[Z] ^ k) * block + (sc[X] ^ j) * half, 128)
            thr_s[:, pl.ds(at, half)] = pack[...].astype(F32)
            if k == 0:
                vec_s[:, pl.ds(mult(sc[X] ^ j, half), half)] = pack[...].astype(F32)

    baseline = vec_s[0:1, :]
    scaling = vec_s[1:2, :]
    shifting = vec_s[2:3, :]
    settling = vec_s[3:4, :]
    rescaling = vec_s[4:5, :]
    reshifting = vec_s[5:6, :]

    for copy in stages[0]:
        copy.wait()
    first = x_ref[...].astype(F32) + tdot(mix_s[...], wc[...]) + baseline
    n1, inv1 = norm(first)
    normed = n1 * scaling + shifting
    low = normed.astype(BF)
    nl_ref[...] = low
    for copy in stages[1]:
        copy.wait()
    for copy in stages[2]:
        copy.wait()
    feed = jnp.zeros((tile, width), F32)
    for n in range(4):
        cols = slice(n * block, (n + 1) * block)
        inner = dot(low, we[:, cols]) + thr_s[6:7, cols]
        cdf = 0.5 * (1.0 + lax.erf(inner * (0.5**0.5)))
        pdf = jnp.exp(-0.5 * inner * inner) * (1.0 / math.sqrt(2.0 * math.pi))
        active = (inner * cdf).astype(BF)
        act_s[:, cols] = active
        gp_s[:, cols] = cdf + inner * pdf
        feed = feed + dot(active, ws[cols, :])
    second = normed + feed + settling
    n2, inv2 = norm(second)
    out_ref[...] = (n2 * rescaling + reshifting).astype(BF)
    dy = cot_ref[...].astype(F32)
    small_ref[...] = jnp.zeros_like(small_ref)
    small_ref[4:5, :] = jnp.sum(dy * n2, axis=0, keepdims=True)
    small_ref[5:6, :] = jnp.sum(dy, axis=0, keepdims=True)
    grad = norm_back(rescaling * dy, n2, inv2)
    small_ref[3:4, :] = jnp.sum(grad, axis=0, keepdims=True)
    feed_back = grad.astype(BF)
    fb_ref[...] = feed_back
    for n in range(4):
        cols = slice(n * block, (n + 1) * block)
        inner_back = (dot_t(feed_back, ws[cols, :]) * gp_s[:, cols]).astype(BF)
        ib_s[:, cols] = inner_back
        small_ref[8 + n : 9 + n, :] = jnp.sum(inner_back.astype(F32), axis=0, keepdims=True)
        grad = grad + dot_t(inner_back, we[:, cols])
    small_ref[1:2, :] = jnp.sum(grad * n1, axis=0, keepdims=True)
    small_ref[2:3, :] = jnp.sum(grad, axis=0, keepdims=True)
    grad_first = norm_back(scaling * grad, n1, inv1)
    small_ref[0:1, :] = jnp.sum(grad_first, axis=0, keepdims=True)
    gf_ref[...] = grad_first
    attended_back = grad_first.astype(BF)
    ab_ref[...] = attended_back
    mb_s[...] = dot_t(wc[...], attended_back).astype(BF)
    for k, mb in enumerate((mb0, mb1, mb2, mb3)):
        mb[...] = mb_s[pl.ds(mult(sc[Z] ^ k, wide), wide), :]
    for n in range(4):
        mine = pl.ds(pl.multiple_of(n * block + c * hb, 128), hb)
        other = pl.ds(pl.multiple_of(n * block + (1 - c) * hb, 128), hb)
        cols = slice(n * hb, (n + 1) * hb)
        act_own[:, cols] = act_s[:, mine]
        act_oth[:, cols] = act_s[:, other]
        ib_own[:, cols] = ib_s[:, mine]
        ib_oth[:, cols] = ib_s[:, other]
        mine = pl.ds(pl.multiple_of(n * wide + c * hw, hw), hw)
        other = pl.ds(pl.multiple_of(n * wide + (1 - c) * hw, hw), hw)
        mix_own[n * hw : (n + 1) * hw, :] = mix_s[mine, :]
        mix_oth[n * hw : (n + 1) * hw, :] = mix_s[other, :]


def wg_body(sc, *refs):
    nl, fb, ab, act, ib, mix = [(refs[i], refs[6 + i]) for i in range(6)]
    outs = refs[12:14]
    half = nl[0].shape[1] // 2
    hb = act[0].shape[1] // 4
    hw = mix[0].shape[0] // 4
    for j in range(2):
        xc = pl.ds(mult(sc[X] ^ j, half), half)
        for k in range(4):
            z = sc[Z] ^ k
            zc = pl.ds(mult(z, hb), hb)
            e = sum(tdot(nl[i][:, xc], ib[i][:, zc]) for i in range(2)).astype(BF)
            s = sum(tdot(act[i][:, zc], fb[i][:, xc]) for i in range(2)).astype(BF)
            zr = pl.ds(mult(z, hw), hw)
            m = sum(dot(mix[i][zr, :], ab[i][:, xc]) for i in range(2)).astype(BF)
            for yh in range(2):
                out = outs[j].at[sc[Y] ^ yh, k]
                out[0 : half // 2, :] = e[yh * (half // 2) : (yh + 1) * (half // 2)]
                out[half // 2 : half // 2 + hb // 2, :] = s[yh * (hb // 2) : (yh + 1) * (hb // 2)]
                out[half // 2 + hb // 2 :, :] = m[yh * (hw // 2) : (yh + 1) * (hw // 2)]


def wfin_body(sc, *refs):
    quarters = refs[0:4]
    e_ref, s_ref, m_ref = refs[4:7]
    he = e_ref.shape[0] // 2
    hb = e_ref.shape[1] // 2
    hs = hb // 2
    hm = m_ref.shape[0] // 4
    for i in range(2):
        for j in range(2):
            part = quarters[2 * i + j]
            c = sc[C] ^ i
            y = sc[Y] ^ j
            e_ref[pl.ds(mult(y, he), he), pl.ds(mult(c, hb), hb)] = part[0:he, :].astype(F32)
            at = pl.multiple_of(c * hb + y * hs, hs)
            s_ref[pl.ds(at, hs), :] = part[he : he + hs, :].astype(F32)
            at = pl.multiple_of((c * 2 + y) * hm, hm)
            m_ref[pl.ds(at, hm), :] = part[he + hs :, :].astype(F32)


def kvfin_body(sc, a_ref, b_ref, c_ref, out_ref):
    tile = out_ref.shape[2]
    for k in range(4):
        cols = pl.ds(mult(sc[Z] ^ k, tile), tile)
        total = a_ref[:, cols].astype(F32) + b_ref[:, cols].astype(F32)
        out_ref[k] = (total + c_ref[:, cols].astype(F32)).astype(BF)


def gp_body(sc, dq_ref, kv_ref, x_ref, out_ref, sum_ref, acc):
    wide = dq_ref.shape[1]
    tile = dq_ref.shape[2]
    ones = jnp.ones((8, tile), BF)
    top = bot = s_top = s_bot = 0.0
    for k in range(4):
        rows = x_ref[pl.ds(mult(sc[Z] ^ k, tile), tile), :]
        top = top + dot(dq_ref[k], rows)
        bot = bot + dot(kv_ref[k], rows)
        s_top = s_top + dot_t(ones, dq_ref[k])
        s_bot = s_bot + dot_t(ones, kv_ref[k, wide:, :])
    acc[:wide, :] = top
    acc[wide:, :] = bot
    sum_ref[...] = jnp.zeros_like(sum_ref)
    sum_ref[:, 0:wide] = s_top
    sum_ref[:, wide : 2 * wide] = s_bot
    n_rows = out_ref.shape[3]
    n_cols = out_ref.shape[4]
    for i in range(2):
        for j in range(2):
            at = pl.multiple_of(((sc[C] ^ i) * 2 + (sc[Y] ^ j)) * n_rows, n_rows)
            for m in range(2):
                cols = pl.ds(mult(sc[X] ^ m, n_cols), n_cols)
                out_ref[i, j, m] = acc[pl.ds(at, n_rows), cols].astype(BF)


def ib_body(sc, *refs):
    dq = refs[0:4]
    kv = refs[4:8]
    gf_ref = refs[8]
    pieces = refs[9:25]
    out_ref, wp, jb, sems = refs[25:]
    wide = dq[0].shape[0]
    half = wp.shape[2] // 2
    hr = wp.shape[1] // 2
    copies = []
    for k in range(4):
        for j in range(2):
            for i in range(2):
                copies.append(
                    pltpu.make_async_copy(
                        pieces[k * 4 + j * 2 + i],
                        wp.at[
                            k,
                            pl.ds(mult(sc[C] ^ i, hr), hr),
                            pl.ds(mult(sc[X] ^ j, half), half),
                        ],
                        sems.at[len(copies)],
                    )
                )
    for copy in copies:
        copy.start()
    for k in range(4):
        jb[k, :wide, :] = dq[k][...]
        jb[k, wide:, :] = kv[k][...]
    for copy in copies:
        copy.wait()
    total = gf_ref[...]
    for k in range(4):
        total = total + tdot(jb[k], wp[k])
    out_ref[...] = total.astype(BF)


def join_body(dtype, sc, *refs):
    out = refs[4]
    tile = refs[0].shape[0]
    for k in range(4):
        out[pl.ds(mult(sc[Z] ^ k, tile), tile), :] = refs[k][...].astype(dtype)


def gpfin_body(sc, *refs):
    out = refs[4]
    n_rows = refs[0].shape[0]
    for i in range(2):
        for j in range(2):
            at = pl.multiple_of(((sc[C] ^ i) * 2 + (sc[Y] ^ j)) * n_rows, n_rows)
            out[pl.ds(at, n_rows), :] = refs[2 * i + j][...].astype(F32)


def make_device(n_dp, n_ctx, n_t, generic):
    def swap(axis, size, k):
        return lambda v: lax.ppermute(v, axis, [(i, i ^ k) for i in range(size)])

    pc = swap("ctx", n_ctx, 1)
    py = swap("ctx", n_ctx, 2)
    px = swap("dp", n_dp, 1)
    pz = [lambda v: v] + [swap("tensor", n_t, k) for k in range(1, n_t)]

    def on_device(
        tokens,
        cotangent,
        segments,
        pairing,
        project,
        offsets,
        combine,
        baseline,
        scaling,
        shifting,
        expand,
        thresholds,
        shrink,
        settling,
        rescaling,
        reshifting,
    ):
        _, rows, width = tokens.shape
        heads = pairing.shape[0] // n_t
        wide = heads * HD
        tile = rows // n_t
        half = width // 2
        block = expand.shape[1]
        hidden = block * n_t
        hb = block // 2
        hw = wide // 2
        x = tokens[0]
        cot = cotangent[0]
        ctx = lax.axis_index("ctx")
        z = lax.axis_index("tensor")
        dp = lax.axis_index("dp")
        xi = jnp.zeros_like(dp) if generic else dp
        c = ctx & 1
        y = ctx >> 1
        pairs = lax.dynamic_slice_in_dim(pairing, z * heads, heads, 0).reshape(-1)
        sc = jnp.concatenate(
            [jnp.stack([ctx, z, xi, c, y, c, c, c]).astype(jnp.int32), pairs.astype(jnp.int32)]
        )

        def both_halves(v, axis):
            full = lax.all_gather(v, "dp", axis=axis, tiled=True)
            return jnp.split(full, 2, axis=axis)

        wt = jnp.transpose(project, (1, 2, 0)).reshape(3 * wide, -1)
        vectors = [baseline, scaling, shifting, settling, rescaling, reshifting]

        def pack_small(vecs, thr, off):
            line = jnp.concatenate([off[0], off[1], jnp.zeros((half - wide,), BF)])
            return jnp.stack(vecs + [thr, line])

        def pack_weights(e, s, m):
            return jnp.concatenate(
                [
                    lax.dynamic_slice_in_dim(e, c * hb, hb, 1),
                    lax.dynamic_slice_in_dim(s, c * hb, hb, 0),
                    lax.dynamic_slice_in_dim(m, c * hw, hw, 0),
                ]
            )

        def half_project(w):
            return lax.dynamic_slice_in_dim(w, c * (3 * hw), 3 * hw, 0)

        if generic:
            wts = both_halves(wt, 1)
            vec_h = [both_halves(v, 0) for v in vectors]
            thr_h = both_halves(thresholds, 0)
            off_h = both_halves(offsets, 1)
            smalls = [
                pack_small([v[j] for v in vec_h], thr_h[j], off_h[j]) for j in range(2)
            ]
            es, ss, ms = both_halves(expand, 0), both_halves(shrink, 1), both_halves(combine, 1)
            wpacks = [pack_weights(es[j], ss[j], ms[j]) for j in range(2)]
            small_pieces = [[p(s) for s in smalls] for p in pz]
            weight_halves = [[p(w) for w in wpacks] for p in pz]
            proj_halves = [[p(half_project(w)) for w in wts] for p in pz]
        else:
            wts = [wt, px(wt)]
            small = pack_small(vectors, thresholds, offsets)
            small_z = [p(small) for p in pz]
            small_pieces = [[s, px(s)] for s in small_z]
            wpack = pack_weights(expand, shrink, combine)
            weight_halves = [[w, px(w)] for w in [p(wpack) for p in pz]]
            proj_halves = [[w, px(w)] for w in [p(half_project(wt)) for p in pz]]
        weight_pieces = [w for k in range(4) for j in range(2) for w in (weight_halves[k][j], pc(weight_halves[k][j]))]
        proj_pieces = [w for k in range(4) for j in range(2) for w in (proj_halves[k][j], pc(proj_halves[k][j]))]
        packs = [small_pieces[k][j] for k in range(4) for j in range(2)]

        hq = wide // 2
        lines = [small_pieces[0][j][7] for j in range(2)]
        lines = [jnp.where(xi == 0, lines[j], lines[1 - j]) for j in range(2)]
        bias = jnp.concatenate(
            [
                lines[0][:hq],
                lines[1][:hq],
                jnp.zeros((wide,), BF),
                lines[0][hq : 2 * hq],
                lines[1][hq : 2 * hq],
            ]
        ).astype(F32)[:, None]
        qT, kvT = call(
            qkv_body,
            (sds((wide, rows), BF), sds((2 * wide, rows), BF)),
            ins=[SM] + [VM] * 4,
            cost=cost(2 * rows * width * 3 * wide, 4 * rows * width),
        )(sc, x, wts[0], wts[1], bias)

        seg = segments[0]
        mine = lax.dynamic_slice_in_dim(seg, c * rows, rows, 0)
        low = jnp.sum((seg[:, None] < mine[None, :]).astype(jnp.int32), axis=0)
        high = jnp.sum((seg[:, None] <= mine[None, :]).astype(jnp.int32), axis=0)
        span = jnp.concatenate(
            [low[None], high[None], jnp.zeros((6, rows), jnp.int32)], axis=0
        )

        par = pc(kvT)
        ra = lax.ppermute(kvT, "ctx", [(0, 2), (1, 3)])
        rb = pc(ra)

        kv_scratch = [pltpu.VMEM((2 * wide, 2 * rows), BF), pltpu.VMEM((2 * wide, 2 * rows), BF)]
        o_tiles = [None] * 4
        lses = [None] * 4
        for k in (1, 2, 3, 0):
            o_tiles[k], lses[k] = call(
                functools.partial(fwd_body, k),
                (sds((wide, tile), BF), sds((8 * heads, tile), F32)),
                ins=[SM, VM, VM] + [ANY] * 4,
                scratch=kv_scratch
                + [pltpu.VMEM((B, tile), F32), pltpu.SemaphoreType.DMA((4,))],
                cost=cost(4 * B * tile * wide, 4 * 2 * wide * rows, B * tile * heads),
            )(sc, qT, span, kvT, par, ra, rb)
        mixed = [pz[k](o_tiles[k]) for k in range(4)]

        x_mine = lax.dynamic_slice_in_dim(x, z * tile, tile, 0)
        cot_mine = lax.dynamic_slice_in_dim(cot, z * tile, tile, 0)
        outs = call(
            mid_body,
            (
                sds((tile, width), BF),
                *[sds((wide, tile), BF)] * 4,
                *[sds((tile, width), BF)] * 3,
                *[sds((tile, hidden // 2), BF)] * 4,
                *[sds((width // 2, tile), BF)] * 2,
                sds((tile, width), F32),
                sds((16, width), F32),
            ),
            ins=[SM] + [VM] * 14 + [ANY] * 16,
            scratch=[
                pltpu.VMEM((width, hidden), BF),
                pltpu.VMEM((hidden, width), BF),
                pltpu.VMEM((width, width), BF),
                pltpu.VMEM((width, tile), BF),
                pltpu.VMEM((tile, hidden), BF),
                pltpu.VMEM((tile, hidden), F32),
                pltpu.VMEM((tile, hidden), BF),
                pltpu.VMEM((8, width), F32),
                pltpu.VMEM((8, hidden), F32),
                pltpu.VMEM((width, tile), BF),
                pltpu.SemaphoreType.DMA((3, 16)),
                pltpu.SemaphoreType.DMA((1,)),
            ],
            cost=cost(8 * tile * width * hidden + 4 * tile * width * width, 4 * width * hidden),
        )(sc, *mixed, x_mine, cot_mine, *packs, *weight_pieces)
        out_low = outs[0]
        mb = outs[1:5]
        nl, fb, ab, act_own, act_oth, ib_own, ib_oth, mix_own, mix_oth, grad_first, small_sum = outs[5:]
        grads = [pz[k](mb[k]) for k in range(4)]

        theirs = [pc(v) for v in (nl, fb, ab, act_oth, ib_oth, mix_oth)]
        n_part = half // 2 + hb // 2 + hw // 2
        g_own, g_oth = call(
            wg_body,
            tuple([sds((2, 4, n_part, half), BF)] * 2),
            ins=[SM] + [VM] * 12,
            cost=cost(4 * tile * width * hidden, 4 * width * hidden),
        )(sc, nl, fb, ab, act_own, ib_own, mix_own, *theirs)

        outs = call(
            bwd_body,
            (sds((4, wide, tile), BF), *[sds((2 * wide, rows), BF)] * 4),
            ins=[SM, VM, VM] + [ANY] * 4 + [VM] * 12,
            scratch=kv_scratch
            + [
                pltpu.VMEM((4, wide, tile), BF),
                pltpu.VMEM((4, 8 * heads, tile), F32),
                pltpu.VMEM((4, wide, tile), BF),
                pltpu.VMEM((2 * rows, 2 * HD), F32),
                pltpu.VMEM((2 * rows, 2 * HD), F32),
                pltpu.SemaphoreType.DMA((4,)),
            ],
            cost=cost(10 * B * rows * wide, 4 * 4 * wide * rows, B * rows * heads),
        )(sc, qT, span, kvT, par, ra, rb, *o_tiles, *lses, *grads)
        dq, d_own, d_par, d_r0, d_r1 = outs
        got_par = pc(d_par)
        got_r = pc(d_r1)
        prompt_part = (d_r0.astype(F32) + got_r.astype(F32)).astype(BF)
        from_y = lax.ppermute(prompt_part, "ctx", [(2, 0), (3, 1)])
        kv_back = call(
            kvfin_body,
            sds((4, 2 * wide, tile), BF),
            ins=[SM] + [VM] * 3,
            cost=cost(2 * wide * rows, 8 * wide * rows),
        )(sc, d_own, got_par, from_y)

        jq = [dq[0]] + [pz[k](dq[k]) for k in range(1, 4)]
        jkv = [kv_back[0]] + [pz[k](kv_back[k]) for k in range(1, 4)]
        gp, sums = call(
            gp_body,
            (sds((2, 2, 2, 3 * wide // 4, half), BF), sds((8, width), F32)),
            ins=[SM] + [VM] * 3,
            scratch=[pltpu.VMEM((3 * wide, width), F32)],
            cost=cost(2 * rows * width * 3 * wide, 4 * rows * width),
        )(sc, dq, kv_back, x)

        low_tokens = call(
            ib_body,
            sds((tile, width), BF),
            ins=[SM] + [VM] * 9 + [ANY] * 16,
            scratch=[
                pltpu.VMEM((4, 3 * wide, width), BF),
                pltpu.VMEM((4, 3 * wide, tile), BF),
                pltpu.SemaphoreType.DMA((16,)),
            ],
            cost=cost(8 * tile * width * 3 * wide, 8 * width * 3 * wide),
        )(sc, *jq, *jkv, grad_first, *proj_pieces)
        token_tiles = [low_tokens] + [pz[k](low_tokens) for k in range(1, 4)]
        grad_tokens = call(
            functools.partial(join_body, F32),
            sds((rows, width), F32),
            ins=[SM] + [VM] * 4,
            cost=cost(rows * width, 6 * rows * width),
        )(sc, *token_tiles)
        layer_tiles = [out_low] + [pz[k](out_low) for k in range(1, 4)]
        layer_out = call(
            functools.partial(join_body, BF),
            sds((rows, width), BF),
            ins=[SM] + [VM] * 4,
            cost=cost(rows * width, 4 * rows * width),
        )(sc, *layer_tiles)

        def add(a, b):
            return (a.astype(F32) + b.astype(F32)).astype(BF)

        def reduce_ff(g):
            s = add(g[0], py(g[1]))
            got = [pz[k](s[k]) for k in range(1, 4)]
            mine = s[0].astype(F32) + got[0].astype(F32) + got[1].astype(F32) + got[2].astype(F32)
            mine = mine.astype(BF)
            quarters = [mine, py(mine)]
            quarters = quarters + [pc(q) for q in quarters]
            return call(
                wfin_body,
                (sds((half, block), F32), sds((block, half), F32), sds((wide, half), F32)),
                ins=[SM] + [VM] * 4,
                cost=cost(2 * half * block, 12 * half * block),
            )(sc, *quarters)

        def reduce_gp(g):
            s = add(g[0], pc(g[1]))
            mine = add(s[0], py(s[1]))
            quarters = [mine, py(mine)]
            return quarters

        def finish_gp(quarters):
            quarters = quarters + [pc(q) for q in quarters]
            return call(
                gpfin_body,
                sds((3 * wide, half), F32),
                ins=[SM] + [VM] * 4,
                cost=cost(3 * wide * half, 6 * 3 * wide * half),
            )(sc, *quarters)

        def gp_cy(g):
            s = add(g[0], pc(g[1]))
            return add(s[0], py(s[1]))

        if generic:
            parts = [reduce_ff(g) for g in (g_own, g_oth)]

            def scatter(v, axis):
                return lax.psum_scatter(
                    v.astype(BF), "dp", scatter_dimension=axis, tiled=True
                ).astype(F32)

            grad_expand = scatter(jnp.concatenate([p[0] for p in parts], axis=0), 0)
            grad_shrink = scatter(jnp.concatenate([p[1] for p in parts], axis=1), 1)
            grad_combine = scatter(jnp.concatenate([p[2] for p in parts], axis=1), 1)
            summed = gp_cy(gp)
            both = []
            for j in range(2):
                both.append(finish_gp([summed[j], py(summed[j])]))
            grad_project = scatter(jnp.concatenate(both, axis=1), 1)
        else:
            g = add(g_own, px(g_oth))
            grad_expand, grad_shrink, grad_combine = reduce_ff(g)
            summed = gp_cy(gp)
            mine = add(summed[0], px(summed[1]))
            grad_project = finish_gp([mine, py(mine)])
        grad_project = jnp.transpose(grad_project.reshape(3, wide, -1), (2, 0, 1))

        slot = lax.broadcasted_iota(jnp.int32, (16, 1), 0) == 12 + z
        total = small_sum + jnp.where(slot, sums[0:1], 0.0)
        total = total + pc(total)
        total = total + py(total)
        total = lax.psum(total, "dp") if generic else total + px(total)
        total = total + pz[1](total)
        total = total + pz[2](total)
        n_vec = baseline.shape[0]

        def row(r):
            return lax.dynamic_slice(total, (r, dp * n_vec), (1, n_vec))[0]

        n_off = offsets.shape[1]
        grad_offsets = jnp.concatenate(
            [lax.dynamic_slice(total, (12 + z, dp * n_off + i * wide), (1, n_off)) for i in range(2)]
        )
        return (
            layer_out[None],
            grad_tokens[None],
            grad_project,
            grad_offsets,
            grad_combine,
            row(0),
            row(1),
            row(2),
            grad_expand,
            row(8 + z),
            grad_shrink,
            row(3),
            row(4),
            row(5),
        )

    return on_device


def solution(mesh):
    in_specs = (
        P("dp", "ctx", None),
        P("dp", "ctx", None),
        P("dp", None),
        P(),
        P("dp", None, "tensor"),
        P(None, ("tensor", "dp")),
        P("tensor", "dp"),
        P("dp"),
        P("dp"),
        P("dp"),
        P("dp", "tensor"),
        P(("tensor", "dp")),
        P("tensor", "dp"),
        P("dp"),
        P("dp"),
        P("dp"),
    )
    out_specs = (
        P("dp", "ctx", None),
        P("dp", "ctx", None),
        P("dp", None, "tensor"),
        P(None, ("tensor", "dp")),
        P("tensor", "dp"),
        P("dp"),
        P("dp"),
        P("dp"),
        P("dp", "tensor"),
        P(("tensor", "dp")),
        P("tensor", "dp"),
        P("dp"),
        P("dp"),
        P("dp"),
    )
    n_dp = mesh.shape["dp"]
    on_device = make_device(n_dp, mesh.shape["ctx"], mesh.shape["tensor"], n_dp != 2)
    return jax.shard_map(
        on_device, mesh=mesh, in_specs=in_specs, out_specs=out_specs, check_vma=False
    )
```

time: 1060 us -> 490 us (0.46); the launches traced: 1040 us -> 485 us
  waiting for transfers between devices: 699 us -> 221 us
  starting transfers between devices: 0.58 us -> 136 us
  Pallas kernels: 0 us -> 96.3 us
  matrix products: 92 us -> 0 us
  other arithmetic: 87.1 us -> 10.1 us
  blocking collectives: 68.3 us -> 0 us
  local copies, waits for them, and re-layouts: 71.7 us -> 20.7 us
  between operations: 17.3 us -> 1.81 us
    psum x5 -> x0, waiting for transfers between devices: 476 us -> none  [the longest x1 152 us: on_device(): lax.psum(jnp.dot(mixed_low, combine_all, preferred_element_type=jnp.float...]
    ppermute x0 -> x87, waiting for transfers between devices: none -> 221 us  [the longest x85 191 us: swap(): return lambda v: lax.ppermute(v, axis, [(i, i ^ k) for i in range(size)])]
    reduce_scatter x2 -> x0, waiting for transfers between devices: 151 us -> none  [the longest x1 128 us: on_device(): lax.psum_scatter(jnp.concatenate([prompt_grads, window_grads], axis=1).as...]
    ppermute x0 -> x87, starting transfers between devices: none -> 136 us  [the longest x85 131 us: swap(): return lambda v: lax.ppermute(v, axis, [(i, i ^ k) for i in range(size)])]
    pallas_call x0 -> x15, Pallas kernels: none -> 96.3 us  [the longest x4 22 us: on_device(): call(functools.partial(fwd_body, k), (sds((wide, tile), BF), sds((8 * hea...]
    dot_general x26 -> x0, matrix products: 92 us -> none  [the longest x4 13.3 us: contract_rows(): lax.dot_general(left, right, (((0,), (0,)), ((), ())), preferred_element_...]
    all_gather x10 -> x0, blocking collectives: 53.4 us -> none  [the longest x1 11.9 us: on_device(): lax.all_gather(project, 'dp', axis=0, tiled=True)]
    unnamed x18 -> x0, waiting for transfers between devices: 49 us -> none
  transfers between devices with their start and end apart: 14 -> 87, of which waited for: 12 -> 28; matrix products, arithmetic and copies ran while one was open for 6% -> 4% of each run, Pallas kernels for 0% -> 14%
where the time goes in v1:
time: 490 us; the launch traced here: 485 us
  waiting for transfers between devices  221 us (45%)
  starting transfers between devices  136 us (28%)
  Pallas kernels  96.3 us (20%)
  local copies, waits for them, and re-layouts  20.7 us (4%)
  other arithmetic  10.1 us (2%)
    ppermute x85, waiting for transfers between devices, swap(): return lambda v: lax.ppermute(v, axis, [(i, i ^ k) for i in range(size)])  191 us
    ppermute x85, starting transfers between devices, swap(): return lambda v: lax.ppermute(v, axis, [(i, i ^ k) for i in range(size)])  131 us
    pallas_call x4, Pallas kernels, on_device(): call(functools.partial(fwd_body, k), (sds((wide, tile), BF), sds((8 * hea...  22 us
    pallas_call x1, Pallas kernels, on_device(): call(bwd_body, (sds((4, wide, tile), BF), *[sds((2 * wide, rows), BF)] *...  21.9 us
    ppermute x1, waiting for transfers between devices, on_device(): from_y = lax.ppermute(prompt_part, 'ctx', [(2, 0), (3, 1)])  21.3 us
    pallas_call x1, Pallas kernels, on_device(): call(mid_body, (sds((tile, width), BF), *[sds((wide, tile), BF)] * 4, *[s...  15 us
    unnamed x182, local copies, waits for them, and re-layouts  11.3 us
  transfers between devices with their start and end apart: 87, of which 28 were waited for; matrix products, arithmetic and copies ran while one was open for 4% of the time, Pallas kernels for 14%

profile of v1, /device:TPU:0, one launch (start us, length us, event | category | flops | bytes accessed | tf_op | source)
XLA Modules:
  0.0 485.3 jit_solution(17204979514045376780)
XLA Ops:
  16.3 50.0 %collective-permute-done.10.refs_10_ = bf16[8,384]{1,0:T(8,128)(2,1)S(1)} collective-permute-done((bf16[8,384]{1,0:T(8,128)(2,1)S(1)}, bf16[8,384]{1,0:T(8,128)(2,1)S(1)}, u32[]{:S(2)}, u32[]{:S(2)}) %collective-permute-start.10) | collective-permute-done | bytes 6176 | tf_op jit(solution)/shard_map/ppermute | solution.py:585
  91.8 8.3 %collective-permute-done.3.ra = bf16[384,1024]{1,0:T(8,128)(2,1)S(1)} collective-permute-done((bf16[384,1024]{1,0:T(8,128)(2,1)}, bf16[384,1024]{1,0:T(8,128)(2,1)S(1)}, u32[]{:S(2)}, u32[]{:S(2)}) %collective-permute-start.3) | collective-permute-done | bytes 786464 | tf_op jit(solution)/shard_map/ppermute | solution.py:708
  100.1 7.2 %collective-permute-done.15.refs_16_ = bf16[864,384]{1,0:T(8,128)(2,1)S(1)} collective-permute-done((bf16[864,384]{1,0:T(8,128)(2,1)S(1)}, bf16[864,384]{1,0:T(8,128)(2,1)S(1)}, u32[]{:S(2)}, u32[]{:S(2)}) %collective-permute-start.15) | collective-permute-done | bytes 663584 | tf_op jit(solution)/shard_map/ppermute | solution.py:585
  109.5 12.1 %collective-permute-done.19.refs_20_ = bf16[864,384]{1,0:T(8,128)(2,1)S(1)} collective-permute-done((bf16[864,384]{1,0:T(8,128)(2,1)}, bf16[864,384]{1,0:T(8,128)(2,1)S(1)}, u32[]{:S(2)}, u32[]{:S(2)}) %collective-permute-start.19) | collective-permute-done | bytes 663584 | tf_op jit(solution)/shard_map/ppermute | solution.py:585
  122.5 13.4 %collective-permute-done.23.refs_24_ = bf16[864,384]{1,0:T(8,128)(2,1)} collective-permute-done((bf16[864,384]{1,0:T(8,128)(2,1)}, bf16[864,384]{1,0:T(8,128)(2,1)}, u32[]{:S(2)}, u32[]{:S(2)}) %collective-permute-start.23) | collective-permute-done | bytes 663584 | tf_op jit(solution)/shard_map/ppermute | solution.py:585
  135.9 13.8 %collective-permute-done.27.refs_28_ = bf16[864,384]{1,0:T(8,128)(2,1)} collective-permute-done((bf16[864,384]{1,0:T(8,128)(2,1)}, bf16[864,384]{1,0:T(8,128)(2,1)}, u32[]{:S(2)}, u32[]{:S(2)}) %collective-permute-start.27) | collective-permute-done | bytes 663584 | tf_op jit(solution)/shard_map/ppermute | solution.py:585
  153.2 5.5 %shard_map.267 = (bf16[192,256]{1,0:T(8,128)(2,1)}, f32[24,256]{1,0:T(8,128)}) custom-call(s32[14]{0:T(128)} %concatenate.35.sc, bf16[192,1024]{1,0:T(8,128)(2,1)} %get-tuple-element.52.q_ref, s32[8,1024]{1,0:T(8,128)} %add_add_fusion.span_ref, bf16[384,1024]{1,0:T(8,128)(2,1)} %get-tuple-element.53.own, bf16[384,1024]{1,0:T(8,128)(2,1)} %copy-done.3, ...), custom_call_target="tpu_custom_call" | custom-call | flops 226492416 | bytes 1572864 | tf_op jit(solution)/shard_map/pallas_call | solution.py:715
  158.7 5.5 %shard_map.266 = (bf16[192,256]{1,0:T(8,128)(2,1)}, f32[24,256]{1,0:T(8,128)}) custom-call(s32[14]{0:T(128)} %concatenate.35.sc, bf16[192,1024]{1,0:T(8,128)(2,1)} %get-tuple-element.52.q_ref, s32[8,1024]{1,0:T(8,128)} %add_add_fusion.span_ref, bf16[384,1024]{1,0:T(8,128)(2,1)} %get-tuple-element.53.own, bf16[384,1024]{1,0:T(8,128)(2,1)} %copy-done.3, ...), custom_call_target="tpu_custom_call" | custom-call | flops 226492416 | bytes 1572864 | tf_op jit(solution)/shard_map/pallas_call | solution.py:715
  164.2 5.5 %shard_map.265 = (bf16[192,256]{1,0:T(8,128)(2,1)}, f32[24,256]{1,0:T(8,128)}) custom-call(s32[14]{0:T(128)} %concatenate.35.sc, bf16[192,1024]{1,0:T(8,128)(2,1)} %get-tuple-element.52.q_ref, s32[8,1024]{1,0:T(8,128)} %add_add_fusion.span_ref, bf16[384,1024]{1,0:T(8,128)(2,1)} %get-tuple-element.53.own, bf16[384,1024]{1,0:T(8,128)(2,1)} %copy-done.3, ...), custom_call_target="tpu_custom_call" | custom-call | flops 226492416 | bytes 1572864 | tf_op jit(solution)/shard_map/pallas_call | solution.py:715
  176.3 5.6 %shard_map.264 = (bf16[192,256]{1,0:T(8,128)(2,1)}, f32[24,256]{1,0:T(8,128)}) custom-call(s32[14]{0:T(128)} %concatenate.35.sc, bf16[192,1024]{1,0:T(8,128)(2,1)} %get-tuple-element.52.q_ref, s32[8,1024]{1,0:T(8,128)} %add_add_fusion.span_ref, bf16[384,1024]{1,0:T(8,128)(2,1)} %get-tuple-element.53.own, bf16[384,1024]{1,0:T(8,128)(2,1)} %copy-done.3, ...), custom_call_target="tpu_custom_call" | custom-call | flops 226492416 | bytes 1572864 | tf_op jit(solution)/shard_map/pallas_call | solution.py:715
  182.7 15.0 %shard_map.268 = (bf16[256,768]{1,0:T(8,128)(2,1)}, bf16[192,256]{1,0:T(8,128)(2,1)}, bf16[192,256]{1,0:T(8,128)(2,1)}, bf16[192,256]{1,0:T(8,128)(2,1)}, bf16[1...) custom-call(s32[14]{0:T(128)} %concatenate.35.sc, ...), custom_call_target="tpu_custom_call" | custom-call | flops 5435817984 | bytes 9437184 | tf_op jit(solution)/shard_map/pallas_call | solution.py:727
  207.5 9.4 %shard_map.276 = (bf16[2,4,432,384]{3,2,1,0:T(8,128)(2,1)}, bf16[2,4,432,384]{3,2,1,0:T(8,128)(2,1)}) custom-call(s32[14]{0:T(128)} %concatenate.35.sc, bf16[256,768]{1,0:T(8,128)(2,1)} %get-tuple-element.76.refs_0_, bf16[256,768]{1,0:T(8,128)(2,1)} %get-tuple-element.77.refs_1_, bf16[256,768]{1,0:T(8,128)(2,1)} %get-tuple-element.78.refs_2_, ...), custom_call_target="tpu_custom_call" | custom-call | flops 2415919104 | bytes 9437184 | tf_op jit(solution)/shard_map/pallas_call | solution.py:762
  223.6 4.9 %collective-permute-done.33.refs_10_ = bf16[192,256]{1,0:T(8,128)(2,1)S(1)} collective-permute-done((bf16[192,256]{1,0:T(8,128)(2,1)S(1)}, bf16[192,256]{1,0:T(8,128)(2,1)S(1)}, u32[]{:S(2)}, u32[]{:S(2)}) %collective-permute-start.33) | collective-permute-done | bytes 98336 | tf_op jit(solution)/shard_map/ppermute | solution.py:585
  229.2 21.9 %shard_map.270 = (bf16[4,192,256]{2,1,0:T(8,128)(2,1)}, bf16[384,1024]{1,0:T(8,128)(2,1)}, bf16[384,1024]{1,0:T(8,128)(2,1)}, bf16[384,1024]{1,0:T(8,128)(2,1)}, bf16[384,1024]{1,0:T(8,128)(2,1)}) custom-call(s32[14]{0:T(128)} %concatenate.35.sc, bf16[192,1024]{1,0:T(8,128)(2,1)} %get-tuple-element.52.q_ref, s32[8,1024]{1,0:T(8,128)} %add_add_fusion.span_ref, ...), custom_call_target="tpu_custom_call" | custom-call | flops 2264924160 | bytes 3145728 | tf_op jit(solution)/shard_map/pallas_call | solution.py:769
  261.3 21.3 %collective-permute-done.40.c_ref = bf16[384,1024]{1,0:T(8,128)(2,1)S(1)} collective-permute-done((bf16[384,1024]{1,0:T(8,128)(2,1)S(1)}, bf16[384,1024]{1,0:T(8,128)(2,1)S(1)}, u32[]{:S(2)}, u32[]{:S(2)}) %collective-permute-start.40) | collective-permute-done | bytes 786464 | tf_op jit(solution)/shard_map/ppermute | solution.py:788
  297.1 6.5 %collective-permute-start.55 = (bf16[288,384]{1,0:T(8,128)(2,1)S(1)}, bf16[288,384]{1,0:T(8,128)(2,1)S(1)}, u32[]{:S(2)}, u32[]{:S(2)}) collective-permute-start(bf16[288,384]{1,0:T(8,128)(2,1)S(1)} %constant_dynamic-slice_fusion.1.refs_9_), channel_id=1, source_target_pairs={{0,3},{1,2},{2,1},{3,0},{4,7},{5,6},{6,5},{7,4},{8,11},{9,10},{10,... | collective-permute-start | bytes 663560 | tf_op jit(solution)/shard_map/ppermute | solution.py:585
  304.9 21.7 %collective-permute-done.69 = f32[16,768]{1,0:T(8,128)S(1)} collective-permute-done((f32[16,768]{1,0:T(8,128)S(1)}, f32[16,768]{1,0:T(8,128)S(1)}, u32[]{:S(2)}, u32[]{:S(2)}) %collective-permute-start.69) | collective-permute-done | bytes 49184 | tf_op jit(solution)/shard_map/ppermute | solution.py:585
  346.5 6.7 %collective-permute-start.36 = (bf16[192,256]{1,0:T(8,128)(2,1)S(1)}, bf16[192,256]{1,0:T(8,128)(2,1)S(1)}, u32[]{:S(2)}, u32[]{:S(2)}) collective-permute-start(bf16[192,256]{1,0:T(8,128)(2,1)S(1)} %get-tuple-element.107), channel_id=1, source_target_pairs={{0,2},{1,3},{2,0},{3,1},{4,6},{5,7},{6,4},{7,5},{8,10},{9,11},{10,... | collective-permute-start | bytes 294920 | tf_op jit(solution)/shard_map/ppermute | solution.py:585
  368.8 7.3 %collective-permute-done.42.refs_6_ = bf16[384,256]{1,0:T(8,128)(2,1)S(1)} collective-permute-done((bf16[384,256]{1,0:T(8,128)(2,1)S(1)}, bf16[384,256]{1,0:T(8,128)(2,1)S(1)}, u32[]{:S(2)}, u32[]{:S(2)}) %collective-permute-start.42) | collective-permute-done | bytes 196640 | tf_op jit(solution)/shard_map/ppermute | solution.py:585
  379.7 15.6 %collective-permute-start.29 = (bf16[256,768]{1,0:T(8,128)(2,1)S(1)}, bf16[256,768]{1,0:T(8,128)(2,1)S(1)}, u32[]{:S(2)}, u32[]{:S(2)}) collective-permute-start(bf16[256,768]{1,0:T(8,128)(2,1)S(1)} %copy-done.19), channel_id=1, source_target_pairs={{0,1},{1,0},{2,3},{3,2},{4,5},{5,4},{6,7},{7,6},{8,9},{9,8},{10,11... | collective-permute-start | bytes 1179656 | tf_op jit(solution)/shard_map/ppermute | solution.py:585
  395.3 6.1 %shard_map.272.refs_0_ = bf16[256,768]{1,0:T(8,128)(2,1)} custom-call(s32[14]{0:T(128)} %concatenate.35.sc, bf16[192,256]{1,0:T(8,128)(2,1)} %get-tuple-element.109.refs_0_, bf16[192,256]{1,0:T(8,128)(2,1)} %copy-done.49, bf16[192,256]{1,0:T(8,128)(2,1)} %copy-done.50, bf16[192,256]{1,0:T(8,128)(2,1)} %copy-done.51, ...), custom_call_target="tpu_custom_call" | custom-call | flops 905969664 | bytes 3538944 | tf_op jit(solution)/shard_map/pallas_call | solution.py:806
  406.5 19.8 %collective-permute-start.59 = (bf16[256,768]{1,0:T(8,128)(2,1)}, bf16[256,768]{1,0:T(8,128)(2,1)S(1)}, u32[]{:S(2)}, u32[]{:S(2)}) collective-permute-start(bf16[256,768]{1,0:T(8,128)(2,1)} %shard_map.272.refs_0_), channel_id=1, source_target_pairs={{0,1},{1,0},{2,3},{3,2},{4,5},{5,4},{6,7},{7,6},{8,9},{9,8},{10,11... | collective-permute-start | bytes 1179656 | tf_op jit(solution)/shard_map/ppermute | solution.py:585
  434.9 11.4 %collective-permute-start.60 = (bf16[256,768]{1,0:T(8,128)(2,1)S(1)}, bf16[256,768]{1,0:T(8,128)(2,1)S(1)}, u32[]{:S(2)}, u32[]{:S(2)}) collective-permute-start(bf16[256,768]{1,0:T(8,128)(2,1)S(1)} %copy-done.7), channel_id=1, source_target_pairs={{0,2},{1,3},{2,0},{3,1},{4,6},{5,7},{6,4},{7,5},{8,10},{9,11},{10,... | collective-permute-start | bytes 1179656 | tf_op jit(solution)/shard_map/ppermute | solution.py:585
  451.4 21.0 %collective-permute-done.60.refs_2_ = bf16[256,768]{1,0:T(8,128)(2,1)S(1)} collective-permute-done((bf16[256,768]{1,0:T(8,128)(2,1)S(1)}, bf16[256,768]{1,0:T(8,128)(2,1)S(1)}, u32[]{:S(2)}, u32[]{:S(2)}) %collective-permute-start.60) | collective-permute-done | bytes 393248 | tf_op jit(solution)/shard_map/ppermute | solution.py:585
  (404 shorter events, 168.2 us)
Async XLA Ops:
  2.8 86.8 %collective-permute-start.17 = (bf16[864,384]{1,0:T(8,128)(2,1)S(1)}, bf16[864,384]{1,0:T(8,128)(2,1)}, u32[]{:S(2)}, u32[]{:S(2)}) collective-permute-start(bf16[864,384]{1,0:T(8,128)(2,1)S(1)} %pad_maximum_fusion.refs_14_), channel_id=1, source_target_pairs={{0,1},{1,0},{2,3},{3,2},{4,5},{5,4},{6,7},{7,6},{8,9},{9,8},{10,11... | collective-permute-start | bytes 1990664 | tf_op jit(solution)/shard_map/ppermute | solution.py:585
  5.9 84.5 %collective-permute-start.21 = (bf16[864,384]{1,0:T(8,128)(2,1)S(1)}, bf16[864,384]{1,0:T(8,128)(2,1)}, u32[]{:S(2)}, u32[]{:S(2)}) collective-permute-start(bf16[864,384]{1,0:T(8,128)(2,1)S(1)} %pad_maximum_fusion.refs_14_), channel_id=1, source_target_pairs={{0,2},{1,3},{2,0},{3,1},{4,6},{5,7},{6,4},{7,5},{8,10},{9,11},{10,... | collective-permute-start | bytes 1990664 | tf_op jit(solution)/shard_map/ppermute | solution.py:585
  8.5 82.1 %collective-permute-start.25 = (bf16[864,384]{1,0:T(8,128)(2,1)S(1)}, bf16[864,384]{1,0:T(8,128)(2,1)}, u32[]{:S(2)}, u32[]{:S(2)}) collective-permute-start(bf16[864,384]{1,0:T(8,128)(2,1)S(1)} %pad_maximum_fusion.refs_14_), channel_id=1, source_target_pairs={{0,3},{1,2},{2,1},{3,0},{4,7},{5,6},{6,5},{7,4},{8,11},{9,10},{10,... | collective-permute-start | bytes 1990664 | tf_op jit(solution)/shard_map/ppermute | solution.py:585
  10.5 55.8 %collective-permute-start.10 = (bf16[8,384]{1,0:T(8,128)(2,1)S(1)}, bf16[8,384]{1,0:T(8,128)(2,1)S(1)}, u32[]{:S(2)}, u32[]{:S(2)}) collective-permute-start(bf16[8,384]{1,0:T(8,128)(2,1)S(1)} %stack.58.refs_6_), channel_id=1, source_target_pairs={{0,2},{1,3},{2,0},{3,1},{4,6},{5,7},{6,4},{7,5},{8,10},{9,11},{10,... | collective-permute-start | bytes 18440 | tf_op jit(solution)/shard_map/ppermute | solution.py:585
  13.1 54.8 %collective-permute-start.12 = (bf16[8,384]{1,0:T(8,128)(2,1)S(1)}, bf16[8,384]{1,0:T(8,128)(2,1)S(1)}, u32[]{:S(2)}, u32[]{:S(2)}) collective-permute-start(bf16[8,384]{1,0:T(8,128)(2,1)S(1)} %stack.58.refs_6_), channel_id=1, source_target_pairs={{0,3},{1,2},{2,1},{3,0},{4,7},{5,6},{6,5},{7,4},{8,11},{9,10},{10,... | collective-permute-start | bytes 18440 | tf_op jit(solution)/shard_map/ppermute | solution.py:585
  90.6 31.0 %collective-permute-start.19 = (bf16[864,384]{1,0:T(8,128)(2,1)}, bf16[864,384]{1,0:T(8,128)(2,1)S(1)}, u32[]{:S(2)}, u32[]{:S(2)}) collective-permute-start(bf16[864,384]{1,0:T(8,128)(2,1)} %collective-permute-done.17.refs_18_), channel_id=1, source_target_pairs={{0,16},{16,0},{1,17},{17,1},{2,18},{18,2},{3,19},{19,3},{4,20},{20... | collective-permute-start | bytes 1990664 | tf_op jit(solution)/shard_map/ppermute | solution.py:585
  100.1 50.2 %collective-permute-start.4 = (bf16[384,1024]{1,0:T(8,128)(2,1)S(1)}, bf16[384,1024]{1,0:T(8,128)(2,1)S(1)}, u32[]{:S(2)}, u32[]{:S(2)}) collective-permute-start(bf16[384,1024]{1,0:T(8,128)(2,1)S(1)} %collective-permute-done.3.ra), channel_id=1, source_target_pairs={{0,4},{4,0},{8,12},{12,8},{1,5},{5,1},{9,13},{13,9},{2,6},{6,2},{1... | collective-permute-start | bytes 2359304 | tf_op jit(solution)/shard_map/ppermute | solution.py:585
  108.1 41.5 %collective-permute-start.27 = (bf16[864,384]{1,0:T(8,128)(2,1)}, bf16[864,384]{1,0:T(8,128)(2,1)}, u32[]{:S(2)}, u32[]{:S(2)}) collective-permute-start(bf16[864,384]{1,0:T(8,128)(2,1)} %collective-permute-done.25.refs_26_), channel_id=1, source_target_pairs={{0,16},{16,0},{1,17},{17,1},{2,18},{18,2},{3,19},{19,3},{4,20},{20... | collective-permute-start | bytes 1990664 | tf_op jit(solution)/shard_map/ppermute | solution.py:585
  109.4 40.3 %collective-permute-start.18 = (bf16[864,384]{1,0:T(8,128)(2,1)}, bf16[864,384]{1,0:T(8,128)(2,1)}, u32[]{:S(2)}, u32[]{:S(2)}) collective-permute-start(bf16[864,384]{1,0:T(8,128)(2,1)} %collective-permute-done.17.refs_18_), channel_id=1, source_target_pairs={{0,4},{4,0},{8,12},{12,8},{1,5},{5,1},{9,13},{13,9},{2,6},{6,2},{1... | collective-permute-start | bytes 1990664 | tf_op jit(solution)/shard_map/ppermute | solution.py:585
  135.9 33.9 %collective-permute-start.26 = (bf16[864,384]{1,0:T(8,128)(2,1)}, bf16[864,384]{1,0:T(8,128)(2,1)}, u32[]{:S(2)}, u32[]{:S(2)}) collective-permute-start(bf16[864,384]{1,0:T(8,128)(2,1)} %collective-permute-done.25.refs_26_), channel_id=1, source_target_pairs={{0,4},{4,0},{8,12},{12,8},{1,5},{5,1},{9,13},{13,9},{2,6},{6,2},{1... | collective-permute-start | bytes 1990664 | tf_op jit(solution)/shard_map/ppermute | solution.py:585
  150.2 31.8 %collective-permute-start.24 = (bf16[864,384]{1,0:T(8,128)(2,1)}, bf16[864,384]{1,0:T(8,128)(2,1)}, u32[]{:S(2)}, u32[]{:S(2)}) collective-permute-start(bf16[864,384]{1,0:T(8,128)(2,1)} %collective-permute-done.23.refs_24_), channel_id=1, source_target_pairs={{0,4},{4,0},{8,12},{12,8},{1,5},{5,1},{9,13},{13,9},{2,6},{6,2},{1... | collective-permute-start | bytes 1990664 | tf_op jit(solution)/shard_map/ppermute | solution.py:585
  150.3 31.7 %collective-permute-start.28 = (bf16[864,384]{1,0:T(8,128)(2,1)}, bf16[864,384]{1,0:T(8,128)(2,1)}, u32[]{:S(2)}, u32[]{:S(2)}) collective-permute-start(bf16[864,384]{1,0:T(8,128)(2,1)} %collective-permute-done.27.refs_28_), channel_id=1, source_target_pairs={{0,4},{4,0},{8,12},{12,8},{1,5},{5,1},{9,13},{13,9},{2,6},{6,2},{1... | collective-permute-start | bytes 1990664 | tf_op jit(solution)/shard_map/ppermute | solution.py:585
  216.9 74.5 %collective-permute-start.79 = (bf16[2,4,432,384]{3,2,1,0:T(8,128)(2,1)}, bf16[2,4,432,384]{3,2,1,0:T(8,128)(2,1)}, u32[]{:S(2)}, u32[]{:S(2)}) collective-permute-start(bf16[2,4,432,384]{3,2,1,0:T(8,128)(2,1)} %get-tuple-element.86), channel_id=1, source_target_pairs={{0,16},{16,0},{1,17},{17,1},{2,18},{18,2},{3,19},{19,3},{4,20},{20... | collective-permute-start | bytes 7962632 | tf_op jit(solution)/shard_map/ppermute | solution.py:585
  258.5 38.7 %collective-permute-start.47 = (bf16[288,384]{1,0:T(8,128)(2,1)S(1)}, bf16[288,384]{1,0:T(8,128)(2,1)S(1)}, u32[]{:S(2)}, u32[]{:S(2)}) collective-permute-start(bf16[288,384]{1,0:T(8,128)(2,1)S(1)} %constant_dynamic-slice_fusion.1.refs_9_), channel_id=1, source_target_pairs={{0,1},{1,0},{2,3},{3,2},{4,5},{5,4},{6,7},{7,6},{8,9},{9,8},{10,11... | collective-permute-start | bytes 663560 | tf_op jit(solution)/shard_map/ppermute | solution.py:585
  261.3 42.3 %collective-permute-start.51 = (bf16[288,384]{1,0:T(8,128)(2,1)S(1)}, bf16[288,384]{1,0:T(8,128)(2,1)S(1)}, u32[]{:S(2)}, u32[]{:S(2)}) collective-permute-start(bf16[288,384]{1,0:T(8,128)(2,1)S(1)} %constant_dynamic-slice_fusion.1.refs_9_), channel_id=1, source_target_pairs={{0,2},{1,3},{2,0},{3,1},{4,6},{5,7},{6,4},{7,5},{8,10},{9,11},{10,... | collective-permute-start | bytes 663560 | tf_op jit(solution)/shard_map/ppermute | solution.py:585
  294.0 59.3 %collective-permute-start.80 = (bf16[4,432,384]{2,1,0:T(8,128)(2,1)S(1)}, bf16[4,432,384]{2,1,0:T(8,128)(2,1)S(1)}, u32[]{:S(2)}, u32[]{:S(2)}) collective-permute-start(bf16[4,432,384]{2,1,0:T(8,128)(2,1)S(1)} %slice_bitcast_fusion), channel_id=1, source_target_pairs={{0,8},{4,12},{8,0},{12,4},{1,9},{5,13},{9,1},{13,5},{2,10},{6,14},... | collective-permute-start | bytes 3981320 | tf_op jit(solution)/shard_map/ppermute | solution.py:585
  295.0 34.7 %collective-permute-start.62 = (bf16[2,2,144,384]{3,2,1,0:T(8,128)(2,1)S(1)}, bf16[2,2,144,384]{3,2,1,0:T(8,128)(2,1)S(1)}, u32[]{:S(2)}, u32[]{:S(2)}) collective-permute-start(bf16[2,2,144,384]{3,2,1,0:T(8,128)(2,1)S(1)} %slice_bitcast_fusion.2), channel_id=1, source_target_pairs={{0,4},{4,0},{8,12},{12,8},{1,5},{5,1},{9,13},{13,9},{2,6},{6,2},{1... | collective-permute-start | bytes 1327112 | tf_op jit(solution)/shard_map/ppermute | solution.py:585
  362.1 39.2 %collective-permute-start.63 = (bf16[2,144,384]{2,1,0:T(8,128)(2,1)S(1)}, bf16[2,144,384]{2,1,0:T(8,128)(2,1)}, u32[]{:S(2)}, u32[]{:S(2)}) collective-permute-start(bf16[2,144,384]{2,1,0:T(8,128)(2,1)S(1)} %slice_bitcast_fusion.7), channel_id=1, source_target_pairs={{0,8},{4,12},{8,0},{12,4},{1,9},{5,13},{9,1},{13,5},{2,10},{6,14},... | collective-permute-start | bytes 663560 | tf_op jit(solution)/shard_map/ppermute | solution.py:585
  363.4 41.0 %collective-permute-start.81 = (bf16[432,384]{1,0:T(8,128)(2,1)}, bf16[432,384]{1,0:T(8,128)(2,1)}, u32[]{:S(2)}, u32[]{:S(2)}) collective-permute-start(bf16[432,384]{1,0:T(8,128)(2,1)} %get-tuple-element.99), channel_id=1, source_target_pairs={{0,1},{1,0},{2,3},{3,2},{4,5},{5,4},{6,7},{7,6},{8,9},{9,8},{10,11... | collective-permute-start | bytes 995336 | tf_op jit(solution)/shard_map/ppermute | solution.py:585
  366.7 39.2 %collective-permute-start.82 = (bf16[432,384]{1,0:T(8,128)(2,1)}, bf16[432,384]{1,0:T(8,128)(2,1)}, u32[]{:S(2)}, u32[]{:S(2)}) collective-permute-start(bf16[432,384]{1,0:T(8,128)(2,1)} %get-tuple-element.101), channel_id=1, source_target_pairs={{0,2},{1,3},{2,0},{3,1},{4,6},{5,7},{6,4},{7,5},{8,10},{9,11},{10,... | collective-permute-start | bytes 995336 | tf_op jit(solution)/shard_map/ppermute | solution.py:585
  379.7 48.0 %collective-permute-start.29 = (bf16[256,768]{1,0:T(8,128)(2,1)S(1)}, bf16[256,768]{1,0:T(8,128)(2,1)S(1)}, u32[]{:S(2)}, u32[]{:S(2)}) collective-permute-start(bf16[256,768]{1,0:T(8,128)(2,1)S(1)} %copy-done.19), channel_id=1, source_target_pairs={{0,1},{1,0},{2,3},{3,2},{4,5},{5,4},{6,7},{7,6},{8,9},{9,8},{10,11... | collective-permute-start | bytes 1179656 | tf_op jit(solution)/shard_map/ppermute | solution.py:585
  401.4 32.8 %collective-permute-start.30 = (bf16[256,768]{1,0:T(8,128)(2,1)S(1)}, bf16[256,768]{1,0:T(8,128)(2,1)S(1)}, u32[]{:S(2)}, u32[]{:S(2)}) collective-permute-start(bf16[256,768]{1,0:T(8,128)(2,1)S(1)} %copy-done.19), channel_id=1, source_target_pairs={{0,2},{1,3},{2,0},{3,1},{4,6},{5,7},{6,4},{7,5},{8,10},{9,11},{10,... | collective-permute-start | bytes 1179656 | tf_op jit(solution)/shard_map/ppermute | solution.py:585
  406.5 44.4 %collective-permute-start.59 = (bf16[256,768]{1,0:T(8,128)(2,1)}, bf16[256,768]{1,0:T(8,128)(2,1)S(1)}, u32[]{:S(2)}, u32[]{:S(2)}) collective-permute-start(bf16[256,768]{1,0:T(8,128)(2,1)} %shard_map.272.refs_0_), channel_id=1, source_target_pairs={{0,1},{1,0},{2,3},{3,2},{4,5},{5,4},{6,7},{7,6},{8,9},{9,8},{10,11... | collective-permute-start | bytes 1179656 | tf_op jit(solution)/shard_map/ppermute | solution.py:585
  434.9 37.5 %collective-permute-start.60 = (bf16[256,768]{1,0:T(8,128)(2,1)S(1)}, bf16[256,768]{1,0:T(8,128)(2,1)S(1)}, u32[]{:S(2)}, u32[]{:S(2)}) collective-permute-start(bf16[256,768]{1,0:T(8,128)(2,1)S(1)} %copy-done.7), channel_id=1, source_target_pairs={{0,2},{1,3},{2,0},{3,1},{4,6},{5,7},{6,4},{7,5},{8,10},{9,11},{10,... | collective-permute-start | bytes 1179656 | tf_op jit(solution)/shard_map/ppermute | solution.py:585
  (154 other events, 2821.1 us)

commit v2 on v1

--- a/solution.py
+++ b/solution.py
@@ -6,6 +6,7 @@
 from jax import lax
 from jax.experimental import pallas as pl
 from jax.experimental.pallas import tpu as pltpu
+from jax.sharding import Mesh
 from jax.sharding import PartitionSpec as P
 
 P_SIZE = 2048
@@ -64,16 +65,51 @@
 CTX, Z, X, C, Y, PAIR = 0, 1, 2, 3, 4, 8
 
 
-def qkv_body(sc, x_ref, w0_ref, w1_ref, bias_ref, q_ref, kv_ref):
-    half = w0_ref.shape[1]
+def qkv_body(sc, x_ref, own_ref, small_ref, w0_ref, w1_ref, q_ref, kv_ref, wt_ref, oth, row):
+    half = own_ref.shape[1]
     wide = q_ref.shape[0]
-    acc = bias_ref[...].astype(F32)
+    part = own_ref.shape[0] // 2
+    hq = wide // 2
+    oth[pl.ds(mult(sc[C], part), part), :] = w0_ref[:part, :]
+    oth[pl.ds(mult(1 - sc[C], part), part), :] = w1_ref[:part, :]
+    mine, theirs = small_ref[...].astype(BF), w0_ref[part:, :]
+    even = jnp.where(sc[X] == 0, mine, theirs)
+    odd = jnp.where(sc[X] == 0, theirs, mine)
+    row[...] = jnp.zeros_like(row)
+    for at, rank in ((0, 7), (2 * wide, 8)):
+        row[0:1, at : at + hq] = even[rank : rank + 1, :hq]
+        row[0:1, at + hq : at + wide] = odd[rank : rank + 1, :hq]
     a0 = x_ref[:, pl.ds(mult(sc[X], half), half)]
     a1 = x_ref[:, pl.ds(mult(1 - sc[X], half), half)]
-    out = dot_t(w0_ref[...], a0) + dot_t(w1_ref[...], a1) + acc
-    low = out.astype(BF)
+    first = lax.broadcasted_iota(jnp.int32, (row.shape[0], x_ref.shape[0]), 0) == 0
+    bias = tdot(row[...], jnp.where(first, 1.0, 0.0).astype(BF))
+    low = (dot_t(own_ref[...], a0) + dot_t(oth[...], a1) + bias).astype(BF)
     q_ref[...] = low[:wide] * jnp.asarray(HD**-0.5, BF)
     kv_ref[...] = low[wide:]
+    wt_ref[:, pl.ds(mult(sc[X], half), half)] = own_ref[...]
+    wt_ref[:, pl.ds(mult(1 - sc[X], half), half)] = oth[...]
+
+
+def pack_body(sc, *refs):
+    wt, e_ref, s_ref, m_ref, off = refs[0:5]
+    vecs = refs[5:12]
+    small, wtc, wc = refs[12:15]
+    part = wt.shape[0] // 2
+    hb = e_ref.shape[1] // 2
+    hw = m_ref.shape[0] // 2
+    half = s_ref.shape[1]
+    c = sc[C]
+    small[...] = jnp.zeros_like(small)
+    for i, vec in enumerate(vecs):
+        small[i : i + 1, :] = vec[...].astype(F32).reshape(1, half)
+    small[7:9, : off.shape[1]] = off[...].astype(F32)
+    low = small[...].astype(BF)
+    wtc[:part, :] = wt[pl.ds(mult(c, part), part), :]
+    wtc[part:, :] = low
+    wc[:half, :] = e_ref[:, pl.ds(mult(c, hb), hb)]
+    wc[half : half + hb, :] = s_ref[pl.ds(mult(c, hb), hb), :]
+    wc[half + hb : half + hb + hw, :] = m_ref[pl.ds(mult(c, hw), hw), :]
+    wc[half + hb + hw :, :] = low
 
 
 def load_pairs(sc, own, par, ra, rb, pbuf, cbuf, sems):
@@ -309,9 +345,8 @@
 
 def mid_body(sc, *refs):
     mixed = refs[0:4]
-    x_ref, cot_ref = refs[4:6]
-    packs = refs[6:14]
-    pieces = refs[14:30]
+    x_hbm, cot_hbm = refs[4:6]
+    packs = refs[6:8]
     (
         out_ref,
         mb0,
@@ -328,9 +363,8 @@
         mix_own,
         mix_oth,
         gf_ref,
-        small_ref,
-    ) = refs[30:46]
-    we, ws, wc, mix_s, act_s, gp_s, ib_s, vec_s, thr_s, mb_s, sems, osems = refs[46:]
+    ) = refs[8:23]
+    we, ws, wc, mix_s, act_s, gp_s, ib_s, vec_s, thr_s, mb_s, pk_s, x_ref, cot_ref, small_ref, sems, psems = refs[23:]
     wide, tile = mixed[0].shape
     width = x_ref.shape[1]
     half = width // 2
@@ -339,49 +373,53 @@
     hb = block // 2
     hw = wide // 2
     c = sc[C]
+    n_pack = half + hb + hw + 16
 
     stages = [[], [], []]
-    for k in range(4):
-        z = sc[Z] ^ k
-        for j in range(2):
-            xc = pl.ds(mult(sc[X] ^ j, half), half)
+    small = []
+
+    def move(stage, src, dst):
+        n = len(stages[stage])
+        stages[stage].append(pltpu.make_async_copy(src, dst, sems.at[stage, n]))
+
+    for xh in range(2):
+        xc = pl.ds(xh * half, half)
+        for z in range(4):
+            at = (xh * 4 + z) * n_pack
             for i in range(2):
                 cc = c ^ i
-                piece = pieces[k * 4 + j * 2 + i]
-                n = len(stages[0])
-                stages[0].append(
-                    pltpu.make_async_copy(
-                        piece.at[pl.ds(half + hb, hw), :],
-                        wc.at[pl.ds(pl.multiple_of(z * wide + cc * hw, hw), hw), xc],
-                        sems.at[0, n],
-                    )
+                rows = pl.multiple_of(z * wide + cc * hw, hw)
+                move(
+                    0,
+                    packs[i].at[pl.ds(at + half + hb, hw), :],
+                    wc.at[pl.ds(rows, hw), xc],
                 )
-                stages[1].append(
-                    pltpu.make_async_copy(
-                        piece.at[pl.ds(0, half), :],
-                        we.at[xc, pl.ds(pl.multiple_of(z * block + cc * hb, hb), hb)],
-                        sems.at[1, n],
-                    )
+                place = pl.ds(pl.multiple_of(z * block + cc * hb, hb), hb)
+                move(1, packs[i].at[pl.ds(at, half), :], we.at[xc, place])
+                move(2, packs[i].at[pl.ds(at + half, hb), :], ws.at[place, xc])
+            n = xh * 4 + z
+            small.append(
+                pltpu.make_async_copy(
+                    packs[0].at[pl.ds(at + half + hb + hw, 16), :], pk_s.at[n], psems.at[n]
                 )
-                stages[2].append(
-                    pltpu.make_async_copy(
-                        piece.at[pl.ds(half, hb), :],
-                        ws.at[pl.ds(pl.multiple_of(z * block + cc * hb, hb), hb), xc],
-                        sems.at[2, n],
-                    )
-                )
-    for stage in stages:
+            )
+    mine = pl.ds(mult(sc[Z], tile), tile)
+    small.append(pltpu.make_async_copy(x_hbm.at[mine, :], x_ref, psems.at[8]))
+    small.append(pltpu.make_async_copy(cot_hbm.at[mine, :], cot_ref, psems.at[9]))
+    for stage in [small] + stages:
         for copy in stage:
             copy.start()
 
+    for copy in small:
+        copy.wait()
     for k in range(4):
         mix_s[pl.ds(mult(sc[Z] ^ k, wide), wide), :] = mixed[k][...]
-        for j in range(2):
-            pack = packs[k * 2 + j]
-            at = pl.multiple_of((sc[Z] ^ k) * block + (sc[X] ^ j) * half, 128)
-            thr_s[:, pl.ds(at, half)] = pack[...].astype(F32)
-            if k == 0:
-                vec_s[:, pl.ds(mult(sc[X] ^ j, half), half)] = pack[...].astype(F32)
+    for xh in range(2):
+        for z in range(4):
+            pack = pk_s[xh * 4 + z].astype(F32)
+            at = z * block + xh * half
+            thr_s[:, at : at + half] = pack[:8]
+        vec_s[:, xh * half : (xh + 1) * half] = pk_s[xh * 4].astype(F32)[:8]
 
     baseline = vec_s[0:1, :]
     scaling = vec_s[1:2, :]
@@ -413,7 +451,7 @@
         feed = feed + dot(active, ws[cols, :])
     second = normed + feed + settling
     n2, inv2 = norm(second)
-    out_ref[...] = (n2 * rescaling + reshifting).astype(BF)
+    out_ref[:tile, :] = (n2 * rescaling + reshifting).astype(BF)
     dy = cot_ref[...].astype(F32)
     small_ref[...] = jnp.zeros_like(small_ref)
     small_ref[4:5, :] = jnp.sum(dy * n2, axis=0, keepdims=True)
@@ -432,6 +470,7 @@
     small_ref[2:3, :] = jnp.sum(grad, axis=0, keepdims=True)
     grad_first = norm_back(scaling * grad, n1, inv1)
     small_ref[0:1, :] = jnp.sum(grad_first, axis=0, keepdims=True)
+    out_ref[tile:, :] = small_ref[...].astype(BF)
     gf_ref[...] = grad_first
     attended_back = grad_first.astype(BF)
     ab_ref[...] = attended_back
@@ -454,24 +493,24 @@
 
 def wg_body(sc, *refs):
     nl, fb, ab, act, ib, mix = [(refs[i], refs[6 + i]) for i in range(6)]
-    outs = refs[12:14]
+    g_ref = refs[12]
     half = nl[0].shape[1] // 2
     hb = act[0].shape[1] // 4
     hw = mix[0].shape[0] // 4
-    for j in range(2):
-        xc = pl.ds(mult(sc[X] ^ j, half), half)
-        for k in range(4):
-            z = sc[Z] ^ k
-            zc = pl.ds(mult(z, hb), hb)
+    for x in range(2):
+        xc = slice(x * half, (x + 1) * half)
+        for z in range(4):
+            zc = slice(z * hb, (z + 1) * hb)
             e = sum(tdot(nl[i][:, xc], ib[i][:, zc]) for i in range(2)).astype(BF)
             s = sum(tdot(act[i][:, zc], fb[i][:, xc]) for i in range(2)).astype(BF)
-            zr = pl.ds(mult(z, hw), hw)
+            zr = slice(z * hw, (z + 1) * hw)
             m = sum(dot(mix[i][zr, :], ab[i][:, xc]) for i in range(2)).astype(BF)
-            for yh in range(2):
-                out = outs[j].at[sc[Y] ^ yh, k]
-                out[0 : half // 2, :] = e[yh * (half // 2) : (yh + 1) * (half // 2)]
-                out[half // 2 : half // 2 + hb // 2, :] = s[yh * (hb // 2) : (yh + 1) * (hb // 2)]
-                out[half // 2 + hb // 2 :, :] = m[yh * (hw // 2) : (yh + 1) * (hw // 2)]
+            at = 0
+            for v in (e, s, m):
+                n = v.shape[0] // 2
+                for yh in range(2):
+                    g_ref[yh, x, z, at : at + n, :] = v[yh * n : (yh + 1) * n]
+                at += n
 
 
 def wfin_body(sc, *refs):
@@ -482,28 +521,43 @@
     hs = hb // 2
     hm = m_ref.shape[0] // 4
     for i in range(2):
+        c = sc[C] ^ i
         for j in range(2):
             part = quarters[2 * i + j]
-            c = sc[C] ^ i
             y = sc[Y] ^ j
-            e_ref[pl.ds(mult(y, he), he), pl.ds(mult(c, hb), hb)] = part[0:he, :].astype(F32)
+            rows = pl.ds(mult(y, he), he)
+            e_ref[rows, pl.ds(mult(c, hb), hb)] = part[:he, :].astype(F32)
             at = pl.multiple_of(c * hb + y * hs, hs)
             s_ref[pl.ds(at, hs), :] = part[he : he + hs, :].astype(F32)
             at = pl.multiple_of((c * 2 + y) * hm, hm)
             m_ref[pl.ds(at, hm), :] = part[he + hs :, :].astype(F32)
 
 
-def kvfin_body(sc, a_ref, b_ref, c_ref, out_ref):
-    tile = out_ref.shape[2]
-    for k in range(4):
+def ib_body(sc, a_ref, b_ref, c_ref, dq_ref, wt_ref, kv_ref, *outs):
+    wide = dq_ref.shape[1]
+    tile = dq_ref.shape[2]
+    for k in (3, 2, 1, 0):
         cols = pl.ds(mult(sc[Z] ^ k, tile), tile)
         total = a_ref[:, cols].astype(F32) + b_ref[:, cols].astype(F32)
-        out_ref[k] = (total + c_ref[:, cols].astype(F32)).astype(BF)
-
-
-def gp_body(sc, dq_ref, kv_ref, x_ref, out_ref, sum_ref, acc):
+        kv = (total + c_ref[:, cols].astype(F32)).astype(BF)
+        kv_ref[k] = kv
+        part = tdot(dq_ref[k], wt_ref[:wide, :]) + tdot(kv, wt_ref[wide:, :])
+        outs[k][...] = part.astype(BF)
+
+
+def pair_body(a_ref, b_ref, out_ref):
+    out_ref[...] = (a_ref[...].astype(F32) + b_ref[...].astype(F32)).astype(BF)
+
+
+def fin_body(a_ref, b_ref, c_ref, gf_ref, out_ref):
+    total = a_ref[...].astype(F32) + b_ref[...].astype(F32)
+    out_ref[...] = (total + c_ref[...].astype(F32) + gf_ref[...]).astype(BF)
+
+
+def gp_body(sc, dq_ref, kv_ref, x_ref, small_ref, out_ref, acc, line, parts):
     wide = dq_ref.shape[1]
     tile = dq_ref.shape[2]
+    half = out_ref.shape[3]
     ones = jnp.ones((8, tile), BF)
     top = bot = s_top = s_bot = 0.0
     for k in range(4):
@@ -512,80 +566,52 @@
         bot = bot + dot(kv_ref[k], rows)
         s_top = s_top + dot_t(ones, dq_ref[k])
         s_bot = s_bot + dot_t(ones, kv_ref[k, wide:, :])
+        parts[k] = small_ref[k].astype(F32)
     acc[:wide, :] = top
     acc[wide:, :] = bot
-    sum_ref[...] = jnp.zeros_like(sum_ref)
-    sum_ref[:, 0:wide] = s_top
-    sum_ref[:, wide : 2 * wide] = s_bot
-    n_rows = out_ref.shape[3]
-    n_cols = out_ref.shape[4]
+    parts[0] = ((parts[0] + parts[1]) + parts[2]) + parts[3]
+    line[...] = jnp.zeros_like(line)
+    line[0, 0:1, :wide] = s_top[0:1]
+    line[0, 0:1, wide:] = s_bot[0:1]
+    line[1, 0:1, :wide] = s_top[0:1]
+    line[1, 0:1, wide:] = s_bot[0:1]
+    for h in range(2):
+        hc = slice(h * half, (h + 1) * half)
+        line[h, 1:7, :] = parts[0, 0:6, hc]
+        line[h, 7:8, :] = parts[0, pl.ds(8 + sc[Z], 1), hc]
+    n_rows = out_ref.shape[2] - 16
     for i in range(2):
-        for j in range(2):
-            at = pl.multiple_of(((sc[C] ^ i) * 2 + (sc[Y] ^ j)) * n_rows, n_rows)
-            for m in range(2):
-                cols = pl.ds(mult(sc[X] ^ m, n_cols), n_cols)
-                out_ref[i, j, m] = acc[pl.ds(at, n_rows), cols].astype(BF)
-
-
-def ib_body(sc, *refs):
-    dq = refs[0:4]
-    kv = refs[4:8]
-    gf_ref = refs[8]
-    pieces = refs[9:25]
-    out_ref, wp, jb, sems = refs[25:]
-    wide = dq[0].shape[0]
-    half = wp.shape[2] // 2
-    hr = wp.shape[1] // 2
-    copies = []
-    for k in range(4):
-        for j in range(2):
-            for i in range(2):
-                copies.append(
-                    pltpu.make_async_copy(
-                        pieces[k * 4 + j * 2 + i],
-                        wp.at[
-                            k,
-                            pl.ds(mult(sc[C] ^ i, hr), hr),
-                            pl.ds(mult(sc[X] ^ j, half), half),
-                        ],
-                        sems.at[len(copies)],
-                    )
-                )
-    for copy in copies:
-        copy.start()
-    for k in range(4):
-        jb[k, :wide, :] = dq[k][...]
-        jb[k, wide:, :] = kv[k][...]
-    for copy in copies:
-        copy.wait()
-    total = gf_ref[...]
-    for k in range(4):
-        total = total + tdot(jb[k], wp[k])
-    out_ref[...] = total.astype(BF)
+        at = pl.multiple_of((sc[C] ^ i) * n_rows, n_rows)
+        for m in range(2):
+            cols = pl.ds(mult(sc[X] ^ m, half), half)
+            out_ref[i, m, :n_rows, :] = acc[pl.ds(at, n_rows), cols].astype(BF)
+            out_ref[i, m, n_rows:, :] = line[sc[X] ^ m].astype(BF)
 
 
 def join_body(dtype, sc, *refs):
     out = refs[4]
-    tile = refs[0].shape[0]
+    tile = out.shape[0] // 4
     for k in range(4):
-        out[pl.ds(mult(sc[Z] ^ k, tile), tile), :] = refs[k][...].astype(dtype)
-
-
-def gpfin_body(sc, *refs):
-    out = refs[4]
-    n_rows = refs[0].shape[0]
-    for i in range(2):
-        for j in range(2):
-            at = pl.multiple_of(((sc[C] ^ i) * 2 + (sc[Y] ^ j)) * n_rows, n_rows)
-            out[pl.ds(at, n_rows), :] = refs[2 * i + j][...].astype(F32)
+        out[pl.ds(mult(sc[Z] ^ k, tile), tile), :] = refs[k][:tile, :].astype(dtype)
+
+
+def gpfin_body(sc, a_ref, b_ref, out, line, *vecs):
+    n_rows = a_ref.shape[0] - 16
+    rows = a_ref[n_rows : n_rows + 8, :].astype(F32)
+    line[...] = rows
+    for i, vec in enumerate(vecs):
+        vec[...] = rows[1 + i]
+    for i, ref in enumerate((a_ref, b_ref)):
+        at = pl.multiple_of((sc[C] ^ i) * n_rows, n_rows)
+        out[pl.ds(at, n_rows), :] = ref[:n_rows, :].astype(F32)
 
 
 def make_device(n_dp, n_ctx, n_t, generic):
     def swap(axis, size, k):
         return lambda v: lax.ppermute(v, axis, [(i, i ^ k) for i in range(size)])
 
-    pc = swap("ctx", n_ctx, 1)
-    py = swap("ctx", n_ctx, 2)
+    pc = swap("core", 2, 1)
+    py = swap("cy", n_ctx // 2, 1)
     px = swap("dp", n_dp, 1)
     pz = [lambda v: v] + [swap("tensor", n_t, k) for k in range(1, n_t)]
 
@@ -618,12 +644,12 @@
         hw = wide // 2
         x = tokens[0]
         cot = cotangent[0]
-        ctx = lax.axis_index("ctx")
+        c = lax.axis_index("core")
+        y = lax.axis_index("cy")
+        ctx = 2 * y + c
         z = lax.axis_index("tensor")
         dp = lax.axis_index("dp")
         xi = jnp.zeros_like(dp) if generic else dp
-        c = ctx & 1
-        y = ctx >> 1
         pairs = lax.dynamic_slice_in_dim(pairing, z * heads, heads, 0).reshape(-1)
         sc = jnp.concatenate(
             [jnp.stack([ctx, z, xi, c, y, c, c, c]).astype(jnp.int32), pairs.astype(jnp.int32)]
@@ -636,65 +662,58 @@
         wt = jnp.transpose(project, (1, 2, 0)).reshape(3 * wide, -1)
         vectors = [baseline, scaling, shifting, settling, rescaling, reshifting]
 
-        def pack_small(vecs, thr, off):
-            line = jnp.concatenate([off[0], off[1], jnp.zeros((half - wide,), BF)])
-            return jnp.stack(vecs + [thr, line])
-
-        def pack_weights(e, s, m):
-            return jnp.concatenate(
-                [
-                    lax.dynamic_slice_in_dim(e, c * hb, hb, 1),
-                    lax.dynamic_slice_in_dim(s, c * hb, hb, 0),
-                    lax.dynamic_slice_in_dim(m, c * hw, hw, 0),
-                ]
-            )
-
-        def half_project(w):
-            return lax.dynamic_slice_in_dim(w, c * (3 * hw), 3 * hw, 0)
-
+        hq = wide // 2
+        part = 3 * wide // 2
+        def pack(wt_h, e_h, s_h, m_h, off_h, vecs_h):
+            return call(
+                pack_body,
+                (
+                    sds((16, half), F32),
+                    sds((part + 16, half), BF),
+                    sds((half + hb + hw + 16, half), BF),
+                ),
+                ins=[SM] + [VM] * 12,
+                cost=cost(0, 8 * half * width),
+            )(sc, wt_h, e_h, s_h, m_h, off_h, *vecs_h)
+
+        vectors = vectors + [thresholds]
         if generic:
-            wts = both_halves(wt, 1)
-            vec_h = [both_halves(v, 0) for v in vectors]
-            thr_h = both_halves(thresholds, 0)
-            off_h = both_halves(offsets, 1)
-            smalls = [
-                pack_small([v[j] for v in vec_h], thr_h[j], off_h[j]) for j in range(2)
+            own_wt, other_wt = both_halves(wt, 1)
+            parts = [both_halves(v, 0) for v in [expand] + vectors]
+            cols = [both_halves(v, 1) for v in (shrink, combine, offsets)]
+            packed = [
+                pack(
+                    w, parts[0][j], cols[0][j], cols[1][j], cols[2][j], [p[j] for p in parts[1:]]
+                )
+                for j, w in enumerate((own_wt, other_wt))
             ]
-            es, ss, ms = both_halves(expand, 0), both_halves(shrink, 1), both_halves(combine, 1)
-            wpacks = [pack_weights(es[j], ss[j], ms[j]) for j in range(2)]
-            small_pieces = [[p(s) for s in smalls] for p in pz]
-            weight_halves = [[p(w) for w in wpacks] for p in pz]
-            proj_halves = [[p(half_project(w)) for w in wts] for p in pz]
+            small, wtc = packed[0][0], packed[0][1]
+            got_wt = packed[1][1]
+            weights = jnp.stack(
+                [lax.all_gather(p[2], "tensor", axis=0) for p in packed]
+            ).reshape(-1, half)
         else:
-            wts = [wt, px(wt)]
-            small = pack_small(vectors, thresholds, offsets)
-            small_z = [p(small) for p in pz]
-            small_pieces = [[s, px(s)] for s in small_z]
-            wpack = pack_weights(expand, shrink, combine)
-            weight_halves = [[w, px(w)] for w in [p(wpack) for p in pz]]
-            proj_halves = [[w, px(w)] for w in [p(half_project(wt)) for p in pz]]
-        weight_pieces = [w for k in range(4) for j in range(2) for w in (weight_halves[k][j], pc(weight_halves[k][j]))]
-        proj_pieces = [w for k in range(4) for j in range(2) for w in (proj_halves[k][j], pc(proj_halves[k][j]))]
-        packs = [small_pieces[k][j] for k in range(4) for j in range(2)]
-
-        hq = wide // 2
-        lines = [small_pieces[0][j][7] for j in range(2)]
-        lines = [jnp.where(xi == 0, lines[j], lines[1 - j]) for j in range(2)]
-        bias = jnp.concatenate(
-            [
-                lines[0][:hq],
-                lines[1][:hq],
-                jnp.zeros((wide,), BF),
-                lines[0][hq : 2 * hq],
-                lines[1][hq : 2 * hq],
-            ]
-        ).astype(F32)[:, None]
-        qT, kvT = call(
+            own_wt = wt
+            small, wtc, wpack = pack(wt, expand, shrink, combine, offsets, vectors)
+            got_wt = px(wtc)
+            weights = lax.all_gather(wpack, ("dp", "tensor"), axis=0, tiled=True)
+
+        def after(v, *deps):
+            return lax.optimization_barrier((v, *deps))[0]
+
+        got_wt2 = pc(got_wt)
+
+        qT, kvT, wt_full = call(
             qkv_body,
-            (sds((wide, rows), BF), sds((2 * wide, rows), BF)),
-            ins=[SM] + [VM] * 4,
+            (
+                sds((wide, rows), BF),
+                sds((2 * wide, rows), BF),
+                sds((3 * wide, width), BF),
+            ),
+            ins=[SM] + [VM] * 5,
+            scratch=[pltpu.VMEM((3 * wide, half), BF), pltpu.VMEM((16, 3 * wide), BF)],
             cost=cost(2 * rows * width * 3 * wide, 4 * rows * width),
-        )(sc, x, wts[0], wts[1], bias)
+        )(sc, x, own_wt, small, got_wt, got_wt2)
 
         seg = segments[0]
         mine = lax.dynamic_slice_in_dim(seg, c * rows, rows, 0)
@@ -705,13 +724,16 @@
         )
 
         par = pc(kvT)
-        ra = lax.ppermute(kvT, "ctx", [(0, 2), (1, 3)])
+        ra = lax.ppermute(kvT, "cy", [(0, 1)])
         rb = pc(ra)
 
         kv_scratch = [pltpu.VMEM((2 * wide, 2 * rows), BF), pltpu.VMEM((2 * wide, 2 * rows), BF)]
         o_tiles = [None] * 4
         lses = [None] * 4
+        mixed = [None] * 4
+        last = qT
         for k in (1, 2, 3, 0):
+            last = after(qT, last) if k else after(qT, last, mixed[1])
             o_tiles[k], lses[k] = call(
                 functools.partial(fwd_body, k),
                 (sds((wide, tile), BF), sds((8 * heads, tile), F32)),
@@ -719,23 +741,22 @@
                 scratch=kv_scratch
                 + [pltpu.VMEM((B, tile), F32), pltpu.SemaphoreType.DMA((4,))],
                 cost=cost(4 * B * tile * wide, 4 * 2 * wide * rows, B * tile * heads),
-            )(sc, qT, span, kvT, par, ra, rb)
-        mixed = [pz[k](o_tiles[k]) for k in range(4)]
-
-        x_mine = lax.dynamic_slice_in_dim(x, z * tile, tile, 0)
-        cot_mine = lax.dynamic_slice_in_dim(cot, z * tile, tile, 0)
+            )(sc, last, span, kvT, par, ra, rb)
+            last = o_tiles[k]
+            mixed[k] = pz[k](o_tiles[k])
+        weights2 = pc(after(weights, *mixed))
+
         outs = call(
             mid_body,
             (
-                sds((tile, width), BF),
+                sds((tile + 16, width), BF),
                 *[sds((wide, tile), BF)] * 4,
                 *[sds((tile, width), BF)] * 3,
                 *[sds((tile, hidden // 2), BF)] * 4,
                 *[sds((width // 2, tile), BF)] * 2,
                 sds((tile, width), F32),
-                sds((16, width), F32),
             ),
-            ins=[SM] + [VM] * 14 + [ANY] * 16,
+            ins=[SM] + [VM] * 4 + [ANY] * 4,
             scratch=[
                 pltpu.VMEM((width, hidden), BF),
                 pltpu.VMEM((hidden, width), BF),
@@ -747,24 +768,23 @@
                 pltpu.VMEM((8, width), F32),
                 pltpu.VMEM((8, hidden), F32),
                 pltpu.VMEM((width, tile), BF),
+                pltpu.VMEM((8, 16, half), BF),
+                pltpu.VMEM((tile, width), BF),
+                pltpu.VMEM((tile, width), BF),
+                pltpu.VMEM((16, width), F32),
                 pltpu.SemaphoreType.DMA((3, 16)),
-                pltpu.SemaphoreType.DMA((1,)),
+                pltpu.SemaphoreType.DMA((10,)),
             ],
             cost=cost(8 * tile * width * hidden + 4 * tile * width * width, 4 * width * hidden),
-        )(sc, *mixed, x_mine, cot_mine, *packs, *weight_pieces)
+        )(sc, *mixed, x, cot, weights, weights2)
         out_low = outs[0]
         mb = outs[1:5]
-        nl, fb, ab, act_own, act_oth, ib_own, ib_oth, mix_own, mix_oth, grad_first, small_sum = outs[5:]
-        grads = [pz[k](mb[k]) for k in range(4)]
+        nl, fb, ab, act_own, act_oth, ib_own, ib_oth, mix_own, mix_oth, grad_first = outs[5:]
+        grads = [mb[0]] + [pz[k](mb[k]) for k in range(1, 4)]
 
         theirs = [pc(v) for v in (nl, fb, ab, act_oth, ib_oth, mix_oth)]
-        n_part = half // 2 + hb // 2 + hw // 2
-        g_own, g_oth = call(
-            wg_body,
-            tuple([sds((2, 4, n_part, half), BF)] * 2),
-            ins=[SM] + [VM] * 12,
-            cost=cost(4 * tile * width * hidden, 4 * width * hidden),
-        )(sc, nl, fb, ab, act_own, ib_own, mix_own, *theirs)
+        gathered = lax.all_gather(out_low, "tensor", axis=0)
+        layer_out = gathered[:, :tile].reshape(rows, width)
 
         outs = call(
             bwd_body,
@@ -785,141 +805,127 @@
         got_par = pc(d_par)
         got_r = pc(d_r1)
         prompt_part = (d_r0.astype(F32) + got_r.astype(F32)).astype(BF)
-        from_y = lax.ppermute(prompt_part, "ctx", [(2, 0), (3, 1)])
-        kv_back = call(
-            kvfin_body,
-            sds((4, 2 * wide, tile), BF),
-            ins=[SM] + [VM] * 3,
-            cost=cost(2 * wide * rows, 8 * wide * rows),
-        )(sc, d_own, got_par, from_y)
-
-        jq = [dq[0]] + [pz[k](dq[k]) for k in range(1, 4)]
-        jkv = [kv_back[0]] + [pz[k](kv_back[k]) for k in range(1, 4)]
-        gp, sums = call(
+        nl = after(nl, prompt_part)
+        n_part = half // 2 + hb // 2 + hw // 2
+        g = call(
+            wg_body,
+            sds((2, 2, 4, n_part, half), BF),
+            ins=[SM] + [VM] * 12,
+            cost=cost(4 * tile * width * hidden, 4 * width * hidden),
+        )(sc, nl, fb, ab, act_own, ib_own, mix_own, *theirs)
+        from_y = lax.ppermute(prompt_part, "cy", [(1, 0)])
+        outs = call(
+            ib_body,
+            (sds((4, 2 * wide, tile), BF), *[sds((tile, width), BF)] * 4),
+            ins=[SM] + [VM] * 5,
+            cost=cost(2 * rows * width * 3 * wide, 8 * rows * width),
+        )(sc, after(d_own, gathered), got_par, from_y, dq, wt_full)
+        kv_back, back = outs[0], outs[1:]
+        relay = call(pair_body, sds((tile, width), BF), ins=[VM] * 2)(back[2], pz[1](back[3]))
+        near = pz[1](back[1])
+        far = pz[2](relay)
+        gp = call(
             gp_body,
-            (sds((2, 2, 2, 3 * wide // 4, half), BF), sds((8, width), F32)),
-            ins=[SM] + [VM] * 3,
-            scratch=[pltpu.VMEM((3 * wide, width), F32)],
+            sds((2, 2, 3 * wide // 2 + 16, half), BF),
+            ins=[SM] + [VM] * 4,
+            scratch=[
+                pltpu.VMEM((3 * wide, width), F32),
+                pltpu.VMEM((2, 16, half), F32),
+                pltpu.VMEM((4, 16, width), F32),
+            ],
             cost=cost(2 * rows * width * 3 * wide, 4 * rows * width),
-        )(sc, dq, kv_back, x)
-
+        )(sc, dq, kv_back, x, after(gathered[:, tile:], layer_out))
+
+        def add(a, b):
+            return (a.astype(F32) + b.astype(F32)).astype(BF)
+
+        gp_c = add(gp[0], pc(gp[1]))
         low_tokens = call(
-            ib_body,
+            fin_body,
             sds((tile, width), BF),
-            ins=[SM] + [VM] * 9 + [ANY] * 16,
-            scratch=[
-                pltpu.VMEM((4, 3 * wide, width), BF),
-                pltpu.VMEM((4, 3 * wide, tile), BF),
-                pltpu.SemaphoreType.DMA((16,)),
-            ],
-            cost=cost(8 * tile * width * 3 * wide, 8 * width * 3 * wide),
-        )(sc, *jq, *jkv, grad_first, *proj_pieces)
-        token_tiles = [low_tokens] + [pz[k](low_tokens) for k in range(1, 4)]
+            ins=[VM] * 4,
+            cost=cost(4 * tile * width, 12 * tile * width),
+        )(back[0], near, far, after(grad_first, gp_c))
+        gp_c = after(gp_c, low_tokens)
+        tiles_near = pz[1](low_tokens)
+        tiles_far = pz[2](low_tokens)
+        token_tiles = [low_tokens, tiles_near, tiles_far, pz[1](tiles_far)]
         grad_tokens = call(
             functools.partial(join_body, F32),
             sds((rows, width), F32),
             ins=[SM] + [VM] * 4,
             cost=cost(rows * width, 6 * rows * width),
         )(sc, *token_tiles)
-        layer_tiles = [out_low] + [pz[k](out_low) for k in range(1, 4)]
-        layer_out = call(
-            functools.partial(join_body, BF),
-            sds((rows, width), BF),
-            ins=[SM] + [VM] * 4,
-            cost=cost(rows * width, 4 * rows * width),
-        )(sc, *layer_tiles)
-
-        def add(a, b):
-            return (a.astype(F32) + b.astype(F32)).astype(BF)
-
-        def reduce_ff(g):
-            s = add(g[0], py(g[1]))
-            got = [pz[k](s[k]) for k in range(1, 4)]
-            mine = s[0].astype(F32) + got[0].astype(F32) + got[1].astype(F32) + got[2].astype(F32)
-            mine = mine.astype(BF)
+        def finish_ff(mine):
             quarters = [mine, py(mine)]
             quarters = quarters + [pc(q) for q in quarters]
             return call(
                 wfin_body,
                 (sds((half, block), F32), sds((block, half), F32), sds((wide, half), F32)),
                 ins=[SM] + [VM] * 4,
-                cost=cost(2 * half * block, 12 * half * block),
             )(sc, *quarters)
 
-        def reduce_gp(g):
-            s = add(g[0], pc(g[1]))
-            mine = add(s[0], py(s[1]))
-            quarters = [mine, py(mine)]
-            return quarters
-
-        def finish_gp(quarters):
-            quarters = quarters + [pc(q) for q in quarters]
+        def finish_gp(mine):
             return call(
                 gpfin_body,
-                sds((3 * wide, half), F32),
-                ins=[SM] + [VM] * 4,
-                cost=cost(3 * wide * half, 6 * 3 * wide * half),
-            )(sc, *quarters)
-
-        def gp_cy(g):
-            s = add(g[0], pc(g[1]))
-            return add(s[0], py(s[1]))
-
+                (
+                    sds((3 * wide, half), F32),
+                    sds((8, half), F32),
+                    *[sds((half,), F32)] * 7,
+                ),
+                ins=[SM] + [VM] * 2,
+            )(sc, mine, pc(mine))
+
+        gp = add(gp_c, py(gp_c))
         if generic:
-            parts = [reduce_ff(g) for g in (g_own, g_oth)]
-
-            def scatter(v, axis):
+            g = lax.psum_scatter(g, "cy", scatter_dimension=0, tiled=False)
+            parts = [
+                finish_ff(lax.psum_scatter(v, "tensor", scatter_dimension=0, tiled=False))
+                for v in (g[0], g[1])
+            ]
+
+            def scatter(two, axis):
+                full = jnp.concatenate(two, axis=axis).astype(BF)
                 return lax.psum_scatter(
-                    v.astype(BF), "dp", scatter_dimension=axis, tiled=True
+                    full, "dp", scatter_dimension=axis, tiled=True
                 ).astype(F32)
 
-            grad_expand = scatter(jnp.concatenate([p[0] for p in parts], axis=0), 0)
-            grad_shrink = scatter(jnp.concatenate([p[1] for p in parts], axis=1), 1)
-            grad_combine = scatter(jnp.concatenate([p[2] for p in parts], axis=1), 1)
-            summed = gp_cy(gp)
-            both = []
-            for j in range(2):
-                both.append(finish_gp([summed[j], py(summed[j])]))
-            grad_project = scatter(jnp.concatenate(both, axis=1), 1)
+            summed = [scatter([p[i] for p in parts], i and 1) for i in range(3)]
+            both = [finish_gp(gp[j]) for j in range(2)]
+            grad_project = scatter([b[0] for b in both], 1)
+            grad_offsets = scatter([both[0][1][0].reshape(2, wide)], 1)
+            vecs = [scatter([b[2 + i] for b in both], 0) for i in range(7)]
         else:
-            g = add(g_own, px(g_oth))
-            grad_expand, grad_shrink, grad_combine = reduce_ff(g)
-            summed = gp_cy(gp)
-            mine = add(summed[0], px(summed[1]))
-            grad_project = finish_gp([mine, py(mine)])
+            g = after(g, from_y)
+            g = lax.psum_scatter(
+                g.reshape(-1, half), ("cy", "dp"), scatter_dimension=0, tiled=True
+            )
+            g = after(g, tiles_near)
+            g = lax.psum_scatter(g, "tensor", scatter_dimension=0, tiled=True)
+            summed = finish_ff(g)
+            grad_project, lines, *vecs = finish_gp(add(gp[0], px(gp[1])))
+            n_off = offsets.shape[1]
+            grad_offsets = lax.dynamic_slice_in_dim(
+                lines[0].reshape(2, wide), dp * n_off, n_off, 1
+            )
+        grad_expand, grad_shrink, grad_combine = summed
         grad_project = jnp.transpose(grad_project.reshape(3, wide, -1), (2, 0, 1))
 
-        slot = lax.broadcasted_iota(jnp.int32, (16, 1), 0) == 12 + z
-        total = small_sum + jnp.where(slot, sums[0:1], 0.0)
-        total = total + pc(total)
-        total = total + py(total)
-        total = lax.psum(total, "dp") if generic else total + px(total)
-        total = total + pz[1](total)
-        total = total + pz[2](total)
-        n_vec = baseline.shape[0]
-
-        def row(r):
-            return lax.dynamic_slice(total, (r, dp * n_vec), (1, n_vec))[0]
-
-        n_off = offsets.shape[1]
-        grad_offsets = jnp.concatenate(
-            [lax.dynamic_slice(total, (12 + z, dp * n_off + i * wide), (1, n_off)) for i in range(2)]
-        )
         return (
             layer_out[None],
             grad_tokens[None],
             grad_project,
             grad_offsets,
             grad_combine,
-            row(0),
-            row(1),
-            row(2),
+            vecs[0],
+            vecs[1],
+            vecs[2],
             grad_expand,
-            row(8 + z),
+            vecs[6],
             grad_shrink,
-            row(3),
-            row(4),
-            row(5),
+            vecs[3],
+            vecs[4],
+            vecs[5],
         )
 
     return on_device
@@ -927,8 +933,8 @@
 
 def solution(mesh):
     in_specs = (
-        P("dp", "ctx", None),
-        P("dp", "ctx", None),
+        P("dp", ("cy", "core"), None),
+        P("dp", ("cy", "core"), None),
         P("dp", None),
         P(),
         P("dp", None, "tensor"),
@@ -945,8 +951,8 @@
         P("dp"),
     )
     out_specs = (
-        P("dp", "ctx", None),
-        P("dp", "ctx", None),
+        P("dp", ("cy", "core"), None),
+        P("dp", ("cy", "core"), None),
         P("dp", None, "tensor"),
         P(None, ("tensor", "dp")),
         P("tensor", "dp"),
@@ -960,8 +966,9 @@
         P("dp"),
         P("dp"),
     )
-    n_dp = mesh.shape["dp"]
-    on_device = make_device(n_dp, mesh.shape["ctx"], mesh.shape["tensor"], n_dp != 2)
+    n_dp, n_ctx, n_t = mesh.shape["dp"], mesh.shape["ctx"], mesh.shape["tensor"]
+    split = Mesh(mesh.devices.reshape(n_dp, n_ctx // 2, 2, n_t), ("dp", "cy", "core", "tensor"))
+    on_device = make_device(n_dp, n_ctx, n_t, n_dp != 2)
     return jax.shard_map(
-        on_device, mesh=mesh, in_specs=in_specs, out_specs=out_specs, check_vma=False
+        on_device, mesh=split, in_specs=in_specs, out_specs=out_specs, check_vma=False
     )

time: 490 us -> 343 us (0.70)
  starting transfers between devices: 136 us -> 39.1 us
  waiting for transfers between devices: 221 us -> 168 us
  between operations: 1.81 us -> 14.1 us
  other arithmetic: 10.1 us -> 4.21 us
    ppermute x85 -> x32, starting transfers between devices: 131 us -> 33.7 us  [swap(): return lambda v: lax.ppermute(v, axis, [(i, i ^ k) for i in range(size)])]
    ppermute x85 -> x32, waiting for transfers between devices: 191 us -> 111 us  [swap(): return lambda v: lax.ppermute(v, axis, [(i, i ^ k) for i in range(size)])]
    all_gather x0 -> x2, waiting for transfers between devices: none -> 24.8 us  [the longest x1 24.8 us: on_device(): weights = lax.all_gather(wpack, ('dp', 'tensor'), axis=0, tiled=True)]
    pallas_call x9 -> x10, Pallas kernels: 49.1 us -> 50.6 us  [the longest x1 16 us: on_device(): call(mid_body, (sds((tile + 16, width), BF), *[sds((wide, tile), BF)] * 4...]
    unnamed x182 -> x74, local copies, waits for them, and re-layouts: 11.3 us -> 10.2 us
  transfers between devices with their start and end apart: 87 -> 38, of which waited for: 28 -> 22; matrix products, arithmetic and copies ran while one was open for 4% -> 3% of each run, Pallas kernels for 14% -> 23%
where the time goes in v2:
time: 343 us; the launch traced here: 340 us
  waiting for transfers between devices  168 us (49%)
  Pallas kernels  98 us (29%)
  starting transfers between devices  39.1 us (11%)
  local copies, waits for them, and re-layouts  16.7 us (5%)
  between operations  14.1 us (4%)
  other arithmetic  4.21 us (1%)
    ppermute x32, waiting for transfers between devices, swap(): return lambda v: lax.ppermute(v, axis, [(i, i ^ k) for i in range(size)])  111 us
    ppermute x32, starting transfers between devices, swap(): return lambda v: lax.ppermute(v, axis, [(i, i ^ k) for i in range(size)])  33.7 us
    all_gather x1, waiting for transfers between devices, on_device(): weights = lax.all_gather(wpack, ('dp', 'tensor'), axis=0, tiled=True)  24.8 us
    pallas_call x4, Pallas kernels, on_device(): call(functools.partial(fwd_body, k), (sds((wide, tile), BF), sds((8 * hea...  22.2 us
    pallas_call x1, Pallas kernels, on_device(): call(bwd_body, (sds((4, wide, tile), BF), *[sds((2 * wide, rows), BF)] *...  22 us
    ppermute x1, waiting for transfers between devices, on_device(): ra = lax.ppermute(kvT, 'cy', [(0, 1)])  17.3 us
    pallas_call x1, Pallas kernels, on_device(): call(mid_body, (sds((tile + 16, width), BF), *[sds((wide, tile), BF)] * 4...  16 us
    ppermute x1, waiting for transfers between devices, on_device(): from_y = lax.ppermute(prompt_part, 'cy', [(1, 0)])  10.8 us
  transfers between devices with their start and end apart: 38, of which 22 were waited for; matrix products, arithmetic and copies ran while one was open for 3% of the time, Pallas kernels for 23%

profile of v2, /device:TPU:0, one launch (start us, length us, event | category | flops | bytes accessed | tf_op | source)
XLA Modules:
  0.0 339.8 jit_solution(8700388165087738190)
XLA Ops:
  14.3 5.9 %collective-permute-done.w0_ref = bf16[304,384]{1,0:T(8,128)(2,1)S(1)} collective-permute-done((bf16[304,384]{1,0:T(8,128)(2,1)}, bf16[304,384]{1,0:T(8,128)(2,1)S(1)}, u32[]{:S(2)}, u32[]{:S(2)}) %collective-permute-start) | collective-permute-done | bytes 233504 | tf_op jit(solution)/shard_map/ppermute | solution.py:611
  22.4 4.7 %shard_map.264 = (bf16[192,1024]{1,0:T(8,128)(2,1)}, bf16[384,1024]{1,0:T(8,128)(2,1)}, bf16[576,768]{1,0:T(8,128)(2,1)}) custom-call(s32[14]{0:T(128)} %concatenate.6.sc, bf16[1024,768]{1,0:T(8,128)(2,1)} %bitcast.40, bf16[576,384]{1,0:T(8,128)(2,1)} %bitcast.44, f32[16,384]{1,0:T(8,128)} %get-tuple-element.76.small_ref, bf16[304,384]{1,0:T(8,128)(2,1)} %copy-done.28, ...), custom_call_target="tpu_custom_call" | custom-call | flops 905969664 | bytes 3145728 | tf_op jit(solution)/shard_map/pallas_call | solution.py:706
  30.9 17.3 %collective-permute-done.3.ra = bf16[384,1024]{1,0:T(8,128)(2,1)S(1)} collective-permute-done((bf16[384,1024]{1,0:T(8,128)(2,1)}, bf16[384,1024]{1,0:T(8,128)(2,1)S(1)}, u32[]{:S(2)}, u32[]{:S(2)}) %collective-permute-start.3) | collective-permute-done | bytes 786464 | tf_op jit(solution)/shard_map/ppermute | solution.py:727
  52.5 5.6 %shard_map.265 = (bf16[192,256]{1,0:T(8,128)(2,1)}, f32[24,256]{1,0:T(8,128)}) custom-call(s32[14]{0:T(128)} %concatenate.6.sc, bf16[192,1024]{1,0:T(8,128)(2,1)} %get-tuple-element.86.q_ref, s32[8,1024]{1,0:T(8,128)} %add_add_fusion.span_ref, bf16[384,1024]{1,0:T(8,128)(2,1)} %get-tuple-element.80.own, bf16[384,1024]{1,0:T(8,128)(2,1)} %copy-done.2, ...), custom_call_target="tpu_custom_call" | custom-call | flops 226492416 | bytes 1572864 | tf_op jit(solution)/shard_map/pallas_call | solution.py:737
  59.9 5.5 %shard_map.266 = (bf16[192,256]{1,0:T(8,128)(2,1)}, f32[24,256]{1,0:T(8,128)}) custom-call(s32[14]{0:T(128)} %concatenate.6.sc, bf16[192,1024]{1,0:T(8,128)(2,1)} %get-tuple-element.86.q_ref, s32[8,1024]{1,0:T(8,128)} %add_add_fusion.span_ref, bf16[384,1024]{1,0:T(8,128)(2,1)} %get-tuple-element.80.own, bf16[384,1024]{1,0:T(8,128)(2,1)} %copy-done.2, ...), custom_call_target="tpu_custom_call" | custom-call | flops 226492416 | bytes 1572864 | tf_op jit(solution)/shard_map/pallas_call | solution.py:737
  67.9 5.4 %shard_map.267 = (bf16[192,256]{1,0:T(8,128)(2,1)}, f32[24,256]{1,0:T(8,128)}) custom-call(s32[14]{0:T(128)} %concatenate.6.sc, bf16[192,1024]{1,0:T(8,128)(2,1)} %get-tuple-element.86.q_ref, s32[8,1024]{1,0:T(8,128)} %add_add_fusion.span_ref, bf16[384,1024]{1,0:T(8,128)(2,1)} %get-tuple-element.80.own, bf16[384,1024]{1,0:T(8,128)(2,1)} %copy-done.2, ...), custom_call_target="tpu_custom_call" | custom-call | flops 226492416 | bytes 1572864 | tf_op jit(solution)/shard_map/pallas_call | solution.py:737
  73.7 5.7 %shard_map.268 = (bf16[192,256]{1,0:T(8,128)(2,1)}, f32[24,256]{1,0:T(8,128)}) custom-call(s32[14]{0:T(128)} %concatenate.6.sc, bf16[192,1024]{1,0:T(8,128)(2,1)} %get-tuple-element.86.q_ref, s32[8,1024]{1,0:T(8,128)} %add_add_fusion.span_ref, bf16[384,1024]{1,0:T(8,128)(2,1)} %get-tuple-element.80.own, bf16[384,1024]{1,0:T(8,128)(2,1)} %copy-done.2, ...), custom_call_target="tpu_custom_call" | custom-call | flops 226492416 | bytes 1572864 | tf_op jit(solution)/shard_map/pallas_call | solution.py:737
  79.3 4.3 %collective-permute-done.6.refs_2_ = bf16[192,256]{1,0:T(8,128)(2,1)S(1)} collective-permute-done((bf16[192,256]{1,0:T(8,128)(2,1)}, bf16[192,256]{1,0:T(8,128)(2,1)S(1)}, u32[]{:S(2)}, u32[]{:S(2)}) %collective-permute-start.6) | collective-permute-done | bytes 98336 | tf_op jit(solution)/shard_map/ppermute | solution.py:611
  83.6 24.8 %all-gather.4.cloned.1.call-done.refs_6_ = bf16[7040,384]{1,0:T(8,128)(2,1)} async-done(((bf16[880,384]{1,0:T(8,128)(2,1)}), bf16[7040,384]{1,0:T(8,128)(2,1)}) %all-gather.4.cloned.1.call-update) | async-done | bytes 5406736 | tf_op jit(solution)/shard_map/all_gather | solution.py:699
  108.4 9.2 %collective-permute-done.8.refs_7_ = bf16[7040,384]{1,0:T(8,128)(2,1)} collective-permute-done((bf16[7040,384]{1,0:T(8,128)(2,1)}, bf16[7040,384]{1,0:T(8,128)(2,1)}, u32[]{:S(2)}, u32[]{:S(2)}) %collective-permute-start.8) | collective-permute-done | bytes 5406752 | tf_op jit(solution)/shard_map/ppermute | solution.py:611
  117.6 16.0 %shard_map.269 = (bf16[272,768]{1,0:T(8,128)(2,1)}, bf16[192,256]{1,0:T(8,128)(2,1)}, bf16[192,256]{1,0:T(8,128)(2,1)}, bf16[192,256]{1,0:T(8,128)(2,1)}, bf16[1...) custom-call(s32[14]{0:T(128)} %concatenate.6.sc, ...), custom_call_target="tpu_custom_call" | custom-call | flops 5435817984 | bytes 9437184 | tf_op jit(solution)/shard_map/pallas_call | solution.py:749
  140.0 6.5 %collective-permute-done.10.refs_10_ = bf16[192,256]{1,0:T(8,128)(2,1)S(1)} collective-permute-done((bf16[192,256]{1,0:T(8,128)(2,1)}, bf16[192,256]{1,0:T(8,128)(2,1)S(1)}, u32[]{:S(2)}, u32[]{:S(2)}) %collective-permute-start.10) | collective-permute-done | bytes 98336 | tf_op jit(solution)/shard_map/ppermute | solution.py:611
  147.2 22.0 %shard_map.270 = (bf16[4,192,256]{2,1,0:T(8,128)(2,1)}, bf16[384,1024]{1,0:T(8,128)(2,1)}, bf16[384,1024]{1,0:T(8,128)(2,1)}, bf16[384,1024]{1,0:T(8,128)(2,1)}, bf16[384,1024]{1,0:T(8,128)(2,1)}) custom-call(s32[14]{0:T(128)} %concatenate.6.sc, bf16[192,1024]{1,0:T(8,128)(2,1)} %get-tuple-element.86.q_ref, s32[8,1024]{1,0:T(8,128)} %add_add_fusion.span_ref, ...), custom_call_target="tpu_custom_call" | custom-call | flops 2264924160 | bytes 3145728 | tf_op jit(solution)/shard_map/pallas_call | solution.py:789
  179.1 9.1 %shard_map.277 = bf16[2,2,4,432,384]{4,3,2,1,0:T(8,128)(2,1)} custom-call(s32[14]{0:T(128)} %concatenate.6.sc, bf16[256,768]{1,0:T(8,128)(2,1)} %get-tuple-element.117.refs_0_, bf16[256,768]{1,0:T(8,128)(2,1)} %get-tuple-element.118.refs_1_, bf16[256,768]{1,0:T(8,128)(2,1)} %get-tuple-element.119.refs_2_, bf16[256,1536]{1,0:T(8,128)(2,1)} %get-tuple-element.120.refs_3_, ...), custom_call_target="tpu_custom_call" | custom-call | flops 2415919104 | bytes 9437184 | tf_op jit(solution)/shard_map/pallas_call | solution.py:810
  188.2 10.8 %collective-permute-done.14.c_ref = bf16[384,1024]{1,0:T(8,128)(2,1)S(1)} collective-permute-done((bf16[384,1024]{1,0:T(8,128)(2,1)S(1)}, bf16[384,1024]{1,0:T(8,128)(2,1)S(1)}, u32[]{:S(2)}, u32[]{:S(2)}) %collective-permute-start.14) | collective-permute-done | bytes 786464 | tf_op jit(solution)/shard_map/ppermute | solution.py:816
  203.6 4.5 %shard_map.271 = (bf16[4,384,256]{2,1,0:T(8,128)(2,1)}, bf16[256,768]{1,0:T(8,128)(2,1)}, bf16[256,768]{1,0:T(8,128)(2,1)}, bf16[256,768]{1,0:T(8,128)(2,1)}, bf16[256,768]{1,0:T(8,128)(2,1)}) custom-call(s32[14]{0:T(128)} %concatenate.6.sc, bf16[384,1024]{1,0:T(8,128)(2,1)} %get-tuple-element.100.a_ref, bf16[384,1024]{1,0:T(8,128)(2,1)} %copy-done.10, ...), custom_call_target="tpu_custom_call" | custom-call | flops 905969664 | bytes 6291456 | tf_op jit(solution)/shard_map/pallas_call | solution.py:817
  208.1 11.8 %collective-permute-start.16 = (bf16[256,768]{1,0:T(8,128)(2,1)}, bf16[256,768]{1,0:T(8,128)(2,1)S(1)}, u32[]{:S(2)}, u32[]{:S(2)}) collective-permute-start(bf16[256,768]{1,0:T(8,128)(2,1)} %get-tuple-element.109), channel_id=1, source_target_pairs={{0,1},{1,0},{2,3},{3,2},{4,5},{5,4},{6,7},{7,6},{8,9},{9,8},{10,11... | collective-permute-start | bytes 1179656 | tf_op jit(solution)/shard_map/ppermute | solution.py:611
  219.9 4.5 %shard_map.273 = bf16[2,2,304,384]{3,2,1,0:T(8,128)(2,1)} custom-call(s32[14]{0:T(128)} %concatenate.6.sc, bf16[4,192,256]{2,1,0:T(8,128)(2,1)} %get-tuple-element.104.dq_ref, bf16[4,384,256]{2,1,0:T(8,128)(2,1)} %get-tuple-element.111.kv_ref, bf16[1024,768]{1,0:T(8,128)(2,1)} %bitcast.42, bf16[4,16,768]{2,1,0:T(8,128)(2,1)} %slice.29.small_ref), custom_call_target="tpu_custom_call" | custom-call | flops 905969664 | bytes 3145728 | tf_op jit(solution)/shard_map/pallas_call | solution.py:827
  233.0 6.0 %collective-permute-done.15.b_ref = bf16[256,768]{1,0:T(8,128)(2,1)S(1)} collective-permute-done((bf16[256,768]{1,0:T(8,128)(2,1)S(1)}, bf16[256,768]{1,0:T(8,128)(2,1)S(1)}, u32[]{:S(2)}, u32[]{:S(2)}) %collective-permute-start.15) | collective-permute-done | bytes 393248 | tf_op jit(solution)/shard_map/ppermute | solution.py:611
  239.0 13.6 %collective-permute-done.17.c_ref = bf16[256,768]{1,0:T(8,128)(2,1)S(1)} collective-permute-done((bf16[256,768]{1,0:T(8,128)(2,1)}, bf16[256,768]{1,0:T(8,128)(2,1)S(1)}, u32[]{:S(2)}, u32[]{:S(2)}) %collective-permute-start.17) | collective-permute-done | bytes 393248 | tf_op jit(solution)/shard_map/ppermute | solution.py:611
  255.8 10.3 %collective-permute-done.19.refs_1_ = bf16[256,768]{1,0:T(8,128)(2,1)S(1)} collective-permute-done((bf16[256,768]{1,0:T(8,128)(2,1)}, bf16[256,768]{1,0:T(8,128)(2,1)S(1)}, u32[]{:S(2)}, u32[]{:S(2)}) %collective-permute-start.19) | collective-permute-done | bytes 393248 | tf_op jit(solution)/shard_map/ppermute | solution.py:611
  272.9 8.7 %collective-permute-done.22 = bf16[2,304,384]{2,1,0:T(8,128)(2,1)S(1)} collective-permute-done((bf16[2,304,384]{2,1,0:T(8,128)(2,1)S(1)}, bf16[2,304,384]{2,1,0:T(8,128)(2,1)S(1)}, u32[]{:S(2)}, u32[]{:S(2)}) %collective-permute-start.22) | collective-permute-done | bytes 466976 | tf_op jit(solution)/shard_map/ppermute | solution.py:611
  283.1 26.6 %collective-permute-done.20.refs_2_ = bf16[256,768]{1,0:T(8,128)(2,1)S(1)} collective-permute-done((bf16[256,768]{1,0:T(8,128)(2,1)}, bf16[256,768]{1,0:T(8,128)(2,1)S(1)}, u32[]{:S(2)}, u32[]{:S(2)}) %collective-permute-start.20) | collective-permute-done | bytes 393248 | tf_op jit(solution)/shard_map/ppermute | solution.py:611
  313.0 8.0 %collective-permute-done.31.refs_1_ = bf16[432,384]{1,0:T(8,128)(2,1)} collective-permute-done((bf16[432,384]{1,0:T(8,128)(2,1)}, bf16[432,384]{1,0:T(8,128)(2,1)}, u32[]{:S(2)}, u32[]{:S(2)}) %collective-permute-start.31) | collective-permute-done | bytes 331808 | tf_op jit(solution)/shard_map/ppermute | solution.py:611
  (166 shorter events, 79.0 us)
Async XLA Ops:
  7.2 101.2 %all-gather.4.cloned.1.call-start = ((), (), s32[]{:S(2)}) async-start(), calls=%async_computation.2 | async-start | bytes 6082560 | tf_op jit(solution)/shard_map/all_gather | solution.py:699
  11.3 189.2 %all-gather.6.cloned.1.call-start = ((), (), s32[]{:S(2)}) async-start(), calls=%async_computation.5 | async-start | bytes 2088960 | tf_op jit(solution)/shard_map/all_gather | solution.py:786
  27.1 21.1 %collective-permute-start.3 = (bf16[384,1024]{1,0:T(8,128)(2,1)}, bf16[384,1024]{1,0:T(8,128)(2,1)S(1)}, u32[]{:S(2)}, u32[]{:S(2)}) collective-permute-start(bf16[384,1024]{1,0:T(8,128)(2,1)} %get-tuple-element.80.own), channel_id=1, source_target_pairs={{0,8},{1,9},{2,10},{3,11},{4,12},{5,13},{6,14},{7,15},{16,24},{17,... | collective-permute-start | bytes 2359304 | tf_op jit(solution)/shard_map/ppermute | solution.py:727
  30.8 19.9 %collective-permute-start.2 = (bf16[384,1024]{1,0:T(8,128)(2,1)}, bf16[384,1024]{1,0:T(8,128)(2,1)S(1)}, u32[]{:S(2)}, u32[]{:S(2)}) collective-permute-start(bf16[384,1024]{1,0:T(8,128)(2,1)} %get-tuple-element.80.own), channel_id=1, source_target_pairs={{0,4},{4,0},{1,5},{5,1},{2,6},{6,2},{3,7},{7,3},{8,12},{12,8},{9,1... | collective-permute-start | bytes 2359304 | tf_op jit(solution)/shard_map/ppermute | solution.py:611
  58.2 15.5 %collective-permute-start.5 = (bf16[192,256]{1,0:T(8,128)(2,1)}, bf16[192,256]{1,0:T(8,128)(2,1)S(1)}, u32[]{:S(2)}, u32[]{:S(2)}) collective-permute-start(bf16[192,256]{1,0:T(8,128)(2,1)} %get-tuple-element.81.refs_1_), channel_id=1, source_target_pairs={{0,1},{1,0},{2,3},{3,2},{4,5},{5,4},{6,7},{7,6},{8,9},{9,8},{10,11... | collective-permute-start | bytes 294920 | tf_op jit(solution)/shard_map/ppermute | solution.py:611
  65.3 18.3 %collective-permute-start.6 = (bf16[192,256]{1,0:T(8,128)(2,1)}, bf16[192,256]{1,0:T(8,128)(2,1)S(1)}, u32[]{:S(2)}, u32[]{:S(2)}) collective-permute-start(bf16[192,256]{1,0:T(8,128)(2,1)} %get-tuple-element.83.refs_2_), channel_id=1, source_target_pairs={{0,2},{1,3},{2,0},{3,1},{4,6},{5,7},{6,4},{7,5},{8,10},{9,11},{10,... | collective-permute-start | bytes 294920 | tf_op jit(solution)/shard_map/ppermute | solution.py:611
  73.4 10.2 %collective-permute-start.7 = (bf16[192,256]{1,0:T(8,128)(2,1)}, bf16[192,256]{1,0:T(8,128)(2,1)S(1)}, u32[]{:S(2)}, u32[]{:S(2)}) collective-permute-start(bf16[192,256]{1,0:T(8,128)(2,1)} %get-tuple-element.85.refs_3_), channel_id=1, source_target_pairs={{0,3},{1,2},{2,1},{3,0},{4,7},{5,6},{6,5},{7,4},{8,11},{9,10},{10,... | collective-permute-start | bytes 294920 | tf_op jit(solution)/shard_map/ppermute | solution.py:611
  108.4 9.2 %collective-permute-start.8 = (bf16[7040,384]{1,0:T(8,128)(2,1)}, bf16[7040,384]{1,0:T(8,128)(2,1)}, u32[]{:S(2)}, u32[]{:S(2)}) collective-permute-start(bf16[7040,384]{1,0:T(8,128)(2,1)} %all-gather.4.cloned.1.call-done.refs_6_), channel_id=1, source_target_pairs={{0,4},{4,0},{1,5},{5,1},{2,6},{6,2},{3,7},{7,3},{8,12},{12,8},{9,1... | collective-permute-start | bytes 16220168 | tf_op jit(solution)/shard_map/ppermute | solution.py:611
  133.6 135.4 %reduce-scatter.3.cloned.1.call-start = ((), (), s32[]{:S(2)}) async-start(), calls=%async_computation.3 | async-start | bytes 6635520 | tf_op jit(solution)/shard_map/reduce_scatter | solution.py:900
  133.8 12.7 %collective-permute-start.10 = (bf16[192,256]{1,0:T(8,128)(2,1)}, bf16[192,256]{1,0:T(8,128)(2,1)S(1)}, u32[]{:S(2)}, u32[]{:S(2)}) collective-permute-start(bf16[192,256]{1,0:T(8,128)(2,1)} %get-tuple-element.97), channel_id=1, source_target_pairs={{0,2},{1,3},{2,0},{3,1},{4,6},{5,7},{6,4},{7,5},{8,10},{9,11},{10,... | collective-permute-start | bytes 294920 | tf_op jit(solution)/shard_map/ppermute | solution.py:611
  135.5 11.0 %collective-permute-start.11 = (bf16[192,256]{1,0:T(8,128)(2,1)}, bf16[192,256]{1,0:T(8,128)(2,1)S(1)}, u32[]{:S(2)}, u32[]{:S(2)}) collective-permute-start(bf16[192,256]{1,0:T(8,128)(2,1)} %get-tuple-element.98), channel_id=1, source_target_pairs={{0,3},{1,2},{2,1},{3,0},{4,7},{5,6},{6,5},{7,4},{8,11},{9,10},{10,... | collective-permute-start | bytes 294920 | tf_op jit(solution)/shard_map/ppermute | solution.py:611
  173.9 25.1 %collective-permute-start.14 = (bf16[384,1024]{1,0:T(8,128)(2,1)S(1)}, bf16[384,1024]{1,0:T(8,128)(2,1)S(1)}, u32[]{:S(2)}, u32[]{:S(2)}) collective-permute-start(bf16[384,1024]{1,0:T(8,128)(2,1)S(1)} %add_convert_fusion), channel_id=1, source_target_pairs={{8,0},{9,1},{10,2},{11,3},{12,4},{13,5},{14,6},{15,7},{24,16},{25,... | collective-permute-start | bytes 2359304 | tf_op jit(solution)/shard_map/ppermute | solution.py:816
  199.9 111.7 %reduce-scatter.5.cloned.1.call-start = ((), (), s32[]{:S(2)}) async-start(), calls=%async_computation.4 | async-start | bytes 1658880 | tf_op jit(solution)/shard_map/reduce_scatter | solution.py:904
  208.1 21.9 %collective-permute-start.16 = (bf16[256,768]{1,0:T(8,128)(2,1)}, bf16[256,768]{1,0:T(8,128)(2,1)S(1)}, u32[]{:S(2)}, u32[]{:S(2)}) collective-permute-start(bf16[256,768]{1,0:T(8,128)(2,1)} %get-tuple-element.109), channel_id=1, source_target_pairs={{0,1},{1,0},{2,3},{3,2},{4,5},{5,4},{6,7},{7,6},{8,9},{9,8},{10,11... | collective-permute-start | bytes 1179656 | tf_op jit(solution)/shard_map/ppermute | solution.py:611
  225.7 13.3 %collective-permute-start.15 = (bf16[256,768]{1,0:T(8,128)(2,1)S(1)}, bf16[256,768]{1,0:T(8,128)(2,1)S(1)}, u32[]{:S(2)}, u32[]{:S(2)}) collective-permute-start(bf16[256,768]{1,0:T(8,128)(2,1)S(1)} %copy-done.27), channel_id=1, source_target_pairs={{0,1},{1,0},{2,3},{3,2},{4,5},{5,4},{6,7},{7,6},{8,9},{9,8},{10,11... | collective-permute-start | bytes 1179656 | tf_op jit(solution)/shard_map/ppermute | solution.py:611
  232.8 19.8 %collective-permute-start.17 = (bf16[256,768]{1,0:T(8,128)(2,1)}, bf16[256,768]{1,0:T(8,128)(2,1)S(1)}, u32[]{:S(2)}, u32[]{:S(2)}) collective-permute-start(bf16[256,768]{1,0:T(8,128)(2,1)} %shard_map.272), channel_id=1, source_target_pairs={{0,2},{1,3},{2,0},{3,1},{4,6},{5,7},{6,4},{7,5},{8,10},{9,11},{10,... | collective-permute-start | bytes 1179656 | tf_op jit(solution)/shard_map/ppermute | solution.py:611
  255.8 10.3 %collective-permute-start.19 = (bf16[256,768]{1,0:T(8,128)(2,1)}, bf16[256,768]{1,0:T(8,128)(2,1)S(1)}, u32[]{:S(2)}, u32[]{:S(2)}) collective-permute-start(bf16[256,768]{1,0:T(8,128)(2,1)} %shard_map.274.refs_0_), channel_id=1, source_target_pairs={{0,1},{1,0},{2,3},{3,2},{4,5},{5,4},{6,7},{7,6},{8,9},{9,8},{10,11... | collective-permute-start | bytes 1179656 | tf_op jit(solution)/shard_map/ppermute | solution.py:611
  269.1 12.5 %collective-permute-start.22 = (bf16[2,304,384]{2,1,0:T(8,128)(2,1)S(1)}, bf16[2,304,384]{2,1,0:T(8,128)(2,1)S(1)}, u32[]{:S(2)}, u32[]{:S(2)}) collective-permute-start(bf16[2,304,384]{2,1,0:T(8,128)(2,1)S(1)} %fusion), channel_id=1, source_target_pairs={{0,8},{8,0},{1,9},{9,1},{2,10},{10,2},{3,11},{11,3},{4,12},{12,4},... | collective-permute-start | bytes 1400840 | tf_op jit(solution)/shard_map/ppermute | solution.py:611
  270.5 39.3 %collective-permute-start.20 = (bf16[256,768]{1,0:T(8,128)(2,1)}, bf16[256,768]{1,0:T(8,128)(2,1)S(1)}, u32[]{:S(2)}, u32[]{:S(2)}) collective-permute-start(bf16[256,768]{1,0:T(8,128)(2,1)} %shard_map.274.refs_0_), channel_id=1, source_target_pairs={{0,2},{1,3},{2,0},{3,1},{4,6},{5,7},{6,4},{7,5},{8,10},{9,11},{10,... | collective-permute-start | bytes 1179656 | tf_op jit(solution)/shard_map/ppermute | solution.py:611
  281.7 30.6 %collective-permute-start.23 = (bf16[304,384]{1,0:T(8,128)(2,1)S(1)}, bf16[304,384]{1,0:T(8,128)(2,1)S(1)}, u32[]{:S(2)}, u32[]{:S(2)}) collective-permute-start(bf16[304,384]{1,0:T(8,128)(2,1)S(1)} %slice_bitcast_fusion.2), channel_id=1, source_target_pairs={{0,16},{16,0},{1,17},{17,1},{2,18},{18,2},{3,19},{19,3},{4,20},{20... | collective-permute-start | bytes 700424 | tf_op jit(solution)/shard_map/ppermute | solution.py:611
  309.8 12.4 %collective-permute-start.21 = (bf16[256,768]{1,0:T(8,128)(2,1)S(1)}, bf16[256,768]{1,0:T(8,128)(2,1)}, u32[]{:S(2)}, u32[]{:S(2)}) collective-permute-start(bf16[256,768]{1,0:T(8,128)(2,1)S(1)} %collective-permute-done.20.refs_2_), channel_id=1, source_target_pairs={{0,1},{1,0},{2,3},{3,2},{4,5},{5,4},{6,7},{7,6},{8,9},{9,8},{10,11... | collective-permute-start | bytes 1179656 | tf_op jit(solution)/shard_map/ppermute | solution.py:611
  311.6 9.3 %collective-permute-start.31 = (bf16[432,384]{1,0:T(8,128)(2,1)}, bf16[432,384]{1,0:T(8,128)(2,1)}, u32[]{:S(2)}, u32[]{:S(2)}) collective-permute-start(bf16[432,384]{1,0:T(8,128)(2,1)} %reduce-scatter.5.cloned.1.call-done.refs_0_), channel_id=1, source_target_pairs={{0,8},{8,0},{1,9},{9,1},{2,10},{10,2},{3,11},{11,3},{4,12},{12,4},... | collective-permute-start | bytes 995336 | tf_op jit(solution)/shard_map/ppermute | solution.py:611
  312.4 13.0 %collective-permute-start.24 = (bf16[304,384]{1,0:T(8,128)(2,1)S(1)}, bf16[304,384]{1,0:T(8,128)(2,1)S(1)}, u32[]{:S(2)}, u32[]{:S(2)}) collective-permute-start(bf16[304,384]{1,0:T(8,128)(2,1)S(1)} %fusion.1.a_ref), channel_id=1, source_target_pairs={{0,4},{4,0},{1,5},{5,1},{2,6},{6,2},{3,7},{7,3},{8,12},{12,8},{9,1... | collective-permute-start | bytes 700424 | tf_op jit(solution)/shard_map/ppermute | solution.py:611
  312.5 17.2 %collective-permute-start.32 = (bf16[432,384]{1,0:T(8,128)(2,1)}, bf16[432,384]{1,0:T(8,128)(2,1)S(1)}, u32[]{:S(2)}, u32[]{:S(2)}) collective-permute-start(bf16[432,384]{1,0:T(8,128)(2,1)} %reduce-scatter.5.cloned.1.call-done.refs_0_), channel_id=1, source_target_pairs={{0,4},{4,0},{1,5},{5,1},{2,6},{6,2},{3,7},{7,3},{8,12},{12,8},{9,1... | collective-permute-start | bytes 995336 | tf_op jit(solution)/shard_map/ppermute | solution.py:611
  (51 other events, 481.7 us)
Sparse Core Ops, SparseCore 0:
  11.4 96.9 all-gather.3
  133.8 39.5 all-gather.5
  199.2 69.7 reduce-scatter.2
  271.2 40.3 reduce-scatter.4

commit v3 on v2

--- a/solution.py
+++ b/solution.py
@@ -93,7 +93,7 @@
 def pack_body(sc, *refs):
     wt, e_ref, s_ref, m_ref, off = refs[0:5]
     vecs = refs[5:12]
-    small, wtc, wc = refs[12:15]
+    small, wtc, wc, tq = refs[12:16]
     part = wt.shape[0] // 2
     hb = e_ref.shape[1] // 2
     hw = m_ref.shape[0] // 2
@@ -106,10 +106,18 @@
     low = small[...].astype(BF)
     wtc[:part, :] = wt[pl.ds(mult(c, part), part), :]
     wtc[part:, :] = low
+    hs = hb // 2
+    y = sc[Y]
     wc[:half, :] = e_ref[:, pl.ds(mult(c, hb), hb)]
-    wc[half : half + hb, :] = s_ref[pl.ds(mult(c, hb), hb), :]
-    wc[half + hb : half + hb + hw, :] = m_ref[pl.ds(mult(c, hw), hw), :]
-    wc[half + hb + hw :, :] = low
+    wc[half:, :] = s_ref[pl.ds(mult(c, hb), hs), :]
+    at = 0
+    for ref, start, n in (
+        (m_ref, (c * 2 + y) * (hw // 2), hw // 2),
+        (s_ref, c * hb + hs + y * (hs // 2), hs // 2),
+    ):
+        tq[at : at + n, :] = ref[pl.ds(pl.multiple_of(start, 16), n), :]
+        at += n
+    tq[at:, :] = low
 
 
 def load_pairs(sc, own, par, ra, rb, pbuf, cbuf, sems):
@@ -162,67 +170,127 @@
     return pl.multiple_of(jnp.clip(local - LMAX, 0, 2 * rows - tile - 2 * LMAX), 128)
 
 
-CHUNK = 384
-
-
-def fwd_body(k, sc, q_ref, span_ref, own, par, ra, rb, o_ref, lse_ref, pbuf, cbuf, s_buf, sems):
-    load_pairs(sc, own, par, ra, rb, pbuf, cbuf, sems)
+FAR = 1e30
+
+
+def attend(src, state, q_h, h, at, n, ok, masks, cols):
+    acc, peaks, totals = state
+    wide = acc.shape[0]
+    h_rows = pl.ds(mult(h, HD), HD)
+    v_rows = pl.ds(mult(h, HD) + wide, HD)
+    h8 = pl.ds(mult(h, 8), 8)
+    place = pl.ds(at, n)
+    s = tdot(src[h_rows, place], q_h)
+    if masks is not None:
+        pos = lax.broadcasted_iota(jnp.int32, s.shape, 0) + at
+        s = jnp.where((pos >= masks[0]) & (pos < masks[1]), s, NEG)
+    peak = peaks[h8, cols]
+    new = jnp.maximum(peak, jnp.max(s, axis=0, keepdims=True))
+    cap = new
+    if ok is not None:
+        new = jnp.where(ok, new, peak)
+        cap = jnp.where(ok, new, FAR)
+    e = jnp.exp(s - cap[0:1])
+    alpha = jnp.exp(peak - new)
+    peaks[h8, cols] = new
+    totals[h8, cols] = totals[h8, cols] * alpha + jnp.sum(e, axis=0, keepdims=True)
+    acc[h_rows, cols] = acc[h_rows, cols] * alpha[0:1] + dot(src[v_rows, place], e.astype(BF))
+
+
+def attend_prompt(sc, src, state, q_h, h, blk, ok, cols):
+    paired = sc[PAIR + 2 * h + blk]
+    start = paired * B
+    count = 4 - paired
+
+    def run(i, _):
+        at = pl.multiple_of(start + i * 256, 128)
+        attend(src, state, q_h, h, at, 256, ok, None, cols)
+        return 0
+
+    lax.fori_loop(0, count, run, 0)
+    at = pl.multiple_of(start + count * 256, 128)
+    attend(src, state, q_h, h, at, 128, ok, None, cols)
+
+
+def load_two(sc, first, second, buf, sems):
+    rows = first.shape[1]
+    copies = [
+        pltpu.make_async_copy(first, buf.at[:, pl.ds(mult(sc[C], rows), rows)], sems.at[0]),
+        pltpu.make_async_copy(second, buf.at[:, pl.ds(mult(1 - sc[C], rows), rows)], sems.at[1]),
+    ]
+    for copy in copies:
+        copy.start()
+    for copy in copies:
+        copy.wait()
+
+
+def fwd_near_body(sc, q_ref, span_ref, own, par, acc, peaks, totals, buf, sems):
+    load_two(sc, own, par, buf, sems)
     rows = own.shape[1]
-    wide, tile = o_ref.shape
-    heads = wide // HD
-    t = sc[Z] ^ k
-    start = sc[CTX] * rows + t * tile
-    cols = pl.ds(mult(t, tile), tile)
-
-    def one_pass(src, key_start, size, low, high, q_h, h, carry):
-        peak, total, acc = carry
-        k_rows = pl.ds(mult(h, HD), HD)
-        v_rows = pl.ds(mult(h, HD) + wide, HD)
-        new_peak = peak
-        for j in range(size // CHUNK):
-            keys = src[k_rows, pl.ds(key_start + j * CHUNK, CHUNK)]
-            s = tdot(keys, q_h)
-            pos = lax.broadcasted_iota(jnp.int32, s.shape, 0) + (key_start + j * CHUNK)
-            s = jnp.where((pos >= low) & (pos < high), s, NEG)
-            s_buf[j * CHUNK : (j + 1) * CHUNK, :] = s
-            new_peak = jnp.maximum(new_peak, jnp.max(s, axis=0, keepdims=True))
-        alpha = jnp.exp(peak - new_peak)
-        total = total * alpha
-        acc = acc * alpha
-        for j in range(size // CHUNK):
-            e = jnp.exp(s_buf[j * CHUNK : (j + 1) * CHUNK, :] - new_peak)
-            total = total + jnp.sum(e, axis=0, keepdims=True)
-            vals = src[v_rows, pl.ds(key_start + j * CHUNK, CHUNK)]
-            acc = acc + dot(vals, e.astype(BF))
-        return new_peak, total, acc
+    tile = rows // 4
+    state = (acc, peaks, totals)
+    peaks[...] = jnp.full_like(peaks, NEG)
+    totals[...] = jnp.zeros_like(totals)
+    acc[...] = jnp.zeros_like(acc)
+    whole = slice(0, rows)
+    lane = lax.broadcasted_iota(jnp.int32, (8, rows), 1)
+    late = jnp.logical_not((lane < B - rows) & (sc[CTX] == 1))
 
     def one_head(h, _):
-        q_h = q_ref[pl.ds(mult(h, HD), HD), cols]
-
-        def prompt(index, carry):
-            _, key_start, low, high = prompt_pass(sc, h, index, start, tile)
-            return one_pass(pbuf, key_start, B, low, high, q_h, h, carry)
-
-        def window(index, carry):
-            first = window_start(sc, t, rows, tile)
-            low = span_ref[0:1, cols]
-            high = span_ref[1:2, cols]
-            return one_pass(cbuf, first, tile + 2 * LMAX, low, high, q_h, h, carry)
-
-        mixed = prompt_pass(sc, h, 0, start, tile)[0]
-        carry = (
-            jnp.full((1, tile), NEG, F32),
-            jnp.zeros((1, tile), F32),
-            jnp.zeros((HD, tile), F32),
-        )
-        carry = lax.fori_loop(0, 1 + mixed, prompt, carry)
-        near = jnp.where((sc[Y] == 1) & (sc[PAIR + 2 * h + 1] == 1), 1, 0)
-        peak, total, acc = lax.fori_loop(0, near, window, carry)
-        o_ref[pl.ds(mult(h, HD), HD), :] = (acc / total).astype(BF)
-        lse_ref[pl.ds(mult(h, 8), 8), :] = jnp.broadcast_to(peak + jnp.log(total), (8, tile))
+        h_rows = pl.ds(mult(h, HD), HD)
+
+        @pl.when(sc[Y] == 0)
+        def _():
+            attend_prompt(sc, buf, state, q_ref[h_rows, :], h, sc[CTX], late, whole)
+
+        @pl.when(sc[CTX] == 1)
+        def _():
+            early = lax.broadcasted_iota(jnp.int32, (8, tile), 1) < B - rows
+            attend_prompt(sc, buf, state, q_ref[h_rows, :tile], h, 0, early, slice(0, tile))
+
+        def window(t, _):
+            cols = pl.ds(mult(t, tile), tile)
+            at = window_start(sc, t, rows, tile)
+            masks = (span_ref[0:1, cols], span_ref[1:2, cols])
+            n = tile + 2 * LMAX
+            attend(buf, state, q_ref[h_rows, cols], h, at, n, None, masks, cols)
+            return 0
+
+        near = jnp.where((sc[Y] == 1) & (sc[PAIR + 2 * h + 1] == 1), 4, 0)
+        lax.fori_loop(0, near, window, 0)
         return 0
 
-    lax.fori_loop(0, heads, one_head, 0)
+    lax.fori_loop(0, acc.shape[0] // HD, one_head, 0)
+
+
+def fwd_far_body(sc, q_ref, ra, rb, acc_in, peaks_in, totals_in, *refs):
+    outs = refs[0:4]
+    lse_ref = refs[4]
+    buf, acc, peaks, totals, sems = refs[5:]
+    rows = ra.shape[1]
+    tile = outs[0].shape[1]
+    acc[...] = acc_in[...]
+    peaks[...] = peaks_in[...]
+    totals[...] = totals_in[...]
+
+    @pl.when(sc[Y] == 1)
+    def _():
+        load_two(sc, ra, rb, buf, sems)
+        state = (acc, peaks, totals)
+
+        def one_head(h, _):
+            q_h = q_ref[pl.ds(mult(h, HD), HD), :]
+            attend_prompt(sc, buf, state, q_h, h, 1, None, slice(0, rows))
+            return 0
+
+        lax.fori_loop(0, acc.shape[0] // HD, one_head, 0)
+
+    lse_ref[...] = peaks[...] + jnp.log(totals[...])
+    for h in range(acc.shape[0] // HD):
+        h_rows = slice(h * HD, (h + 1) * HD)
+        acc[h_rows, :] = acc[h_rows, :] / totals[8 * h : 8 * h + 1, :]
+    for k in range(4):
+        outs[k][...] = acc[:, pl.ds(mult(sc[Z] ^ k, tile), tile)].astype(BF)
 
 
 def bwd_body(
@@ -236,77 +304,111 @@
     *refs,
 ):
     o_in = refs[0:4]
-    lse_in = refs[4:8]
-    g_in = refs[8:12]
-    dq_ref, d_own, d_par, d_r0, d_r1 = refs[12:17]
-    pbuf, cbuf, o_s, lse_s, g_s, acc_p, acc_c, sems = refs[17:]
+    lse_s = refs[4]
+    g_in = refs[5:9]
+    dq_ref, d_own, d_par, d_r0, d_r1 = refs[9:14]
+    pbuf, cbuf, o_s, g_s, acc_p, acc_c, p_rows, c_rows, both_s, dq_s, sems = refs[14:]
     load_pairs(sc, own, par, ra, rb, pbuf, cbuf, sems)
     rows = own.shape[1]
     wide, tile = o_in[0].shape
     heads = wide // HD
     for k in range(4):
-        o_s[k] = o_in[k][...]
-        lse_s[k] = lse_in[k][...]
-        g_s[k] = g_in[k][...]
-
-    def one_pass(src, acc_ref, key_start, size, low, high, q_h, g_h, lse, delta, h, dq):
-        k_rows = pl.ds(mult(h, HD), HD)
-        v_rows = pl.ds(mult(h, HD) + wide, HD)
+        cols = pl.ds(mult(sc[Z] ^ k, tile), tile)
+        o_s[:, cols] = o_in[k][...]
+        g_s[:, cols] = g_in[k][...]
+    later = jnp.where(sc[CTX] > 0, 1, 0)
+    split = jnp.where(sc[CTX] == 1, 1, 0)
+    early = B - rows
+
+    def chunk(src, flat, acc_ref, place, pos, masks, both, lse, delta, h):
+        n_q = lse.shape[1]
+        pair = dot(flat[place, :], both)
+        s = pair[:, :n_q]
+        if masks is not None:
+            row = lax.broadcasted_iota(jnp.int32, s.shape, 0) + pos
+            s = jnp.where((row >= masks[0]) & (row < masks[1]), s, NEG)
+        probs = jnp.exp(s - lse)
+        ds = (probs * (pair[:, n_q:] - delta)).astype(BF)
+        acc_ref[place, :] += dot_t(jnp.concatenate([ds, probs.astype(BF)], axis=1), both)
+        return dot(src[pl.ds(mult(h, HD), HD), place], ds)
+
+    def pair_up(q_h, g_h):
         zero = jnp.zeros_like(q_h)
-        both = jnp.concatenate(
+        return jnp.concatenate(
             [jnp.concatenate([q_h, zero], axis=1), jnp.concatenate([zero, g_h], axis=1)], axis=0
         )
-        for j in range(size // CHUNK):
-            place = pl.ds(key_start + j * CHUNK, CHUNK)
-            keys = src[k_rows, place]
-            vals = src[v_rows, place]
-            s = tdot(keys, q_h)
-            pos = lax.broadcasted_iota(jnp.int32, s.shape, 0) + (key_start + j * CHUNK)
-            s = jnp.where((pos >= low) & (pos < high), s, NEG)
-            probs = jnp.exp(s - lse)
-            ds = probs * (tdot(vals, g_h) - delta)
-            ds = ds.astype(BF)
-            dq = dq + dot(keys, ds)
-            acc_ref[place, :] += dot_t(jnp.concatenate([ds, probs.astype(BF)], axis=1), both)
-        return dq
 
     def one_head(h, _):
+        h_rows = pl.ds(mult(h, HD), HD)
+        v_rows = pl.ds(mult(h, HD) + wide, HD)
+        near = jnp.where((sc[Y] == 1) & (sc[PAIR + 2 * h + 1] == 1), 1, 0)
+
+        def turn(src, dst):
+            dst[...] = jnp.concatenate([src[h_rows, :], src[v_rows, :]], axis=0).T
+
         acc_p[...] = jnp.zeros_like(acc_p)
-        acc_c[...] = jnp.zeros_like(acc_c)
-        h_rows = pl.ds(mult(h, HD), HD)
-
-        def one_tile(k, _):
-            t = sc[Z] ^ k
-            start = sc[CTX] * rows + t * tile
+        turn(pbuf, p_rows)
+
+        @pl.when(sc[Y] == 1)
+        def _():
+            acc_c[...] = jnp.zeros_like(acc_c)
+
+        @pl.when(near == 1)
+        def _():
+            turn(cbuf, c_rows)
+
+        lse = lse_s[pl.ds(mult(h, 8), 8), :][0:1]
+        delta = jnp.sum(
+            o_s[h_rows, :].astype(F32) * g_s[h_rows, :].astype(F32), axis=0, keepdims=True
+        )
+        both_s[...] = pair_up(q_ref[h_rows, :], g_s[h_rows, :])
+        dq_s[...] = jnp.zeros_like(dq_s)
+        lane = lax.broadcasted_iota(jnp.int32, lse.shape, 1)
+        first = (lane < early) & (split == 1)
+
+        def prompt(blk, both, lse, delta, n_q):
+            start = sc[PAIR + 2 * h + blk] * B
+            count = 4 - sc[PAIR + 2 * h + blk]
+
+            def step(at, n):
+                at = pl.multiple_of(at, 128)
+                place = pl.ds(at, n)
+                dq_s[:, :n_q] += chunk(
+                    pbuf, p_rows, acc_p, place, at, None, both, lse, delta, h
+                )
+
+            def run(i, _):
+                step(start + i * 256, 256)
+                return 0
+
+            lax.fori_loop(0, count, run, 0)
+            step(start + count * 256, 128)
+
+        prompt(later, both_s[...], jnp.where(first, FAR, lse), delta, rows)
+
+        @pl.when(split == 1)
+        def _():
+            both = pair_up(q_ref[h_rows, :tile], g_s[h_rows, :tile])
+            prompt(0, both, jnp.where(first, lse, FAR)[:, :tile], delta[:, :tile], tile)
+
+        def window(t, _):
             cols = pl.ds(mult(t, tile), tile)
-            q_h = q_ref[h_rows, cols]
-            g_h = g_s[k, h_rows, :]
-            o_h = o_s[k, h_rows, :]
-            lse = lse_s[k, pl.ds(mult(h, 8), 8), :][0:1]
-            delta = jnp.sum(o_h.astype(F32) * g_h.astype(F32), axis=0, keepdims=True)
-
-            def prompt(index, dq):
-                _, key_start, low, high = prompt_pass(sc, h, index, start, tile)
-                return one_pass(
-                    pbuf, acc_p, key_start, B, low, high, q_h, g_h, lse, delta, h, dq
-                )
-
-            def window(index, dq):
-                first = window_start(sc, t, rows, tile)
-                low = span_ref[0:1, cols]
-                high = span_ref[1:2, cols]
-                return one_pass(
-                    cbuf, acc_c, first, tile + 2 * LMAX, low, high, q_h, g_h, lse, delta, h, dq
-                )
-
-            mixed = prompt_pass(sc, h, 0, start, tile)[0]
-            dq = lax.fori_loop(0, 1 + mixed, prompt, jnp.zeros((HD, tile), F32))
-            near = jnp.where((sc[Y] == 1) & (sc[PAIR + 2 * h + 1] == 1), 1, 0)
-            dq = lax.fori_loop(0, near, window, dq)
-            dq_ref[k, h_rows, :] = (dq * HD**-0.5).astype(BF)
+            at = window_start(sc, t, rows, tile)
+            n = tile + 2 * LMAX
+            masks = (span_ref[0:1, cols], span_ref[1:2, cols])
+            g_h = g_s[h_rows, cols]
+            d = jnp.sum(o_s[h_rows, cols].astype(F32) * g_h.astype(F32), axis=0, keepdims=True)
+            both = pair_up(q_ref[h_rows, cols], g_h)
+            l = lse_s[pl.ds(mult(h, 8), 8), cols][0:1]
+            dq_s[:, cols] += chunk(
+                cbuf, c_rows, acc_c, pl.ds(at, n), at, masks, both, l, d, h
+            )
             return 0
 
-        lax.fori_loop(0, 4, one_tile, 0)
+        lax.fori_loop(0, 4 * near, window, 0)
+        for k in range(4):
+            cols = pl.ds(mult(sc[Z] ^ k, tile), tile)
+            dq_ref[k, h_rows, :] = (dq_s[:, cols] * HD**-0.5).astype(BF)
 
         def give(acc, row, out):
             turned = acc[pl.ds(mult(row, rows), rows), :].T.astype(BF)
@@ -347,6 +449,7 @@
     mixed = refs[0:4]
     x_hbm, cot_hbm = refs[4:6]
     packs = refs[6:8]
+    others = refs[8:24]
     (
         out_ref,
         mb0,
@@ -363,8 +466,8 @@
         mix_own,
         mix_oth,
         gf_ref,
-    ) = refs[8:23]
-    we, ws, wc, mix_s, act_s, gp_s, ib_s, vec_s, thr_s, mb_s, pk_s, x_ref, cot_ref, small_ref, sems, psems = refs[23:]
+    ) = refs[24:39]
+    we, ws, wc, mix_s, act_s, gp_s, ib_s, vec_s, thr_s, mb_s, pk_s, x_ref, cot_ref, small_ref, sems, psems = refs[39:]
     wide, tile = mixed[0].shape
     width = x_ref.shape[1]
     half = width // 2
@@ -373,7 +476,9 @@
     hb = block // 2
     hw = wide // 2
     c = sc[C]
-    n_pack = half + hb + hw + 16
+    hs = hb // 2
+    n_pack = half + hs
+    n_other = hw // 2 + hs // 2 + 16
 
     stages = [[], [], []]
     small = []
@@ -382,27 +487,35 @@
         n = len(stages[stage])
         stages[stage].append(pltpu.make_async_copy(src, dst, sems.at[stage, n]))
 
+    for k in range(4):
+        z = sc[Z] ^ k
+        for j in range(2):
+            xc = pl.ds(mult(sc[X] ^ j, half), half)
+            for q in range(4):
+                cc, yy = c ^ (q // 2), sc[Y] ^ (q % 2)
+                piece = others[4 * q + k]
+                at = j * n_other
+                rows = pl.multiple_of(z * wide + cc * hw + yy * (hw // 2), hw // 2)
+                move(0, piece.at[pl.ds(at, hw // 2), :], wc.at[pl.ds(rows, hw // 2), xc])
+                rows = z * block + cc * hb + hs + yy * (hs // 2)
+                rows = pl.ds(pl.multiple_of(rows, hs // 2), hs // 2)
+                move(2, piece.at[pl.ds(at + hw // 2, hs // 2), :], ws.at[rows, xc])
+            n = 2 * k + j
+            small.append(
+                pltpu.make_async_copy(
+                    others[k].at[pl.ds(at + hw // 2 + hs // 2, 16), :], pk_s.at[n], psems.at[n]
+                )
+            )
     for xh in range(2):
         xc = pl.ds(xh * half, half)
         for z in range(4):
             at = (xh * 4 + z) * n_pack
             for i in range(2):
                 cc = c ^ i
-                rows = pl.multiple_of(z * wide + cc * hw, hw)
-                move(
-                    0,
-                    packs[i].at[pl.ds(at + half + hb, hw), :],
-                    wc.at[pl.ds(rows, hw), xc],
-                )
                 place = pl.ds(pl.multiple_of(z * block + cc * hb, hb), hb)
                 move(1, packs[i].at[pl.ds(at, half), :], we.at[xc, place])
-                move(2, packs[i].at[pl.ds(at + half, hb), :], ws.at[place, xc])
-            n = xh * 4 + z
-            small.append(
-                pltpu.make_async_copy(
-                    packs[0].at[pl.ds(at + half + hb + hw, 16), :], pk_s.at[n], psems.at[n]
-                )
-            )
+                place = pl.ds(pl.multiple_of(z * block + cc * hb, hs), hs)
+                move(2, packs[i].at[pl.ds(at + half, hs), :], ws.at[place, xc])
     mine = pl.ds(mult(sc[Z], tile), tile)
     small.append(pltpu.make_async_copy(x_hbm.at[mine, :], x_ref, psems.at[8]))
     small.append(pltpu.make_async_copy(cot_hbm.at[mine, :], cot_ref, psems.at[9]))
@@ -414,12 +527,13 @@
         copy.wait()
     for k in range(4):
         mix_s[pl.ds(mult(sc[Z] ^ k, wide), wide), :] = mixed[k][...]
-    for xh in range(2):
-        for z in range(4):
-            pack = pk_s[xh * 4 + z].astype(F32)
-            at = z * block + xh * half
-            thr_s[:, at : at + half] = pack[:8]
-        vec_s[:, xh * half : (xh + 1) * half] = pk_s[xh * 4].astype(F32)[:8]
+    for k in range(4):
+        for j in range(2):
+            pack = pk_s[2 * k + j].astype(F32)
+            at = pl.multiple_of((sc[Z] ^ k) * block + (sc[X] ^ j) * half, 128)
+            thr_s[:, pl.ds(at, half)] = pack[:8]
+            if k == 0:
+                vec_s[:, pl.ds(mult(sc[X] ^ j, half), half)] = pack[:8]
 
     baseline = vec_s[0:1, :]
     scaling = vec_s[1:2, :]
@@ -499,17 +613,18 @@
     hw = mix[0].shape[0] // 4
     for x in range(2):
         xc = slice(x * half, (x + 1) * half)
-        for z in range(4):
-            zc = slice(z * hb, (z + 1) * hb)
+        for k in range(4):
+            z = sc[Z] ^ k
+            zc = pl.ds(mult(z, hb), hb)
             e = sum(tdot(nl[i][:, xc], ib[i][:, zc]) for i in range(2)).astype(BF)
             s = sum(tdot(act[i][:, zc], fb[i][:, xc]) for i in range(2)).astype(BF)
-            zr = slice(z * hw, (z + 1) * hw)
+            zr = pl.ds(mult(z, hw), hw)
             m = sum(dot(mix[i][zr, :], ab[i][:, xc]) for i in range(2)).astype(BF)
             at = 0
             for v in (e, s, m):
                 n = v.shape[0] // 2
                 for yh in range(2):
-                    g_ref[yh, x, z, at : at + n, :] = v[yh * n : (yh + 1) * n]
+                    g_ref[yh, x, k, at : at + n, :] = v[yh * n : (yh + 1) * n]
                 at += n
 
 
@@ -670,7 +785,8 @@
                 (
                     sds((16, half), F32),
                     sds((part + 16, half), BF),
-                    sds((half + hb + hw + 16, half), BF),
+                    sds((half + hb // 2, half), BF),
+                    sds((hw // 2 + hb // 4 + 16, half), BF),
                 ),
                 ins=[SM] + [VM] * 12,
                 cost=cost(0, 8 * half * width),
@@ -692,16 +808,18 @@
             weights = jnp.stack(
                 [lax.all_gather(p[2], "tensor", axis=0) for p in packed]
             ).reshape(-1, half)
+            other_wide = jnp.concatenate([p[3] for p in packed])
         else:
             own_wt = wt
-            small, wtc, wpack = pack(wt, expand, shrink, combine, offsets, vectors)
+            small, wtc, wpack, o_c = pack(wt, expand, shrink, combine, offsets, vectors)
             got_wt = px(wtc)
             weights = lax.all_gather(wpack, ("dp", "tensor"), axis=0, tiled=True)
+            other_wide = jnp.concatenate([o_c, px(o_c)])
 
         def after(v, *deps):
             return lax.optimization_barrier((v, *deps))[0]
 
-        got_wt2 = pc(got_wt)
+        got_wt2 = after(pc(got_wt), other_wide)
 
         qT, kvT, wt_full = call(
             qkv_body,
@@ -723,28 +841,45 @@
             [low[None], high[None], jnp.zeros((6, rows), jnp.int32)], axis=0
         )
 
+        z_near = pz[1](other_wide)
+        z_far = pz[2](other_wide)
+        other_z = [other_wide, z_near, z_far, pz[1](z_far)]
+
         par = pc(kvT)
         ra = lax.ppermute(kvT, "cy", [(0, 1)])
-        rb = pc(ra)
 
         kv_scratch = [pltpu.VMEM((2 * wide, 2 * rows), BF), pltpu.VMEM((2 * wide, 2 * rows), BF)]
-        o_tiles = [None] * 4
-        lses = [None] * 4
-        mixed = [None] * 4
-        last = qT
-        for k in (1, 2, 3, 0):
-            last = after(qT, last) if k else after(qT, last, mixed[1])
-            o_tiles[k], lses[k] = call(
-                functools.partial(fwd_body, k),
-                (sds((wide, tile), BF), sds((8 * heads, tile), F32)),
-                ins=[SM, VM, VM] + [ANY] * 4,
-                scratch=kv_scratch
-                + [pltpu.VMEM((B, tile), F32), pltpu.SemaphoreType.DMA((4,))],
-                cost=cost(4 * B * tile * wide, 4 * 2 * wide * rows, B * tile * heads),
-            )(sc, last, span, kvT, par, ra, rb)
-            last = o_tiles[k]
-            mixed[k] = pz[k](o_tiles[k])
-        weights2 = pc(after(weights, *mixed))
+        state = [
+            sds((wide, rows), F32),
+            sds((8 * heads, rows), F32),
+            sds((8 * heads, rows), F32),
+        ]
+        sofar = call(
+            fwd_near_body,
+            tuple(state),
+            ins=[SM, VM, VM] + [ANY] * 2,
+            scratch=[kv_scratch[0], pltpu.SemaphoreType.DMA((2,))],
+            cost=cost(0, 1000),
+        )(sc, qT, span, kvT, par)
+        ra = after(ra, sofar[0])
+        rb = pc(after(ra, z_near, z_far))
+        other_y = [py(after(w, ra)) for w in other_z[:3]]
+        *o_tiles, lse = call(
+            fwd_far_body,
+            (*[sds((wide, tile), BF)] * 4, sds((8 * heads, rows), F32)),
+            ins=[SM, VM] + [ANY] * 2 + [VM] * 3,
+            scratch=[kv_scratch[0]]
+            + [pltpu.VMEM(v.shape, v.dtype) for v in state]
+            + [pltpu.SemaphoreType.DMA((2,))],
+            cost=cost(0, 1000),
+        )(sc, qT, ra, rb, *sofar)
+        relayed = after(other_z[3], o_tiles[0])
+        o_tiles = [after(o, *other_y, relayed) for o in o_tiles]
+        other_y = other_y + [py(relayed)]
+        mixed = [pz[k](o_tiles[k]) for k in range(4)]
+        weights2 = pc(after(weights, *mixed, other_y[3]))
+        others = other_z + other_y
+        others = others + [pc(after(w, o_tiles[0])) for w in others]
 
         outs = call(
             mid_body,
@@ -756,7 +891,7 @@
                 *[sds((width // 2, tile), BF)] * 2,
                 sds((tile, width), F32),
             ),
-            ins=[SM] + [VM] * 4 + [ANY] * 4,
+            ins=[SM] + [VM] * 4 + [ANY] * 20,
             scratch=[
                 pltpu.VMEM((width, hidden), BF),
                 pltpu.VMEM((hidden, width), BF),
@@ -772,11 +907,11 @@
                 pltpu.VMEM((tile, width), BF),
                 pltpu.VMEM((tile, width), BF),
                 pltpu.VMEM((16, width), F32),
-                pltpu.SemaphoreType.DMA((3, 16)),
+                pltpu.SemaphoreType.DMA((3, 48)),
                 pltpu.SemaphoreType.DMA((10,)),
             ],
             cost=cost(8 * tile * width * hidden + 4 * tile * width * width, 4 * width * hidden),
-        )(sc, *mixed, x, cot, weights, weights2)
+        )(sc, *mixed, x, cot, weights, weights2, *others)
         out_low = outs[0]
         mb = outs[1:5]
         nl, fb, ab, act_own, act_oth, ib_own, ib_oth, mix_own, mix_oth, grad_first = outs[5:]
@@ -784,28 +919,30 @@
 
         theirs = [pc(v) for v in (nl, fb, ab, act_oth, ib_oth, mix_oth)]
         gathered = lax.all_gather(out_low, "tensor", axis=0)
-        layer_out = gathered[:, :tile].reshape(rows, width)
 
         outs = call(
             bwd_body,
             (sds((4, wide, tile), BF), *[sds((2 * wide, rows), BF)] * 4),
-            ins=[SM, VM, VM] + [ANY] * 4 + [VM] * 12,
+            ins=[SM, VM, VM] + [ANY] * 4 + [VM] * 9,
             scratch=kv_scratch
             + [
-                pltpu.VMEM((4, wide, tile), BF),
-                pltpu.VMEM((4, 8 * heads, tile), F32),
-                pltpu.VMEM((4, wide, tile), BF),
+                pltpu.VMEM((wide, rows), BF),
+                pltpu.VMEM((wide, rows), BF),
                 pltpu.VMEM((2 * rows, 2 * HD), F32),
                 pltpu.VMEM((2 * rows, 2 * HD), F32),
+                pltpu.VMEM((2 * rows, 2 * HD), BF),
+                pltpu.VMEM((2 * rows, 2 * HD), BF),
+                pltpu.VMEM((2 * HD, 2 * rows), BF),
+                pltpu.VMEM((HD, rows), F32),
                 pltpu.SemaphoreType.DMA((4,)),
             ],
             cost=cost(10 * B * rows * wide, 4 * 4 * wide * rows, B * rows * heads),
-        )(sc, qT, span, kvT, par, ra, rb, *o_tiles, *lses, *grads)
+        )(sc, qT, span, kvT, par, ra, rb, *o_tiles, lse, *grads)
         dq, d_own, d_par, d_r0, d_r1 = outs
         got_par = pc(d_par)
         got_r = pc(d_r1)
         prompt_part = (d_r0.astype(F32) + got_r.astype(F32)).astype(BF)
-        nl = after(nl, prompt_part)
+        nl = after(nl, prompt_part, got_par)
         n_part = half // 2 + hb // 2 + hw // 2
         g = call(
             wg_body,
@@ -821,8 +958,11 @@
             cost=cost(2 * rows * width * 3 * wide, 8 * rows * width),
         )(sc, after(d_own, gathered), got_par, from_y, dq, wt_full)
         kv_back, back = outs[0], outs[1:]
-        relay = call(pair_body, sds((tile, width), BF), ins=[VM] * 2)(back[2], pz[1](back[3]))
-        near = pz[1](back[1])
+        gathered = after(gathered, kv_back)
+        layer_out = gathered[:, :tile].reshape(rows, width)
+        passed = pz[1](back[3])
+        relay = call(pair_body, sds((tile, width), BF), ins=[VM] * 2)(back[2], passed)
+        near = pz[1](after(back[1], passed))
         far = pz[2](relay)
         gp = call(
             gp_body,
@@ -856,8 +996,15 @@
             ins=[SM] + [VM] * 4,
             cost=cost(rows * width, 6 * rows * width),
         )(sc, *token_tiles)
-        def finish_ff(mine):
-            quarters = [mine, py(mine)]
+        def sum_z(parts, wait=()):
+            relay = after(add(parts[2], pz[1](parts[3])), *wait)
+            near = pz[1](parts[1])
+            far = pz[2](relay)
+            total = parts[0].astype(F32) + near.astype(F32) + far.astype(F32)
+            return total.astype(BF)
+
+        def finish_ff(mine, *wait):
+            quarters = [mine, after(py(mine), *wait)]
             quarters = quarters + [pc(q) for q in quarters]
             return call(
                 wfin_body,
@@ -880,7 +1027,7 @@
         if generic:
             g = lax.psum_scatter(g, "cy", scatter_dimension=0, tiled=False)
             parts = [
-                finish_ff(lax.psum_scatter(v, "tensor", scatter_dimension=0, tiled=False))
+                finish_ff(sum_z(v))
                 for v in (g[0], g[1])
             ]
 
@@ -900,10 +1047,10 @@
             g = lax.psum_scatter(
                 g.reshape(-1, half), ("cy", "dp"), scatter_dimension=0, tiled=True
             )
-            g = after(g, tiles_near)
-            g = lax.psum_scatter(g, "tensor", scatter_dimension=0, tiled=True)
-            summed = finish_ff(g)
+            g = after(g, tiles_near, tiles_far)
+            g = sum_z(g.reshape(4, n_part, half))
             grad_project, lines, *vecs = finish_gp(add(gp[0], px(gp[1])))
+            summed = finish_ff(g, grad_tokens, layer_out, grad_project)
             n_off = offsets.shape[1]
             grad_offsets = lax.dynamic_slice_in_dim(
                 lines[0].reshape(2, wide), dp * n_off, n_off, 1

time: 343 us -> 310 us (0.904)
  waiting for transfers between devices: 168 us -> 136 us
  Pallas kernels: 98 us -> 85.2 us
  starting transfers between devices: 39.1 us -> 48.5 us
    all_gather x1, waiting for transfers between devices: 24.8 us -> 1.46 us  [on_device(): weights = lax.all_gather(wpack, ('dp', 'tensor'), axis=0, tiled=True)]
    ppermute x1, waiting for transfers between devices: 17.3 us -> 0.01 us  [on_device(): ra = lax.ppermute(kvT, 'cy', [(0, 1)])]
    ppermute x32 -> x51, waiting for transfers between devices: 111 us -> 123 us  [swap(): return lambda v: lax.ppermute(v, axis, [(i, i ^ k) for i in range(size)])]
    ppermute x32 -> x51, starting transfers between devices: 33.7 us -> 43.2 us  [swap(): return lambda v: lax.ppermute(v, axis, [(i, i ^ k) for i in range(size)])]
    pallas_call x5 -> x3, Pallas kernels: 24.2 us -> 16.6 us  [the longest x1 12.2 us: on_device(): call(fwd_near_body, tuple(state), ins=[SM, VM, VM] + [ANY] * 2, scratch=[...]
    pallas_call x1, Pallas kernels: 22 us -> 16 us  [on_device(): call(bwd_body, (sds((4, wide, tile), BF), *[sds((2 * wide, rows), BF)] *...]
    unnamed x74 -> x113, local copies, waits for them, and re-layouts: 10.2 us -> 11.1 us
  transfers between devices with their start and end apart: 38 -> 56, of which waited for: 22 -> 26; matrix products, arithmetic and copies ran while one was open for 3% -> 4% of each run, Pallas kernels for 23% -> 20%
where the time goes in v3:
time: 310 us; the launch traced here: 309 us
  waiting for transfers between devices  136 us (44%)
  Pallas kernels  85.2 us (27%)
  starting transfers between devices  48.5 us (16%)
  local copies, waits for them, and re-layouts  17.8 us (6%)
  between operations  14.4 us (5%)
  other arithmetic  6.35 us (2%)
    ppermute x51, waiting for transfers between devices, swap(): return lambda v: lax.ppermute(v, axis, [(i, i ^ k) for i in range(size)])  123 us
    ppermute x51, starting transfers between devices, swap(): return lambda v: lax.ppermute(v, axis, [(i, i ^ k) for i in range(size)])  43.2 us
    pallas_call x1, Pallas kernels, on_device(): call(mid_body, (sds((tile + 16, width), BF), *[sds((wide, tile), BF)] * 4...  17 us
    pallas_call x1, Pallas kernels, on_device(): call(bwd_body, (sds((4, wide, tile), BF), *[sds((2 * wide, rows), BF)] *...  16 us
    pallas_call x1, Pallas kernels, on_device(): call(fwd_near_body, tuple(state), ins=[SM, VM, VM] + [ANY] * 2, scratch=[...  12.2 us
    ppermute x1, waiting for transfers between devices, on_device(): from_y = lax.ppermute(prompt_part, 'cy', [(1, 0)])  12.1 us
    unnamed x113, local copies, waits for them, and re-layouts  11.1 us
    pallas_call x1, Pallas kernels, on_device(): call(wg_body, sds((2, 2, 4, n_part, half), BF), ins=[SM] + [VM] * 12, cos...  9.09 us
  transfers between devices with their start and end apart: 56, of which 26 were waited for; matrix products, arithmetic and copies ran while one was open for 4% of the time, Pallas kernels for 20%

profile of v3, /device:TPU:0, one launch (start us, length us, event | category | flops | bytes accessed | tf_op | source)
XLA Modules:
  0.0 308.6 jit_solution(1602972178190515383)
XLA Ops:
  14.3 6.7 %collective-permute-done.w0_ref = bf16[304,384]{1,0:T(8,128)(2,1)S(1)} collective-permute-done((bf16[304,384]{1,0:T(8,128)(2,1)}, bf16[304,384]{1,0:T(8,128)(2,1)S(1)}, u32[]{:S(2)}, u32[]{:S(2)}) %collective-permute-start) | collective-permute-done | bytes 233504 | tf_op jit(solution)/shard_map/ppermute | solution.py:726
  23.6 4.5 %shard_map.264 = (bf16[192,1024]{1,0:T(8,128)(2,1)}, bf16[384,1024]{1,0:T(8,128)(2,1)}, bf16[576,768]{1,0:T(8,128)(2,1)}) custom-call(s32[14]{0:T(128)} %concatenate.9.sc, bf16[1024,768]{1,0:T(8,128)(2,1)} %bitcast.41, bf16[576,384]{1,0:T(8,128)(2,1)} %bitcast.45, f32[16,384]{1,0:T(8,128)} %get-tuple-element.96.small_ref, bf16[304,384]{1,0:T(8,128)(2,1)} %copy-done.48, ...), custom_call_target="tpu_custom_call" | custom-call | flops 905969664 | bytes 3145728 | tf_op jit(solution)/shard_map/pallas_call | solution.py:824
  28.0 3.7 %collective-permute-start.3 = (bf16[384,1024]{1,0:T(8,128)(2,1)}, bf16[384,1024]{1,0:T(8,128)(2,1)S(1)}, u32[]{:S(2)}, u32[]{:S(2)}) collective-permute-start(bf16[384,1024]{1,0:T(8,128)(2,1)} %get-tuple-element.101.own), channel_id=1, source_target_pairs={{0,8},{1,9},{2,10},{3,11},{4,12},{5,13},{6,14},{7,15},{16,24},{17,... | collective-permute-start | bytes 2359304 | tf_op jit(solution)/shard_map/ppermute | solution.py:849
  39.5 12.2 %shard_map.265 = (f32[192,1024]{1,0:T(8,128)}, f32[24,1024]{1,0:T(8,128)}, f32[24,1024]{1,0:T(8,128)}) custom-call(s32[14]{0:T(128)} %concatenate.9.sc, bf16[192,1024]{1,0:T(8,128)(2,1)} %get-tuple-element.100.q_ref, s32[8,1024]{1,0:T(8,128)} %add_add_fusion.span_ref, bf16[384,1024]{1,0:T(8,128)(2,1)} %get-tuple-element.101.own, bf16[384,1024]{1,0:T(8,128)(2,1)} %copy-done.8), custom_call_target="tpu_custom_call" | custom-call | bytes 1000 | tf_op jit(solution)/shard_map/pallas_call | solution.py:857
  51.8 4.8 %collective-permute-start.7 = (bf16[384,1024]{1,0:T(8,128)(2,1)S(1)}, bf16[384,1024]{1,0:T(8,128)(2,1)S(1)}, u32[]{:S(2)}, u32[]{:S(2)}) collective-permute-start(bf16[384,1024]{1,0:T(8,128)(2,1)S(1)} %collective-permute-done.3.ra), channel_id=1, source_target_pairs={{0,4},{4,0},{1,5},{5,1},{2,6},{6,2},{3,7},{7,3},{8,12},{12,8},{9,1... | collective-permute-start | bytes 2359304 | tf_op jit(solution)/shard_map/ppermute | solution.py:726
  62.5 16.0 %collective-permute-done.11.refs_11_ = bf16[320,384]{1,0:T(8,128)(2,1)S(1)} collective-permute-done((bf16[320,384]{1,0:T(8,128)(2,1)S(1)}, bf16[320,384]{1,0:T(8,128)(2,1)S(1)}, u32[]{:S(2)}, u32[]{:S(2)}) %collective-permute-start.11) | collective-permute-done | bytes 245792 | tf_op jit(solution)/shard_map/ppermute | solution.py:726
  79.7 3.3 %collective-permute-start.14 = (bf16[192,256]{1,0:T(8,128)(2,1)}, bf16[192,256]{1,0:T(8,128)(2,1)S(1)}, u32[]{:S(2)}, u32[]{:S(2)}) collective-permute-start(bf16[192,256]{1,0:T(8,128)(2,1)} %get-tuple-element.118.refs_3_), channel_id=1, source_target_pairs={{0,3},{1,2},{2,1},{3,0},{4,7},{5,6},{6,5},{7,4},{8,11},{9,10},{10,... | collective-permute-start | bytes 294920 | tf_op jit(solution)/shard_map/ppermute | solution.py:726
  83.0 6.1 %collective-permute-done.12.refs_1_ = bf16[192,256]{1,0:T(8,128)(2,1)S(1)} collective-permute-done((bf16[192,256]{1,0:T(8,128)(2,1)}, bf16[192,256]{1,0:T(8,128)(2,1)S(1)}, u32[]{:S(2)}, u32[]{:S(2)}) %collective-permute-start.12) | collective-permute-done | bytes 98336 | tf_op jit(solution)/shard_map/ppermute | solution.py:726
  89.1 4.6 %collective-permute-done.13.refs_2_ = bf16[192,256]{1,0:T(8,128)(2,1)S(1)} collective-permute-done((bf16[192,256]{1,0:T(8,128)(2,1)}, bf16[192,256]{1,0:T(8,128)(2,1)S(1)}, u32[]{:S(2)}, u32[]{:S(2)}) %collective-permute-start.13) | collective-permute-done | bytes 98336 | tf_op jit(solution)/shard_map/ppermute | solution.py:726
  96.3 5.1 %collective-permute-done.17.refs_16_ = bf16[320,384]{1,0:T(8,128)(2,1)S(1)} collective-permute-done((bf16[320,384]{1,0:T(8,128)(2,1)S(1)}, bf16[320,384]{1,0:T(8,128)(2,1)S(1)}, u32[]{:S(2)}, u32[]{:S(2)}) %collective-permute-start.17) | collective-permute-done | bytes 245792 | tf_op jit(solution)/shard_map/ppermute | solution.py:726
  104.9 17.0 %shard_map.267 = (bf16[272,768]{1,0:T(8,128)(2,1)}, bf16[192,256]{1,0:T(8,128)(2,1)}, bf16[192,256]{1,0:T(8,128)(2,1)}, bf16[192,256]{1,0:T(8,128)(2,1)}, bf16[1...) custom-call(s32[14]{0:T(128)} %concatenate.9.sc, ...), custom_call_target="tpu_custom_call" | custom-call | flops 5435817984 | bytes 9437184 | tf_op jit(solution)/shard_map/pallas_call | solution.py:884
  127.7 10.9 %collective-permute-done.26.refs_7_ = bf16[192,256]{1,0:T(8,128)(2,1)S(1)} collective-permute-done((bf16[192,256]{1,0:T(8,128)(2,1)}, bf16[192,256]{1,0:T(8,128)(2,1)S(1)}, u32[]{:S(2)}, u32[]{:S(2)}) %collective-permute-start.26) | collective-permute-done | bytes 98336 | tf_op jit(solution)/shard_map/ppermute | solution.py:726
  139.2 16.0 %shard_map.268 = (bf16[4,192,256]{2,1,0:T(8,128)(2,1)}, bf16[384,1024]{1,0:T(8,128)(2,1)}, bf16[384,1024]{1,0:T(8,128)(2,1)}, bf16[384,1024]{1,0:T(8,128)(2,1)}, bf16[384,1024]{1,0:T(8,128)(2,1)}) custom-call(s32[14]{0:T(128)} %concatenate.9.sc, bf16[192,1024]{1,0:T(8,128)(2,1)} %get-tuple-element.100.q_ref, s32[8,1024]{1,0:T(8,128)} %add_add_fusion.span_ref, ...), custom_call_target="tpu_custom_call" | custom-call | flops 2264924160 | bytes 3145728 | tf_op jit(solution)/shard_map/pallas_call | solution.py:923
  164.4 9.1 %shard_map.275 = bf16[2,2,4,432,384]{4,3,2,1,0:T(8,128)(2,1)} custom-call(s32[14]{0:T(128)} %concatenate.9.sc, bf16[256,768]{1,0:T(8,128)(2,1)} %get-tuple-element.156.refs_0_, bf16[256,768]{1,0:T(8,128)(2,1)} %get-tuple-element.157.refs_1_, bf16[256,768]{1,0:T(8,128)(2,1)} %get-tuple-element.158.refs_2_, bf16[256,1536]{1,0:T(8,128)(2,1)} %get-tuple-element.159.refs_3_, ...), custom_call_target="tpu_custom_call" | custom-call | flops 2415919104 | bytes 9437184 | tf_op jit(solution)/shard_map/pallas_call | solution.py:947
  173.5 12.1 %collective-permute-done.30.c_ref = bf16[384,1024]{1,0:T(8,128)(2,1)S(1)} collective-permute-done((bf16[384,1024]{1,0:T(8,128)(2,1)S(1)}, bf16[384,1024]{1,0:T(8,128)(2,1)S(1)}, u32[]{:S(2)}, u32[]{:S(2)}) %collective-permute-start.30) | collective-permute-done | bytes 786464 | tf_op jit(solution)/shard_map/ppermute | solution.py:953
  186.5 4.6 %shard_map.269 = (bf16[4,384,256]{2,1,0:T(8,128)(2,1)}, bf16[256,768]{1,0:T(8,128)(2,1)}, bf16[256,768]{1,0:T(8,128)(2,1)}, bf16[256,768]{1,0:T(8,128)(2,1)}, bf16[256,768]{1,0:T(8,128)(2,1)}) custom-call(s32[14]{0:T(128)} %concatenate.9.sc, bf16[384,1024]{1,0:T(8,128)(2,1)} %get-tuple-element.136.a_ref, bf16[384,1024]{1,0:T(8,128)(2,1)} %copy-done.11, ...), custom_call_target="tpu_custom_call" | custom-call | flops 905969664 | bytes 6291456 | tf_op jit(solution)/shard_map/pallas_call | solution.py:954
  193.0 7.6 %collective-permute-start.31 = (bf16[256,768]{1,0:T(8,128)(2,1)S(1)}, bf16[256,768]{1,0:T(8,128)(2,1)S(1)}, u32[]{:S(2)}, u32[]{:S(2)}) collective-permute-start(bf16[256,768]{1,0:T(8,128)(2,1)S(1)} %copy-done.32), channel_id=1, source_target_pairs={{0,1},{1,0},{2,3},{3,2},{4,5},{5,4},{6,7},{7,6},{8,9},{9,8},{10,11... | collective-permute-start | bytes 1179656 | tf_op jit(solution)/shard_map/ppermute | solution.py:726
  200.6 4.1 %shard_map.271 = bf16[2,2,304,384]{3,2,1,0:T(8,128)(2,1)} custom-call(s32[14]{0:T(128)} %concatenate.9.sc, bf16[4,192,256]{2,1,0:T(8,128)(2,1)} %get-tuple-element.140.dq_ref, bf16[4,384,256]{2,1,0:T(8,128)(2,1)} %get-tuple-element.142.kv_ref, bf16[1024,768]{1,0:T(8,128)(2,1)} %bitcast.43, bf16[4,16,768]{2,1,0:T(8,128)(2,1)} %slice.38.small_ref), custom_call_target="tpu_custom_call" | custom-call | flops 905969664 | bytes 3145728 | tf_op jit(solution)/shard_map/pallas_call | solution.py:967
  205.9 3.7 %collective-permute-done.31.b_ref = bf16[256,768]{1,0:T(8,128)(2,1)S(1)} collective-permute-done((bf16[256,768]{1,0:T(8,128)(2,1)S(1)}, bf16[256,768]{1,0:T(8,128)(2,1)S(1)}, u32[]{:S(2)}, u32[]{:S(2)}) %collective-permute-start.31) | collective-permute-done | bytes 393248 | tf_op jit(solution)/shard_map/ppermute | solution.py:726
  213.5 9.6 %collective-permute-done.32.b_ref = bf16[256,768]{1,0:T(8,128)(2,1)S(1)} collective-permute-done((bf16[256,768]{1,0:T(8,128)(2,1)S(1)}, bf16[256,768]{1,0:T(8,128)(2,1)S(1)}, u32[]{:S(2)}, u32[]{:S(2)}) %collective-permute-start.32) | collective-permute-done | bytes 393248 | tf_op jit(solution)/shard_map/ppermute | solution.py:726
  223.1 9.6 %collective-permute-done.33.c_ref = bf16[256,768]{1,0:T(8,128)(2,1)S(1)} collective-permute-done((bf16[256,768]{1,0:T(8,128)(2,1)}, bf16[256,768]{1,0:T(8,128)(2,1)S(1)}, u32[]{:S(2)}, u32[]{:S(2)}) %collective-permute-start.33) | collective-permute-done | bytes 393248 | tf_op jit(solution)/shard_map/ppermute | solution.py:726
  237.2 15.9 %collective-permute-done.36.refs_2_ = bf16[256,768]{1,0:T(8,128)(2,1)S(1)} collective-permute-done((bf16[256,768]{1,0:T(8,128)(2,1)}, bf16[256,768]{1,0:T(8,128)(2,1)S(1)}, u32[]{:S(2)}, u32[]{:S(2)}) %collective-permute-start.36) | collective-permute-done | bytes 393248 | tf_op jit(solution)/shard_map/ppermute | solution.py:726
  257.7 8.4 %collective-permute-done.48 = bf16[432,384]{1,0:T(8,128)(2,1)S(1)} collective-permute-done((bf16[432,384]{1,0:T(8,128)(2,1)S(1)}, bf16[432,384]{1,0:T(8,128)(2,1)S(1)}, u32[]{:S(2)}, u32[]{:S(2)}) %collective-permute-start.48) | collective-permute-done | bytes 331808 | tf_op jit(solution)/shard_map/ppermute | solution.py:726
  268.9 18.1 %collective-permute-done.47 = bf16[432,384]{1,0:T(8,128)(2,1)S(1)} collective-permute-done((bf16[432,384]{1,0:T(8,128)(2,1)S(1)}, bf16[432,384]{1,0:T(8,128)(2,1)S(1)}, u32[]{:S(2)}, u32[]{:S(2)}) %collective-permute-start.47) | collective-permute-done | bytes 331808 | tf_op jit(solution)/shard_map/ppermute | solution.py:726
  (242 shorter events, 80.3 us)
Async XLA Ops:
  7.2 88.0 %all-gather.4.cloned.1.call-start = ((), (), s32[]{:S(2)}) async-start(), calls=%async_computation.1 | async-start | bytes 3981312 | tf_op jit(solution)/shard_map/all_gather | solution.py:816
  11.2 175.3 %all-gather.6.cloned.1.call-start = ((), (), s32[]{:S(2)}) async-start(), calls=%async_computation.3 | async-start | bytes 2088960 | tf_op jit(solution)/shard_map/all_gather | solution.py:921
  28.0 23.7 %collective-permute-start.3 = (bf16[384,1024]{1,0:T(8,128)(2,1)}, bf16[384,1024]{1,0:T(8,128)(2,1)S(1)}, u32[]{:S(2)}, u32[]{:S(2)}) collective-permute-start(bf16[384,1024]{1,0:T(8,128)(2,1)} %get-tuple-element.101.own), channel_id=1, source_target_pairs={{0,8},{1,9},{2,10},{3,11},{4,12},{5,13},{6,14},{7,15},{16,24},{17,... | collective-permute-start | bytes 2359304 | tf_op jit(solution)/shard_map/ppermute | solution.py:849
  31.8 19.9 %collective-permute-start.6 = (bf16[320,384]{1,0:T(8,128)(2,1)S(1)}, bf16[320,384]{1,0:T(8,128)(2,1)S(1)}, u32[]{:S(2)}, u32[]{:S(2)}) collective-permute-start(bf16[320,384]{1,0:T(8,128)(2,1)S(1)} %constant_dynamic-update-slice_fusion.refs_8_), channel_id=1, source_target_pairs={{0,2},{1,3},{2,0},{3,1},{4,6},{5,7},{6,4},{7,5},{8,10},{9,11},{10,... | collective-permute-start | bytes 737288 | tf_op jit(solution)/shard_map/ppermute | solution.py:726
  34.5 17.3 %collective-permute-start.5 = (bf16[320,384]{1,0:T(8,128)(2,1)S(1)}, bf16[320,384]{1,0:T(8,128)(2,1)S(1)}, u32[]{:S(2)}, u32[]{:S(2)}) collective-permute-start(bf16[320,384]{1,0:T(8,128)(2,1)S(1)} %constant_dynamic-update-slice_fusion.refs_8_), channel_id=1, source_target_pairs={{0,1},{1,0},{2,3},{3,2},{4,5},{5,4},{6,7},{7,6},{8,9},{9,8},{10,11... | collective-permute-start | bytes 737288 | tf_op jit(solution)/shard_map/ppermute | solution.py:726
  56.6 21.9 %collective-permute-start.11 = (bf16[320,384]{1,0:T(8,128)(2,1)S(1)}, bf16[320,384]{1,0:T(8,128)(2,1)S(1)}, u32[]{:S(2)}, u32[]{:S(2)}) collective-permute-start(bf16[320,384]{1,0:T(8,128)(2,1)S(1)} %collective-permute-done.6.refs_10_), channel_id=1, source_target_pairs={{0,1},{1,0},{2,3},{3,2},{4,5},{5,4},{6,7},{7,6},{8,9},{9,8},{10,11... | collective-permute-start | bytes 737288 | tf_op jit(solution)/shard_map/ppermute | solution.py:726
  57.1 21.5 %collective-permute-start.8 = (bf16[320,384]{1,0:T(8,128)(2,1)S(1)}, bf16[320,384]{1,0:T(8,128)(2,1)S(1)}, u32[]{:S(2)}, u32[]{:S(2)}) collective-permute-start(bf16[320,384]{1,0:T(8,128)(2,1)S(1)} %constant_dynamic-update-slice_fusion.refs_8_), channel_id=1, source_target_pairs={{0,8},{8,0},{1,9},{9,1},{2,10},{10,2},{3,11},{11,3},{4,12},{12,4},... | collective-permute-start | bytes 737288 | tf_op jit(solution)/shard_map/ppermute | solution.py:726
  57.1 21.5 %collective-permute-start.9 = (bf16[320,384]{1,0:T(8,128)(2,1)S(1)}, bf16[320,384]{1,0:T(8,128)(2,1)S(1)}, u32[]{:S(2)}, u32[]{:S(2)}) collective-permute-start(bf16[320,384]{1,0:T(8,128)(2,1)S(1)} %collective-permute-done.5.refs_9_), channel_id=1, source_target_pairs={{0,8},{8,0},{1,9},{9,1},{2,10},{10,2},{3,11},{11,3},{4,12},{12,4},... | collective-permute-start | bytes 737288 | tf_op jit(solution)/shard_map/ppermute | solution.py:726
  59.1 19.5 %collective-permute-start.10 = (bf16[320,384]{1,0:T(8,128)(2,1)S(1)}, bf16[320,384]{1,0:T(8,128)(2,1)S(1)}, u32[]{:S(2)}, u32[]{:S(2)}) collective-permute-start(bf16[320,384]{1,0:T(8,128)(2,1)S(1)} %collective-permute-done.6.refs_10_), channel_id=1, source_target_pairs={{0,8},{8,0},{1,9},{9,1},{2,10},{10,2},{3,11},{11,3},{4,12},{12,4},... | collective-permute-start | bytes 737288 | tf_op jit(solution)/shard_map/ppermute | solution.py:726
  78.5 15.2 %collective-permute-start.15 = (bf16[320,384]{1,0:T(8,128)(2,1)S(1)}, bf16[320,384]{1,0:T(8,128)(2,1)S(1)}, u32[]{:S(2)}, u32[]{:S(2)}) collective-permute-start(bf16[320,384]{1,0:T(8,128)(2,1)S(1)} %collective-permute-done.11.refs_11_), channel_id=1, source_target_pairs={{0,8},{8,0},{1,9},{9,1},{2,10},{10,2},{3,11},{11,3},{4,12},{12,4},... | collective-permute-start | bytes 737288 | tf_op jit(solution)/shard_map/ppermute | solution.py:726
  78.7 15.1 %collective-permute-start.13 = (bf16[192,256]{1,0:T(8,128)(2,1)}, bf16[192,256]{1,0:T(8,128)(2,1)S(1)}, u32[]{:S(2)}, u32[]{:S(2)}) collective-permute-start(bf16[192,256]{1,0:T(8,128)(2,1)} %get-tuple-element.116.refs_2_), channel_id=1, source_target_pairs={{0,2},{1,3},{2,0},{3,1},{4,6},{5,7},{6,4},{7,5},{8,10},{9,11},{10,... | collective-permute-start | bytes 294920 | tf_op jit(solution)/shard_map/ppermute | solution.py:726
  79.7 14.0 %collective-permute-start.14 = (bf16[192,256]{1,0:T(8,128)(2,1)}, bf16[192,256]{1,0:T(8,128)(2,1)S(1)}, u32[]{:S(2)}, u32[]{:S(2)}) collective-permute-start(bf16[192,256]{1,0:T(8,128)(2,1)} %get-tuple-element.118.refs_3_), channel_id=1, source_target_pairs={{0,3},{1,2},{2,1},{3,0},{4,7},{5,6},{6,5},{7,4},{8,11},{9,10},{10,... | collective-permute-start | bytes 294920 | tf_op jit(solution)/shard_map/ppermute | solution.py:726
  122.0 132.0 %reduce-scatter.2.cloned.1.call-start = ((), (), s32[]{:S(2)}) async-start(), calls=%async_computation.2 | async-start | bytes 6635520 | tf_op jit(solution)/shard_map/reduce_scatter | solution.py:1047
  124.2 14.3 %collective-permute-start.26 = (bf16[192,256]{1,0:T(8,128)(2,1)}, bf16[192,256]{1,0:T(8,128)(2,1)S(1)}, u32[]{:S(2)}, u32[]{:S(2)}) collective-permute-start(bf16[192,256]{1,0:T(8,128)(2,1)} %get-tuple-element.133), channel_id=1, source_target_pairs={{0,2},{1,3},{2,0},{3,1},{4,6},{5,7},{6,4},{7,5},{8,10},{9,11},{10,... | collective-permute-start | bytes 294920 | tf_op jit(solution)/shard_map/ppermute | solution.py:726
  159.5 26.1 %collective-permute-start.30 = (bf16[384,1024]{1,0:T(8,128)(2,1)S(1)}, bf16[384,1024]{1,0:T(8,128)(2,1)S(1)}, u32[]{:S(2)}, u32[]{:S(2)}) collective-permute-start(bf16[384,1024]{1,0:T(8,128)(2,1)S(1)} %add_convert_fusion), channel_id=1, source_target_pairs={{8,0},{9,1},{10,2},{11,3},{12,4},{13,5},{14,6},{15,7},{24,16},{25,... | collective-permute-start | bytes 2359304 | tf_op jit(solution)/shard_map/ppermute | solution.py:953
  193.0 16.7 %collective-permute-start.31 = (bf16[256,768]{1,0:T(8,128)(2,1)S(1)}, bf16[256,768]{1,0:T(8,128)(2,1)S(1)}, u32[]{:S(2)}, u32[]{:S(2)}) collective-permute-start(bf16[256,768]{1,0:T(8,128)(2,1)S(1)} %copy-done.32), channel_id=1, source_target_pairs={{0,1},{1,0},{2,3},{3,2},{4,5},{5,4},{6,7},{7,6},{8,9},{9,8},{10,11... | collective-permute-start | bytes 1179656 | tf_op jit(solution)/shard_map/ppermute | solution.py:726
  209.6 13.5 %collective-permute-start.32 = (bf16[256,768]{1,0:T(8,128)(2,1)S(1)}, bf16[256,768]{1,0:T(8,128)(2,1)S(1)}, u32[]{:S(2)}, u32[]{:S(2)}) collective-permute-start(bf16[256,768]{1,0:T(8,128)(2,1)S(1)} %copy-done.31), channel_id=1, source_target_pairs={{0,1},{1,0},{2,3},{3,2},{4,5},{5,4},{6,7},{7,6},{8,9},{9,8},{10,11... | collective-permute-start | bytes 1179656 | tf_op jit(solution)/shard_map/ppermute | solution.py:726
  213.3 19.4 %collective-permute-start.33 = (bf16[256,768]{1,0:T(8,128)(2,1)}, bf16[256,768]{1,0:T(8,128)(2,1)S(1)}, u32[]{:S(2)}, u32[]{:S(2)}) collective-permute-start(bf16[256,768]{1,0:T(8,128)(2,1)} %shard_map.270), channel_id=1, source_target_pairs={{0,2},{1,3},{2,0},{3,1},{4,6},{5,7},{6,4},{7,5},{8,10},{9,11},{10,... | collective-permute-start | bytes 1179656 | tf_op jit(solution)/shard_map/ppermute | solution.py:726
  236.1 17.0 %collective-permute-start.36 = (bf16[256,768]{1,0:T(8,128)(2,1)}, bf16[256,768]{1,0:T(8,128)(2,1)S(1)}, u32[]{:S(2)}, u32[]{:S(2)}) collective-permute-start(bf16[256,768]{1,0:T(8,128)(2,1)} %shard_map.272.refs_0_), channel_id=1, source_target_pairs={{0,2},{1,3},{2,0},{3,1},{4,6},{5,7},{6,4},{7,5},{8,10},{9,11},{10,... | collective-permute-start | bytes 1179656 | tf_op jit(solution)/shard_map/ppermute | solution.py:726
  236.1 17.9 %collective-permute-start.35 = (bf16[256,768]{1,0:T(8,128)(2,1)}, bf16[256,768]{1,0:T(8,128)(2,1)S(1)}, u32[]{:S(2)}, u32[]{:S(2)}) collective-permute-start(bf16[256,768]{1,0:T(8,128)(2,1)} %shard_map.272.refs_0_), channel_id=1, source_target_pairs={{0,1},{1,0},{2,3},{3,2},{4,5},{5,4},{6,7},{7,6},{8,9},{9,8},{10,11... | collective-permute-start | bytes 1179656 | tf_op jit(solution)/shard_map/ppermute | solution.py:726
  255.7 32.7 %collective-permute-start.37 = (bf16[256,768]{1,0:T(8,128)(2,1)S(1)}, bf16[256,768]{1,0:T(8,128)(2,1)S(1)}, u32[]{:S(2)}, u32[]{:S(2)}) collective-permute-start(bf16[256,768]{1,0:T(8,128)(2,1)S(1)} %collective-permute-done.36.refs_2_), channel_id=1, source_target_pairs={{0,1},{1,0},{2,3},{3,2},{4,5},{5,4},{6,7},{7,6},{8,9},{9,8},{10,11... | collective-permute-start | bytes 1179656 | tf_op jit(solution)/shard_map/ppermute | solution.py:726
  257.4 29.6 %collective-permute-start.47 = (bf16[432,384]{1,0:T(8,128)(2,1)S(1)}, bf16[432,384]{1,0:T(8,128)(2,1)S(1)}, u32[]{:S(2)}, u32[]{:S(2)}) collective-permute-start(bf16[432,384]{1,0:T(8,128)(2,1)S(1)} %get-tuple-element.180), channel_id=1, source_target_pairs={{0,1},{1,0},{2,3},{3,2},{4,5},{5,4},{6,7},{7,6},{8,9},{9,8},{10,11... | collective-permute-start | bytes 995336 | tf_op jit(solution)/shard_map/ppermute | solution.py:726
  267.1 19.8 %collective-permute-start.49 = (bf16[432,384]{1,0:T(8,128)(2,1)S(1)}, bf16[432,384]{1,0:T(8,128)(2,1)S(1)}, u32[]{:S(2)}, u32[]{:S(2)}) collective-permute-start(bf16[432,384]{1,0:T(8,128)(2,1)S(1)} %add_convert_fusion.3), channel_id=1, source_target_pairs={{0,2},{1,3},{2,0},{3,1},{4,6},{5,7},{6,4},{7,5},{8,10},{9,11},{10,... | collective-permute-start | bytes 995336 | tf_op jit(solution)/shard_map/ppermute | solution.py:726
  267.8 20.3 %collective-permute-start.39 = (bf16[304,384]{1,0:T(8,128)(2,1)S(1)}, bf16[304,384]{1,0:T(8,128)(2,1)S(1)}, u32[]{:S(2)}, u32[]{:S(2)}) collective-permute-start(bf16[304,384]{1,0:T(8,128)(2,1)S(1)} %slice_bitcast_fusion.2), channel_id=1, source_target_pairs={{0,16},{16,0},{1,17},{17,1},{2,18},{18,2},{3,19},{19,3},{4,20},{20... | collective-permute-start | bytes 700424 | tf_op jit(solution)/shard_map/ppermute | solution.py:726
  (88 other events, 687.0 us)
Sparse Core Ops, SparseCore 0:
  11.3 83.8 all-gather.3
  122.1 41.3 all-gather.5
  185.7 65.8 reduce-scatter.1

commit v4 on v3

--- a/solution.py
+++ b/solution.py
@@ -36,6 +36,10 @@
         cost_estimate=cost,
         compiler_params=pltpu.CompilerParams(vmem_limit_bytes=LIMIT),
     )
+
+
+def gathered_rows(n):
+    return n // 3
 
 
 def sds(shape, dtype):
@@ -106,14 +110,15 @@
     low = small[...].astype(BF)
     wtc[:part, :] = wt[pl.ds(mult(c, part), part), :]
     wtc[part:, :] = low
-    hs = hb // 2
+    hs = wc.shape[0] - half
+    ht = hb - hs
     y = sc[Y]
     wc[:half, :] = e_ref[:, pl.ds(mult(c, hb), hb)]
     wc[half:, :] = s_ref[pl.ds(mult(c, hb), hs), :]
     at = 0
     for ref, start, n in (
         (m_ref, (c * 2 + y) * (hw // 2), hw // 2),
-        (s_ref, c * hb + hs + y * (hs // 2), hs // 2),
+        (s_ref, c * hb + hs + y * (ht // 2), ht // 2),
     ):
         tq[at : at + n, :] = ref[pl.ds(pl.multiple_of(start, 16), n), :]
         at += n
@@ -148,21 +153,6 @@
                 (par, cbuf.at[:, there]),
             ]
         )
-
-
-def prompt_pass(sc, h, index, start, tile):
-    first = jnp.where(start >= B, 1, 0)
-    last = jnp.where(start + tile // 2 >= B, 1, 0)
-    mixed = jnp.where(first != last, 1, 0)
-    blk = jnp.where(index == 0, first, last)
-    paired = sc[PAIR + 2 * h + blk]
-    lane = lax.broadcasted_iota(jnp.int32, (1, tile), 1)
-    wanted = jnp.where(lane >= tile // 2, last, first)
-    mine = jnp.where(wanted == blk, 1, 0)
-    low = mine * (paired * B)
-    high = mine * (B + paired * (P_SIZE - B))
-    key_start = pl.multiple_of(paired * (P_SIZE - B), 128)
-    return mixed, key_start, low, high
 
 
 def window_start(sc, t, rows, tile):
@@ -197,6 +187,11 @@
     acc[h_rows, cols] = acc[h_rows, cols] * alpha[0:1] + dot(src[v_rows, place], e.astype(BF))
 
 
+def whole_block(paired):
+    at = pl.multiple_of(paired * (P_SIZE - B), 128)
+    return at, (paired * B, B + paired * (P_SIZE - B))
+
+
 def attend_prompt(sc, src, state, q_h, h, blk, ok, cols):
     paired = sc[PAIR + 2 * h + blk]
     start = paired * B
@@ -245,8 +240,9 @@
 
         @pl.when(sc[CTX] == 1)
         def _():
-            early = lax.broadcasted_iota(jnp.int32, (8, tile), 1) < B - rows
-            attend_prompt(sc, buf, state, q_ref[h_rows, :tile], h, 0, early, slice(0, tile))
+            early = B - rows
+            at, masks = whole_block(sc[PAIR + 2 * h])
+            attend(buf, state, q_ref[h_rows, :early], h, at, B, None, masks, slice(0, early))
 
         def window(t, _):
             cols = pl.ds(mult(t, tile), tile)
@@ -388,8 +384,20 @@
 
         @pl.when(split == 1)
         def _():
-            both = pair_up(q_ref[h_rows, :tile], g_s[h_rows, :tile])
-            prompt(0, both, jnp.where(first, lse, FAR)[:, :tile], delta[:, :tile], tile)
+            both = pair_up(q_ref[h_rows, :early], g_s[h_rows, :early])
+            at, masks = whole_block(sc[PAIR + 2 * h])
+            dq_s[:, :early] += chunk(
+                pbuf,
+                p_rows,
+                acc_p,
+                pl.ds(at, B),
+                at,
+                masks,
+                both,
+                lse[:, :early],
+                delta[:, :early],
+                h,
+            )
 
         def window(t, _):
             cols = pl.ds(mult(t, tile), tile)
@@ -476,9 +484,10 @@
     hb = block // 2
     hw = wide // 2
     c = sc[C]
-    hs = hb // 2
+    hs = gathered_rows(hb)
+    ht = hb - hs
     n_pack = half + hs
-    n_other = hw // 2 + hs // 2 + 16
+    n_other = hw // 2 + ht // 2 + 16
 
     stages = [[], [], []]
     small = []
@@ -497,13 +506,13 @@
                 at = j * n_other
                 rows = pl.multiple_of(z * wide + cc * hw + yy * (hw // 2), hw // 2)
                 move(0, piece.at[pl.ds(at, hw // 2), :], wc.at[pl.ds(rows, hw // 2), xc])
-                rows = z * block + cc * hb + hs + yy * (hs // 2)
-                rows = pl.ds(pl.multiple_of(rows, hs // 2), hs // 2)
-                move(2, piece.at[pl.ds(at + hw // 2, hs // 2), :], ws.at[rows, xc])
+                rows = z * block + cc * hb + hs + yy * (ht // 2)
+                rows = pl.ds(pl.multiple_of(rows, 16), ht // 2)
+                move(2, piece.at[pl.ds(at + hw // 2, ht // 2), :], ws.at[rows, xc])
             n = 2 * k + j
             small.append(
                 pltpu.make_async_copy(
-                    others[k].at[pl.ds(at + hw // 2 + hs // 2, 16), :], pk_s.at[n], psems.at[n]
+                    others[k].at[pl.ds(at + hw // 2 + ht // 2, 16), :], pk_s.at[n], psems.at[n]
                 )
             )
     for xh in range(2):
@@ -514,7 +523,7 @@
                 cc = c ^ i
                 place = pl.ds(pl.multiple_of(z * block + cc * hb, hb), hb)
                 move(1, packs[i].at[pl.ds(at, half), :], we.at[xc, place])
-                place = pl.ds(pl.multiple_of(z * block + cc * hb, hs), hs)
+                place = pl.ds(pl.multiple_of(z * block + cc * hb, 16), hs)
                 move(2, packs[i].at[pl.ds(at + half, hs), :], ws.at[place, xc])
     mine = pl.ds(mult(sc[Z], tile), tile)
     small.append(pltpu.make_async_copy(x_hbm.at[mine, :], x_ref, psems.at[8]))
@@ -669,10 +678,16 @@
     out_ref[...] = (total + c_ref[...].astype(F32) + gf_ref[...]).astype(BF)
 
 
-def gp_body(sc, dq_ref, kv_ref, x_ref, small_ref, out_ref, acc, line, parts):
+def gp_body(sc, dq_ref, kv_ref, x_ref, all_ref, out_ref, acc, line, parts, small_ref, sems):
     wide = dq_ref.shape[1]
     tile = dq_ref.shape[2]
     half = out_ref.shape[3]
+    copies = [
+        pltpu.make_async_copy(all_ref.at[k, pl.ds(tile, 16), :], small_ref.at[k], sems.at[k])
+        for k in range(4)
+    ]
+    for copy in copies:
+        copy.start()
     ones = jnp.ones((8, tile), BF)
     top = bot = s_top = s_bot = 0.0
     for k in range(4):
@@ -681,9 +696,11 @@
         bot = bot + dot(kv_ref[k], rows)
         s_top = s_top + dot_t(ones, dq_ref[k])
         s_bot = s_bot + dot_t(ones, kv_ref[k, wide:, :])
-        parts[k] = small_ref[k].astype(F32)
     acc[:wide, :] = top
     acc[wide:, :] = bot
+    for k in range(4):
+        copies[k].wait()
+        parts[k] = small_ref[k].astype(F32)
     parts[0] = ((parts[0] + parts[1]) + parts[2]) + parts[3]
     line[...] = jnp.zeros_like(line)
     line[0, 0:1, :wide] = s_top[0:1]
@@ -785,8 +802,8 @@
                 (
                     sds((16, half), F32),
                     sds((part + 16, half), BF),
-                    sds((half + hb // 2, half), BF),
-                    sds((hw // 2 + hb // 4 + 16, half), BF),
+                    sds((half + gathered_rows(hb), half), BF),
+                    sds((hw // 2 + (hb - gathered_rows(hb)) // 2 + 16, half), BF),
                 ),
                 ins=[SM] + [VM] * 12,
                 cost=cost(0, 8 * half * width),
@@ -958,8 +975,7 @@
             cost=cost(2 * rows * width * 3 * wide, 8 * rows * width),
         )(sc, after(d_own, gathered), got_par, from_y, dq, wt_full)
         kv_back, back = outs[0], outs[1:]
-        gathered = after(gathered, kv_back)
-        layer_out = gathered[:, :tile].reshape(rows, width)
+        layer_out = after(gathered, kv_back)[:, :tile].reshape(rows, width)
         passed = pz[1](back[3])
         relay = call(pair_body, sds((tile, width), BF), ins=[VM] * 2)(back[2], passed)
         near = pz[1](after(back[1], passed))
@@ -967,14 +983,16 @@
         gp = call(
             gp_body,
             sds((2, 2, 3 * wide // 2 + 16, half), BF),
-            ins=[SM] + [VM] * 4,
+            ins=[SM] + [VM] * 3 + [ANY],
             scratch=[
                 pltpu.VMEM((3 * wide, width), F32),
                 pltpu.VMEM((2, 16, half), F32),
                 pltpu.VMEM((4, 16, width), F32),
+                pltpu.VMEM((4, 16, width), BF),
+                pltpu.SemaphoreType.DMA((4,)),
             ],
             cost=cost(2 * rows * width * 3 * wide, 4 * rows * width),
-        )(sc, dq, kv_back, x, after(gathered[:, tile:], layer_out))
+        )(sc, dq, kv_back, x, gathered)
 
         def add(a, b):
             return (a.astype(F32) + b.astype(F32)).astype(BF)
@@ -985,7 +1003,7 @@
             sds((tile, width), BF),
             ins=[VM] * 4,
             cost=cost(4 * tile * width, 12 * tile * width),
-        )(back[0], near, far, after(grad_first, gp_c))
+        )(back[0], near, far, after(grad_first, gp_c, layer_out))
         gp_c = after(gp_c, low_tokens)
         tiles_near = pz[1](low_tokens)
         tiles_far = pz[2](low_tokens)

time: 310 us -> 307 us (level)
    unnamed x113 -> x109, local copies, waits for them, and re-layouts: 11.1 us -> 13.4 us
  transfers between devices with their start and end apart: 56 -> 56, of which waited for: 26 -> 27; matrix products, arithmetic and copies ran while one was open for 4% -> 4% of each run, Pallas kernels for 20% -> 21%
where the time goes in v4:
time: 307 us; the launch traced here: 308 us
  waiting for transfers between devices  135 us (44%)
  Pallas kernels  86.3 us (28%)
  starting transfers between devices  45.9 us (15%)
  local copies, waits for them, and re-layouts  19.6 us (6%)
  between operations  14.4 us (5%)
  other arithmetic  6.35 us (2%)
    ppermute x51, waiting for transfers between devices, swap(): return lambda v: lax.ppermute(v, axis, [(i, i ^ k) for i in range(size)])  121 us
    ppermute x51, starting transfers between devices, swap(): return lambda v: lax.ppermute(v, axis, [(i, i ^ k) for i in range(size)])  40.5 us
    pallas_call x1, Pallas kernels, on_device(): call(mid_body, (sds((tile + 16, width), BF), *[sds((wide, tile), BF)] * 4...  17.1 us
    pallas_call x1, Pallas kernels, on_device(): call(bwd_body, (sds((4, wide, tile), BF), *[sds((2 * wide, rows), BF)] *...  16.8 us
    ppermute x1, waiting for transfers between devices, on_device(): from_y = lax.ppermute(prompt_part, 'cy', [(1, 0)])  14.1 us
    unnamed x109, local copies, waits for them, and re-layouts  13.4 us
    pallas_call x1, Pallas kernels, on_device(): call(fwd_near_body, tuple(state), ins=[SM, VM, VM] + [ANY] * 2, scratch=[...  12.9 us
    pallas_call x1, Pallas kernels, on_device(): call(wg_body, sds((2, 2, 4, n_part, half), BF), ins=[SM] + [VM] * 12, cos...  9.09 us
  transfers between devices with their start and end apart: 56, of which 27 were waited for; matrix products, arithmetic and copies ran while one was open for 4% of the time, Pallas kernels for 21%

profile of v4, /device:TPU:0, one launch (start us, length us, event | category | flops | bytes accessed | tf_op | source)
XLA Modules:
  0.0 307.7 jit_solution(4219556084863816531)
XLA Ops:
  14.4 6.7 %collective-permute-done.w0_ref = bf16[304,384]{1,0:T(8,128)(2,1)S(1)} collective-permute-done((bf16[304,384]{1,0:T(8,128)(2,1)}, bf16[304,384]{1,0:T(8,128)(2,1)S(1)}, u32[]{:S(2)}, u32[]{:S(2)}) %collective-permute-start) | collective-permute-done | bytes 233504 | tf_op jit(solution)/shard_map/ppermute | solution.py:743
  24.1 4.5 %shard_map.264 = (bf16[192,1024]{1,0:T(8,128)(2,1)}, bf16[384,1024]{1,0:T(8,128)(2,1)}, bf16[576,768]{1,0:T(8,128)(2,1)}) custom-call(s32[14]{0:T(128)} %concatenate.9.sc, bf16[1024,768]{1,0:T(8,128)(2,1)} %bitcast.41, bf16[576,384]{1,0:T(8,128)(2,1)} %bitcast.45, f32[16,384]{1,0:T(8,128)} %get-tuple-element.95.small_ref, bf16[304,384]{1,0:T(8,128)(2,1)} %copy-done.46, ...), custom_call_target="tpu_custom_call" | custom-call | flops 905969664 | bytes 3145728 | tf_op jit(solution)/shard_map/pallas_call | solution.py:841
  28.6 3.7 %collective-permute-start.3 = (bf16[384,1024]{1,0:T(8,128)(2,1)}, bf16[384,1024]{1,0:T(8,128)(2,1)S(1)}, u32[]{:S(2)}, u32[]{:S(2)}) collective-permute-start(bf16[384,1024]{1,0:T(8,128)(2,1)} %get-tuple-element.100.own), channel_id=1, source_target_pairs={{0,8},{1,9},{2,10},{3,11},{4,12},{5,13},{6,14},{7,15},{16,24},{17,... | collective-permute-start | bytes 2359304 | tf_op jit(solution)/shard_map/ppermute | solution.py:866
  40.1 12.9 %shard_map.265 = (f32[192,1024]{1,0:T(8,128)}, f32[24,1024]{1,0:T(8,128)}, f32[24,1024]{1,0:T(8,128)}) custom-call(s32[14]{0:T(128)} %concatenate.9.sc, bf16[192,1024]{1,0:T(8,128)(2,1)} %get-tuple-element.99.q_ref, s32[8,1024]{1,0:T(8,128)} %add_add_fusion.span_ref, bf16[384,1024]{1,0:T(8,128)(2,1)} %get-tuple-element.100.own, bf16[384,1024]{1,0:T(8,128)(2,1)} %copy-done.8), custom_call_target="tpu_custom_call" | custom-call | bytes 1000 | tf_op jit(solution)/shard_map/pallas_call | solution.py:874
  59.5 18.6 %collective-permute-done.11.refs_11_ = bf16[384,384]{1,0:T(8,128)(2,1)S(1)} collective-permute-done((bf16[384,384]{1,0:T(8,128)(2,1)S(1)}, bf16[384,384]{1,0:T(8,128)(2,1)S(1)}, u32[]{:S(2)}, u32[]{:S(2)}) %collective-permute-start.11) | collective-permute-done | bytes 294944 | tf_op jit(solution)/shard_map/ppermute | solution.py:743
  79.4 3.9 %collective-permute-start.13 = (bf16[192,256]{1,0:T(8,128)(2,1)}, bf16[192,256]{1,0:T(8,128)(2,1)S(1)}, u32[]{:S(2)}, u32[]{:S(2)}) collective-permute-start(bf16[192,256]{1,0:T(8,128)(2,1)} %get-tuple-element.115.refs_2_), channel_id=1, source_target_pairs={{0,2},{1,3},{2,0},{3,1},{4,6},{5,7},{6,4},{7,5},{8,10},{9,11},{10,... | collective-permute-start | bytes 294920 | tf_op jit(solution)/shard_map/ppermute | solution.py:743
  83.8 5.3 %collective-permute-done.12.refs_1_ = bf16[192,256]{1,0:T(8,128)(2,1)S(1)} collective-permute-done((bf16[192,256]{1,0:T(8,128)(2,1)}, bf16[192,256]{1,0:T(8,128)(2,1)S(1)}, u32[]{:S(2)}, u32[]{:S(2)}) %collective-permute-start.12) | collective-permute-done | bytes 98336 | tf_op jit(solution)/shard_map/ppermute | solution.py:743
  89.0 4.6 %collective-permute-done.14.refs_3_ = bf16[192,256]{1,0:T(8,128)(2,1)S(1)} collective-permute-done((bf16[192,256]{1,0:T(8,128)(2,1)}, bf16[192,256]{1,0:T(8,128)(2,1)S(1)}, u32[]{:S(2)}, u32[]{:S(2)}) %collective-permute-start.14) | collective-permute-done | bytes 98336 | tf_op jit(solution)/shard_map/ppermute | solution.py:743
  95.3 4.5 %collective-permute-done.17.refs_16_ = bf16[384,384]{1,0:T(8,128)(2,1)S(1)} collective-permute-done((bf16[384,384]{1,0:T(8,128)(2,1)S(1)}, bf16[384,384]{1,0:T(8,128)(2,1)S(1)}, u32[]{:S(2)}, u32[]{:S(2)}) %collective-permute-start.17) | collective-permute-done | bytes 294944 | tf_op jit(solution)/shard_map/ppermute | solution.py:743
  104.2 17.1 %shard_map.267 = (bf16[272,768]{1,0:T(8,128)(2,1)}, bf16[192,256]{1,0:T(8,128)(2,1)}, bf16[192,256]{1,0:T(8,128)(2,1)}, bf16[192,256]{1,0:T(8,128)(2,1)}, bf16[1...) custom-call(s32[14]{0:T(128)} %concatenate.9.sc, ...), custom_call_target="tpu_custom_call" | custom-call | flops 5435817984 | bytes 9437184 | tf_op jit(solution)/shard_map/pallas_call | solution.py:901
  127.9 10.1 %collective-permute-done.26.refs_7_ = bf16[192,256]{1,0:T(8,128)(2,1)S(1)} collective-permute-done((bf16[192,256]{1,0:T(8,128)(2,1)}, bf16[192,256]{1,0:T(8,128)(2,1)S(1)}, u32[]{:S(2)}, u32[]{:S(2)}) %collective-permute-start.26) | collective-permute-done | bytes 98336 | tf_op jit(solution)/shard_map/ppermute | solution.py:743
  138.7 16.8 %shard_map.268 = (bf16[4,192,256]{2,1,0:T(8,128)(2,1)}, bf16[384,1024]{1,0:T(8,128)(2,1)}, bf16[384,1024]{1,0:T(8,128)(2,1)}, bf16[384,1024]{1,0:T(8,128)(2,1)}, bf16[384,1024]{1,0:T(8,128)(2,1)}) custom-call(s32[14]{0:T(128)} %concatenate.9.sc, bf16[192,1024]{1,0:T(8,128)(2,1)} %get-tuple-element.99.q_ref, s32[8,1024]{1,0:T(8,128)} %add_add_fusion.span_ref, ...), custom_call_target="tpu_custom_call" | custom-call | flops 2264924160 | bytes 3145728 | tf_op jit(solution)/shard_map/pallas_call | solution.py:940
  164.6 9.1 %shard_map.275 = bf16[2,2,4,432,384]{4,3,2,1,0:T(8,128)(2,1)} custom-call(s32[14]{0:T(128)} %concatenate.9.sc, bf16[256,768]{1,0:T(8,128)(2,1)} %get-tuple-element.154.refs_0_, bf16[256,768]{1,0:T(8,128)(2,1)} %get-tuple-element.155.refs_1_, bf16[256,768]{1,0:T(8,128)(2,1)} %get-tuple-element.156.refs_2_, bf16[256,1536]{1,0:T(8,128)(2,1)} %get-tuple-element.157.refs_3_, ...), custom_call_target="tpu_custom_call" | custom-call | flops 2415919104 | bytes 9437184 | tf_op jit(solution)/shard_map/pallas_call | solution.py:964
  173.7 14.1 %collective-permute-done.30.c_ref = bf16[384,1024]{1,0:T(8,128)(2,1)S(1)} collective-permute-done((bf16[384,1024]{1,0:T(8,128)(2,1)S(1)}, bf16[384,1024]{1,0:T(8,128)(2,1)S(1)}, u32[]{:S(2)}, u32[]{:S(2)}) %collective-permute-start.30) | collective-permute-done | bytes 786464 | tf_op jit(solution)/shard_map/ppermute | solution.py:970
  188.7 4.4 %shard_map.269 = (bf16[4,384,256]{2,1,0:T(8,128)(2,1)}, bf16[256,768]{1,0:T(8,128)(2,1)}, bf16[256,768]{1,0:T(8,128)(2,1)}, bf16[256,768]{1,0:T(8,128)(2,1)}, bf16[256,768]{1,0:T(8,128)(2,1)}) custom-call(s32[14]{0:T(128)} %concatenate.9.sc, bf16[384,1024]{1,0:T(8,128)(2,1)} %get-tuple-element.135.a_ref, bf16[384,1024]{1,0:T(8,128)(2,1)} %copy-done.11, ...), custom_call_target="tpu_custom_call" | custom-call | flops 905969664 | bytes 6291456 | tf_op jit(solution)/shard_map/pallas_call | solution.py:971
  193.2 5.0 %collective-permute-start.31 = (bf16[256,768]{1,0:T(8,128)(2,1)}, bf16[256,768]{1,0:T(8,128)(2,1)S(1)}, u32[]{:S(2)}, u32[]{:S(2)}) collective-permute-start(bf16[256,768]{1,0:T(8,128)(2,1)} %get-tuple-element.145), channel_id=1, source_target_pairs={{0,1},{1,0},{2,3},{3,2},{4,5},{5,4},{6,7},{7,6},{8,9},{9,8},{10,11... | collective-permute-start | bytes 1179656 | tf_op jit(solution)/shard_map/ppermute | solution.py:743
  198.2 4.2 %shard_map.271 = bf16[2,2,304,384]{3,2,1,0:T(8,128)(2,1)} custom-call(s32[14]{0:T(128)} %concatenate.9.sc, bf16[4,192,256]{2,1,0:T(8,128)(2,1)} %get-tuple-element.139.dq_ref, bf16[4,384,256]{2,1,0:T(8,128)(2,1)} %get-tuple-element.141.kv_ref, bf16[1024,768]{1,0:T(8,128)(2,1)} %bitcast.43, bf16[4,272,768]{2,1,0:T(8,128)(2,1)} %bitcast.37), custom_call_target="tpu_custom_call" | custom-call | flops 905969664 | bytes 3145728 | tf_op jit(solution)/shard_map/pallas_call | solution.py:983
  203.6 3.8 %collective-permute-done.31.b_ref = bf16[256,768]{1,0:T(8,128)(2,1)S(1)} collective-permute-done((bf16[256,768]{1,0:T(8,128)(2,1)}, bf16[256,768]{1,0:T(8,128)(2,1)S(1)}, u32[]{:S(2)}, u32[]{:S(2)}) %collective-permute-start.31) | collective-permute-done | bytes 393248 | tf_op jit(solution)/shard_map/ppermute | solution.py:743
  212.8 6.7 %collective-permute-done.32.b_ref = bf16[256,768]{1,0:T(8,128)(2,1)S(1)} collective-permute-done((bf16[256,768]{1,0:T(8,128)(2,1)}, bf16[256,768]{1,0:T(8,128)(2,1)S(1)}, u32[]{:S(2)}, u32[]{:S(2)}) %collective-permute-start.32) | collective-permute-done | bytes 393248 | tf_op jit(solution)/shard_map/ppermute | solution.py:743
  219.5 15.2 %collective-permute-done.33.c_ref = bf16[256,768]{1,0:T(8,128)(2,1)S(1)} collective-permute-done((bf16[256,768]{1,0:T(8,128)(2,1)}, bf16[256,768]{1,0:T(8,128)(2,1)S(1)}, u32[]{:S(2)}, u32[]{:S(2)}) %collective-permute-start.33) | collective-permute-done | bytes 393248 | tf_op jit(solution)/shard_map/ppermute | solution.py:743
  237.8 10.9 %collective-permute-done.36.refs_2_ = bf16[256,768]{1,0:T(8,128)(2,1)S(1)} collective-permute-done((bf16[256,768]{1,0:T(8,128)(2,1)}, bf16[256,768]{1,0:T(8,128)(2,1)S(1)}, u32[]{:S(2)}, u32[]{:S(2)}) %collective-permute-start.36) | collective-permute-done | bytes 393248 | tf_op jit(solution)/shard_map/ppermute | solution.py:743
  257.9 6.2 %collective-permute-done.48 = bf16[432,384]{1,0:T(8,128)(2,1)S(1)} collective-permute-done((bf16[432,384]{1,0:T(8,128)(2,1)S(1)}, bf16[432,384]{1,0:T(8,128)(2,1)S(1)}, u32[]{:S(2)}, u32[]{:S(2)}) %collective-permute-start.48) | collective-permute-done | bytes 331808 | tf_op jit(solution)/shard_map/ppermute | solution.py:743
  268.8 16.4 %collective-permute-done.47 = bf16[432,384]{1,0:T(8,128)(2,1)S(1)} collective-permute-done((bf16[432,384]{1,0:T(8,128)(2,1)S(1)}, bf16[432,384]{1,0:T(8,128)(2,1)S(1)}, u32[]{:S(2)}, u32[]{:S(2)}) %collective-permute-start.47) | collective-permute-done | bytes 331808 | tf_op jit(solution)/shard_map/ppermute | solution.py:743
  288.6 3.2 %shard_map.273 = f32[1024,768]{1,0:T(8,128)} custom-call(s32[14]{0:T(128)} %concatenate.9.sc, bf16[256,768]{1,0:T(8,128)(2,1)} %shard_map.272.refs_0_, bf16[256,768]{1,0:T(8,128)(2,1)} %copy-done.19, bf16[256,768]{1,0:T(8,128)(2,1)} %copy-done.18, bf16[256,768]{1,0:T(8,128)(2,1)} %copy-done.20), custom_call_target="tpu_custom_call" | custom-call | flops 786432 | bytes 4718592 | tf_op jit(solution)/shard_map/pallas_call | solution.py:1011
  (237 shorter events, 85.7 us)
Async XLA Ops:
  7.2 86.5 %all-gather.4.cloned.1.call-start = ((), (), s32[]{:S(2)}) async-start(), calls=%async_computation.1 | async-start | bytes 3538944 | tf_op jit(solution)/shard_map/all_gather | solution.py:833
  11.2 177.5 %all-gather.6.cloned.1.call-start = ((), (), s32[]{:S(2)}) async-start(), calls=%async_computation.3 | async-start | bytes 2088960 | tf_op jit(solution)/shard_map/all_gather | solution.py:938
  28.6 24.3 %collective-permute-start.3 = (bf16[384,1024]{1,0:T(8,128)(2,1)}, bf16[384,1024]{1,0:T(8,128)(2,1)S(1)}, u32[]{:S(2)}, u32[]{:S(2)}) collective-permute-start(bf16[384,1024]{1,0:T(8,128)(2,1)} %get-tuple-element.100.own), channel_id=1, source_target_pairs={{0,8},{1,9},{2,10},{3,11},{4,12},{5,13},{6,14},{7,15},{16,24},{17,... | collective-permute-start | bytes 2359304 | tf_op jit(solution)/shard_map/ppermute | solution.py:866
  32.4 20.6 %collective-permute-start.6 = (bf16[384,384]{1,0:T(8,128)(2,1)S(1)}, bf16[384,384]{1,0:T(8,128)(2,1)S(1)}, u32[]{:S(2)}, u32[]{:S(2)}) collective-permute-start(bf16[384,384]{1,0:T(8,128)(2,1)S(1)} %constant_dynamic-update-slice_fusion.refs_8_), channel_id=1, source_target_pairs={{0,2},{1,3},{2,0},{3,1},{4,6},{5,7},{6,4},{7,5},{8,10},{9,11},{10,... | collective-permute-start | bytes 884744 | tf_op jit(solution)/shard_map/ppermute | solution.py:743
  35.0 17.9 %collective-permute-start.5 = (bf16[384,384]{1,0:T(8,128)(2,1)S(1)}, bf16[384,384]{1,0:T(8,128)(2,1)S(1)}, u32[]{:S(2)}, u32[]{:S(2)}) collective-permute-start(bf16[384,384]{1,0:T(8,128)(2,1)S(1)} %constant_dynamic-update-slice_fusion.refs_8_), channel_id=1, source_target_pairs={{0,1},{1,0},{2,3},{3,2},{4,5},{5,4},{6,7},{7,6},{8,9},{9,8},{10,11... | collective-permute-start | bytes 884744 | tf_op jit(solution)/shard_map/ppermute | solution.py:743
  53.1 25.0 %collective-permute-start.11 = (bf16[384,384]{1,0:T(8,128)(2,1)S(1)}, bf16[384,384]{1,0:T(8,128)(2,1)S(1)}, u32[]{:S(2)}, u32[]{:S(2)}) collective-permute-start(bf16[384,384]{1,0:T(8,128)(2,1)S(1)} %collective-permute-done.6.refs_10_), channel_id=1, source_target_pairs={{0,1},{1,0},{2,3},{3,2},{4,5},{5,4},{6,7},{7,6},{8,9},{9,8},{10,11... | collective-permute-start | bytes 884744 | tf_op jit(solution)/shard_map/ppermute | solution.py:743
  53.6 25.0 %collective-permute-start.8 = (bf16[384,384]{1,0:T(8,128)(2,1)S(1)}, bf16[384,384]{1,0:T(8,128)(2,1)S(1)}, u32[]{:S(2)}, u32[]{:S(2)}) collective-permute-start(bf16[384,384]{1,0:T(8,128)(2,1)S(1)} %constant_dynamic-update-slice_fusion.refs_8_), channel_id=1, source_target_pairs={{0,8},{8,0},{1,9},{9,1},{2,10},{10,2},{3,11},{11,3},{4,12},{12,4},... | collective-permute-start | bytes 884744 | tf_op jit(solution)/shard_map/ppermute | solution.py:743
  54.2 24.4 %collective-permute-start.9 = (bf16[384,384]{1,0:T(8,128)(2,1)S(1)}, bf16[384,384]{1,0:T(8,128)(2,1)S(1)}, u32[]{:S(2)}, u32[]{:S(2)}) collective-permute-start(bf16[384,384]{1,0:T(8,128)(2,1)S(1)} %collective-permute-done.5.refs_9_), channel_id=1, source_target_pairs={{0,8},{8,0},{1,9},{9,1},{2,10},{10,2},{3,11},{11,3},{4,12},{12,4},... | collective-permute-start | bytes 884744 | tf_op jit(solution)/shard_map/ppermute | solution.py:743
  55.6 23.0 %collective-permute-start.10 = (bf16[384,384]{1,0:T(8,128)(2,1)S(1)}, bf16[384,384]{1,0:T(8,128)(2,1)S(1)}, u32[]{:S(2)}, u32[]{:S(2)}) collective-permute-start(bf16[384,384]{1,0:T(8,128)(2,1)S(1)} %collective-permute-done.6.refs_10_), channel_id=1, source_target_pairs={{0,8},{8,0},{1,9},{9,1},{2,10},{10,2},{3,11},{11,3},{4,12},{12,4},... | collective-permute-start | bytes 884744 | tf_op jit(solution)/shard_map/ppermute | solution.py:743
  78.1 15.6 %collective-permute-start.15 = (bf16[384,384]{1,0:T(8,128)(2,1)S(1)}, bf16[384,384]{1,0:T(8,128)(2,1)S(1)}, u32[]{:S(2)}, u32[]{:S(2)}) collective-permute-start(bf16[384,384]{1,0:T(8,128)(2,1)S(1)} %collective-permute-done.11.refs_11_), channel_id=1, source_target_pairs={{0,8},{8,0},{1,9},{9,1},{2,10},{10,2},{3,11},{11,3},{4,12},{12,4},... | collective-permute-start | bytes 884744 | tf_op jit(solution)/shard_map/ppermute | solution.py:743
  121.3 130.7 %reduce-scatter.2.cloned.1.call-start = ((), (), s32[]{:S(2)}) async-start(), calls=%async_computation.2 | async-start | bytes 6635520 | tf_op jit(solution)/shard_map/reduce_scatter | solution.py:1065
  122.4 15.7 %collective-permute-start.26 = (bf16[192,256]{1,0:T(8,128)(2,1)}, bf16[192,256]{1,0:T(8,128)(2,1)S(1)}, u32[]{:S(2)}, u32[]{:S(2)}) collective-permute-start(bf16[192,256]{1,0:T(8,128)(2,1)} %get-tuple-element.132), channel_id=1, source_target_pairs={{0,2},{1,3},{2,0},{3,1},{4,6},{5,7},{6,4},{7,5},{8,10},{9,11},{10,... | collective-permute-start | bytes 294920 | tf_op jit(solution)/shard_map/ppermute | solution.py:743
  123.0 15.0 %collective-permute-start.27 = (bf16[192,256]{1,0:T(8,128)(2,1)}, bf16[192,256]{1,0:T(8,128)(2,1)S(1)}, u32[]{:S(2)}, u32[]{:S(2)}) collective-permute-start(bf16[192,256]{1,0:T(8,128)(2,1)} %get-tuple-element.133), channel_id=1, source_target_pairs={{0,3},{1,2},{2,1},{3,0},{4,7},{5,6},{6,5},{7,4},{8,11},{9,10},{10,... | collective-permute-start | bytes 294920 | tf_op jit(solution)/shard_map/ppermute | solution.py:743
  159.7 28.2 %collective-permute-start.30 = (bf16[384,1024]{1,0:T(8,128)(2,1)S(1)}, bf16[384,1024]{1,0:T(8,128)(2,1)S(1)}, u32[]{:S(2)}, u32[]{:S(2)}) collective-permute-start(bf16[384,1024]{1,0:T(8,128)(2,1)S(1)} %add_convert_fusion), channel_id=1, source_target_pairs={{8,0},{9,1},{10,2},{11,3},{12,4},{13,5},{14,6},{15,7},{24,16},{25,... | collective-permute-start | bytes 2359304 | tf_op jit(solution)/shard_map/ppermute | solution.py:970
  193.2 14.3 %collective-permute-start.31 = (bf16[256,768]{1,0:T(8,128)(2,1)}, bf16[256,768]{1,0:T(8,128)(2,1)S(1)}, u32[]{:S(2)}, u32[]{:S(2)}) collective-permute-start(bf16[256,768]{1,0:T(8,128)(2,1)} %get-tuple-element.145), channel_id=1, source_target_pairs={{0,1},{1,0},{2,3},{3,2},{4,5},{5,4},{6,7},{7,6},{8,9},{9,8},{10,11... | collective-permute-start | bytes 1179656 | tf_op jit(solution)/shard_map/ppermute | solution.py:743
  207.5 12.0 %collective-permute-start.32 = (bf16[256,768]{1,0:T(8,128)(2,1)}, bf16[256,768]{1,0:T(8,128)(2,1)S(1)}, u32[]{:S(2)}, u32[]{:S(2)}) collective-permute-start(bf16[256,768]{1,0:T(8,128)(2,1)} %get-tuple-element.146), channel_id=1, source_target_pairs={{0,1},{1,0},{2,3},{3,2},{4,5},{5,4},{6,7},{7,6},{8,9},{9,8},{10,11... | collective-permute-start | bytes 1179656 | tf_op jit(solution)/shard_map/ppermute | solution.py:743
  211.2 23.5 %collective-permute-start.33 = (bf16[256,768]{1,0:T(8,128)(2,1)}, bf16[256,768]{1,0:T(8,128)(2,1)S(1)}, u32[]{:S(2)}, u32[]{:S(2)}) collective-permute-start(bf16[256,768]{1,0:T(8,128)(2,1)} %shard_map.270), channel_id=1, source_target_pairs={{0,2},{1,3},{2,0},{3,1},{4,6},{5,7},{6,4},{7,5},{8,10},{9,11},{10,... | collective-permute-start | bytes 1179656 | tf_op jit(solution)/shard_map/ppermute | solution.py:743
  237.8 10.9 %collective-permute-start.36 = (bf16[256,768]{1,0:T(8,128)(2,1)}, bf16[256,768]{1,0:T(8,128)(2,1)S(1)}, u32[]{:S(2)}, u32[]{:S(2)}) collective-permute-start(bf16[256,768]{1,0:T(8,128)(2,1)} %shard_map.272.refs_0_), channel_id=1, source_target_pairs={{0,2},{1,3},{2,0},{3,1},{4,6},{5,7},{6,4},{7,5},{8,10},{9,11},{10,... | collective-permute-start | bytes 1179656 | tf_op jit(solution)/shard_map/ppermute | solution.py:743
  237.8 14.1 %collective-permute-start.35 = (bf16[256,768]{1,0:T(8,128)(2,1)}, bf16[256,768]{1,0:T(8,128)(2,1)S(1)}, u32[]{:S(2)}, u32[]{:S(2)}) collective-permute-start(bf16[256,768]{1,0:T(8,128)(2,1)} %shard_map.272.refs_0_), channel_id=1, source_target_pairs={{0,1},{1,0},{2,3},{3,2},{4,5},{5,4},{6,7},{7,6},{8,9},{9,8},{10,11... | collective-permute-start | bytes 1179656 | tf_op jit(solution)/shard_map/ppermute | solution.py:743
  254.5 12.7 %collective-permute-start.38 = (bf16[2,304,384]{2,1,0:T(8,128)(2,1)S(1)}, bf16[2,304,384]{2,1,0:T(8,128)(2,1)S(1)}, u32[]{:S(2)}, u32[]{:S(2)}) collective-permute-start(bf16[2,304,384]{2,1,0:T(8,128)(2,1)S(1)} %fusion), channel_id=1, source_target_pairs={{0,8},{8,0},{1,9},{9,1},{2,10},{10,2},{3,11},{11,3},{4,12},{12,4},... | collective-permute-start | bytes 1400840 | tf_op jit(solution)/shard_map/ppermute | solution.py:743
  255.8 32.0 %collective-permute-start.37 = (bf16[256,768]{1,0:T(8,128)(2,1)S(1)}, bf16[256,768]{1,0:T(8,128)(2,1)S(1)}, u32[]{:S(2)}, u32[]{:S(2)}) collective-permute-start(bf16[256,768]{1,0:T(8,128)(2,1)S(1)} %collective-permute-done.36.refs_2_), channel_id=1, source_target_pairs={{0,1},{1,0},{2,3},{3,2},{4,5},{5,4},{6,7},{7,6},{8,9},{9,8},{10,11... | collective-permute-start | bytes 1179656 | tf_op jit(solution)/shard_map/ppermute | solution.py:743
  256.4 28.8 %collective-permute-start.47 = (bf16[432,384]{1,0:T(8,128)(2,1)S(1)}, bf16[432,384]{1,0:T(8,128)(2,1)S(1)}, u32[]{:S(2)}, u32[]{:S(2)}) collective-permute-start(bf16[432,384]{1,0:T(8,128)(2,1)S(1)} %get-tuple-element.178), channel_id=1, source_target_pairs={{0,1},{1,0},{2,3},{3,2},{4,5},{5,4},{6,7},{7,6},{8,9},{9,8},{10,11... | collective-permute-start | bytes 995336 | tf_op jit(solution)/shard_map/ppermute | solution.py:743
  265.1 20.1 %collective-permute-start.49 = (bf16[432,384]{1,0:T(8,128)(2,1)S(1)}, bf16[432,384]{1,0:T(8,128)(2,1)S(1)}, u32[]{:S(2)}, u32[]{:S(2)}) collective-permute-start(bf16[432,384]{1,0:T(8,128)(2,1)S(1)} %add_convert_fusion.3), channel_id=1, source_target_pairs={{0,2},{1,3},{2,0},{3,1},{4,6},{5,7},{6,4},{7,5},{8,10},{9,11},{10,... | collective-permute-start | bytes 995336 | tf_op jit(solution)/shard_map/ppermute | solution.py:743
  267.4 20.3 %collective-permute-start.39 = (bf16[304,384]{1,0:T(8,128)(2,1)S(1)}, bf16[304,384]{1,0:T(8,128)(2,1)S(1)}, u32[]{:S(2)}, u32[]{:S(2)}) collective-permute-start(bf16[304,384]{1,0:T(8,128)(2,1)S(1)} %slice_bitcast_fusion.2), channel_id=1, source_target_pairs={{0,16},{16,0},{1,17},{17,1},{2,18},{18,2},{3,19},{19,3},{4,20},{20... | collective-permute-start | bytes 700424 | tf_op jit(solution)/shard_map/ppermute | solution.py:743
  (86 other events, 647.3 us)
Sparse Core Ops, SparseCore 0:
  11.3 78.7 all-gather.3
  121.4 40.2 all-gather.5
  188.0 63.7 reduce-scatter.1

commit v5 on v4

--- a/solution.py
+++ b/solution.py
@@ -489,7 +489,7 @@
     n_pack = half + hs
     n_other = hw // 2 + ht // 2 + 16
 
-    stages = [[], [], []]
+    stages = [[], [], [], []]
     small = []
 
     def move(stage, src, dst):
@@ -515,16 +515,17 @@
                     others[k].at[pl.ds(at + hw // 2 + ht // 2, 16), :], pk_s.at[n], psems.at[n]
                 )
             )
-    for xh in range(2):
-        xc = pl.ds(xh * half, half)
-        for z in range(4):
-            at = (xh * 4 + z) * n_pack
+    for k in range(4):
+        z = sc[Z] ^ k
+        for xh in range(2):
+            xc = pl.ds(xh * half, half)
+            at = pl.multiple_of((xh * 4 + z) * n_pack, 16)
             for i in range(2):
                 cc = c ^ i
                 place = pl.ds(pl.multiple_of(z * block + cc * hb, hb), hb)
                 move(1, packs[i].at[pl.ds(at, half), :], we.at[xc, place])
                 place = pl.ds(pl.multiple_of(z * block + cc * hb, 16), hs)
-                move(2, packs[i].at[pl.ds(at + half, hs), :], ws.at[place, xc])
+                move(3, packs[i].at[pl.ds(at + half, hs), :], ws.at[place, xc])
     mine = pl.ds(mult(sc[Z], tile), tile)
     small.append(pltpu.make_async_copy(x_hbm.at[mine, :], x_ref, psems.at[8]))
     small.append(pltpu.make_async_copy(cot_hbm.at[mine, :], cot_ref, psems.at[9]))
@@ -558,13 +559,12 @@
     normed = n1 * scaling + shifting
     low = normed.astype(BF)
     nl_ref[...] = low
-    for copy in stages[1]:
-        copy.wait()
-    for copy in stages[2]:
-        copy.wait()
     feed = jnp.zeros((tile, width), F32)
-    for n in range(4):
-        cols = slice(n * block, (n + 1) * block)
+    for k in range(4):
+        for stage, n in ((1, 4), (3, 4), (2, 8)):
+            for copy in stages[stage][k * n : (k + 1) * n]:
+                copy.wait()
+        cols = pl.ds(mult(sc[Z] ^ k, block), block)
         inner = dot(low, we[:, cols]) + thr_s[6:7, cols]
         cdf = 0.5 * (1.0 + lax.erf(inner * (0.5**0.5)))
         pdf = jnp.exp(-0.5 * inner * inner) * (1.0 / math.sqrt(2.0 * math.pi))
@@ -924,7 +924,7 @@
                 pltpu.VMEM((tile, width), BF),
                 pltpu.VMEM((tile, width), BF),
                 pltpu.VMEM((16, width), F32),
-                pltpu.SemaphoreType.DMA((3, 48)),
+                pltpu.SemaphoreType.DMA((4, 32)),
                 pltpu.SemaphoreType.DMA((10,)),
             ],
             cost=cost(8 * tile * width * hidden + 4 * tile * width * width, 4 * width * hidden),

time: 307 us -> 308 us (level)
  starting transfers between devices: 45.9 us -> 56.2 us
  waiting for transfers between devices: 135 us -> 128 us
  Pallas kernels: 86.3 us -> 82.9 us
    ppermute x51, starting transfers between devices: 40.5 us -> 50.8 us  [swap(): return lambda v: lax.ppermute(v, axis, [(i, i ^ k) for i in range(size)])]
    ppermute x1, waiting for transfers between devices: 14.1 us -> 8.97 us  [on_device(): from_y = lax.ppermute(prompt_part, 'cy', [(1, 0)])]
  transfers between devices with their start and end apart: 56 -> 56, of which waited for: 27 -> 29; matrix products, arithmetic and copies ran while one was open for 4% -> 4% of each run, Pallas kernels for 21% -> 19%
where the time goes in v5:
time: 308 us; the launch traced here: 307 us
  waiting for transfers between devices  128 us (42%)
  Pallas kernels  82.9 us (27%)
  starting transfers between devices  56.2 us (18%)
  local copies, waits for them, and re-layouts  19.2 us (6%)
  between operations  14.4 us (5%)
  other arithmetic  6.35 us (2%)
    ppermute x51, waiting for transfers between devices, swap(): return lambda v: lax.ppermute(v, axis, [(i, i ^ k) for i in range(size)])  118 us
    ppermute x51, starting transfers between devices, swap(): return lambda v: lax.ppermute(v, axis, [(i, i ^ k) for i in range(size)])  50.8 us
    pallas_call x1, Pallas kernels, on_device(): call(mid_body, (sds((tile + 16, width), BF), *[sds((wide, tile), BF)] * 4...  17.9 us
    pallas_call x1, Pallas kernels, on_device(): call(bwd_body, (sds((4, wide, tile), BF), *[sds((2 * wide, rows), BF)] *...  14.6 us
    unnamed x109, local copies, waits for them, and re-layouts  13 us
    pallas_call x1, Pallas kernels, on_device(): call(fwd_near_body, tuple(state), ins=[SM, VM, VM] + [ANY] * 2, scratch=[...  10.9 us
    pallas_call x1, Pallas kernels, on_device(): call(wg_body, sds((2, 2, 4, n_part, half), BF), ins=[SM] + [VM] * 12, cos...  9.09 us
    ppermute x1, waiting for transfers between devices, on_device(): from_y = lax.ppermute(prompt_part, 'cy', [(1, 0)])  8.97 us
  transfers between devices with their start and end apart: 56, of which 29 were waited for; matrix products, arithmetic and copies ran while one was open for 4% of the time, Pallas kernels for 19%

profile of v5, /device:TPU:0, one launch (start us, length us, event | category | flops | bytes accessed | tf_op | source)
XLA Modules:
  0.0 306.6 jit_solution(13192941938967205637)
XLA Ops:
  14.4 6.7 %collective-permute-done.w0_ref = bf16[304,384]{1,0:T(8,128)(2,1)S(1)} collective-permute-done((bf16[304,384]{1,0:T(8,128)(2,1)}, bf16[304,384]{1,0:T(8,128)(2,1)S(1)}, u32[]{:S(2)}, u32[]{:S(2)}) %collective-permute-start) | collective-permute-done | bytes 233504 | tf_op jit(solution)/shard_map/ppermute | solution.py:743
  24.1 4.5 %shard_map.264 = (bf16[192,1024]{1,0:T(8,128)(2,1)}, bf16[384,1024]{1,0:T(8,128)(2,1)}, bf16[576,768]{1,0:T(8,128)(2,1)}) custom-call(s32[14]{0:T(128)} %concatenate.9.sc, bf16[1024,768]{1,0:T(8,128)(2,1)} %bitcast.41, bf16[576,384]{1,0:T(8,128)(2,1)} %bitcast.45, f32[16,384]{1,0:T(8,128)} %get-tuple-element.95.small_ref, bf16[304,384]{1,0:T(8,128)(2,1)} %copy-done.46, ...), custom_call_target="tpu_custom_call" | custom-call | flops 905969664 | bytes 3145728 | tf_op jit(solution)/shard_map/pallas_call | solution.py:841
  28.6 3.7 %collective-permute-start.3 = (bf16[384,1024]{1,0:T(8,128)(2,1)}, bf16[384,1024]{1,0:T(8,128)(2,1)S(1)}, u32[]{:S(2)}, u32[]{:S(2)}) collective-permute-start(bf16[384,1024]{1,0:T(8,128)(2,1)} %get-tuple-element.100.own), channel_id=1, source_target_pairs={{0,8},{1,9},{2,10},{3,11},{4,12},{5,13},{6,14},{7,15},{16,24},{17,... | collective-permute-start | bytes 2359304 | tf_op jit(solution)/shard_map/ppermute | solution.py:866
  40.1 10.9 %shard_map.265 = (f32[192,1024]{1,0:T(8,128)}, f32[24,1024]{1,0:T(8,128)}, f32[24,1024]{1,0:T(8,128)}) custom-call(s32[14]{0:T(128)} %concatenate.9.sc, bf16[192,1024]{1,0:T(8,128)(2,1)} %get-tuple-element.99.q_ref, s32[8,1024]{1,0:T(8,128)} %add_add_fusion.span_ref, bf16[384,1024]{1,0:T(8,128)(2,1)} %get-tuple-element.100.own, bf16[384,1024]{1,0:T(8,128)(2,1)} %copy-done.8), custom_call_target="tpu_custom_call" | custom-call | bytes 1000 | tf_op jit(solution)/shard_map/pallas_call | solution.py:874
  59.8 19.3 %collective-permute-done.11.refs_11_ = bf16[384,384]{1,0:T(8,128)(2,1)S(1)} collective-permute-done((bf16[384,384]{1,0:T(8,128)(2,1)S(1)}, bf16[384,384]{1,0:T(8,128)(2,1)S(1)}, u32[]{:S(2)}, u32[]{:S(2)}) %collective-permute-start.11) | collective-permute-done | bytes 294944 | tf_op jit(solution)/shard_map/ppermute | solution.py:743
  80.0 3.3 %collective-permute-start.13 = (bf16[192,256]{1,0:T(8,128)(2,1)}, bf16[192,256]{1,0:T(8,128)(2,1)S(1)}, u32[]{:S(2)}, u32[]{:S(2)}) collective-permute-start(bf16[192,256]{1,0:T(8,128)(2,1)} %get-tuple-element.115.refs_2_), channel_id=1, source_target_pairs={{0,2},{1,3},{2,0},{3,1},{4,6},{5,7},{6,4},{7,5},{8,10},{9,11},{10,... | collective-permute-start | bytes 294920 | tf_op jit(solution)/shard_map/ppermute | solution.py:743
  84.4 5.1 %collective-permute-done.12.refs_1_ = bf16[192,256]{1,0:T(8,128)(2,1)S(1)} collective-permute-done((bf16[192,256]{1,0:T(8,128)(2,1)}, bf16[192,256]{1,0:T(8,128)(2,1)S(1)}, u32[]{:S(2)}, u32[]{:S(2)}) %collective-permute-start.12) | collective-permute-done | bytes 98336 | tf_op jit(solution)/shard_map/ppermute | solution.py:743
  89.5 4.3 %collective-permute-done.14.refs_3_ = bf16[192,256]{1,0:T(8,128)(2,1)S(1)} collective-permute-done((bf16[192,256]{1,0:T(8,128)(2,1)}, bf16[192,256]{1,0:T(8,128)(2,1)S(1)}, u32[]{:S(2)}, u32[]{:S(2)}) %collective-permute-start.14) | collective-permute-done | bytes 98336 | tf_op jit(solution)/shard_map/ppermute | solution.py:743
  95.4 4.5 %collective-permute-done.17.refs_16_ = bf16[384,384]{1,0:T(8,128)(2,1)S(1)} collective-permute-done((bf16[384,384]{1,0:T(8,128)(2,1)S(1)}, bf16[384,384]{1,0:T(8,128)(2,1)S(1)}, u32[]{:S(2)}, u32[]{:S(2)}) %collective-permute-start.17) | collective-permute-done | bytes 294944 | tf_op jit(solution)/shard_map/ppermute | solution.py:743
  104.3 17.9 %shard_map.267 = (bf16[272,768]{1,0:T(8,128)(2,1)}, bf16[192,256]{1,0:T(8,128)(2,1)}, bf16[192,256]{1,0:T(8,128)(2,1)}, bf16[192,256]{1,0:T(8,128)(2,1)}, bf16[1...) custom-call(s32[14]{0:T(128)} %concatenate.9.sc, ...), custom_call_target="tpu_custom_call" | custom-call | flops 5435817984 | bytes 9437184 | tf_op jit(solution)/shard_map/pallas_call | solution.py:901
  128.8 10.6 %collective-permute-done.26.refs_7_ = bf16[192,256]{1,0:T(8,128)(2,1)S(1)} collective-permute-done((bf16[192,256]{1,0:T(8,128)(2,1)}, bf16[192,256]{1,0:T(8,128)(2,1)S(1)}, u32[]{:S(2)}, u32[]{:S(2)}) %collective-permute-start.26) | collective-permute-done | bytes 98336 | tf_op jit(solution)/shard_map/ppermute | solution.py:743
  140.1 14.6 %shard_map.268 = (bf16[4,192,256]{2,1,0:T(8,128)(2,1)}, bf16[384,1024]{1,0:T(8,128)(2,1)}, bf16[384,1024]{1,0:T(8,128)(2,1)}, bf16[384,1024]{1,0:T(8,128)(2,1)}, bf16[384,1024]{1,0:T(8,128)(2,1)}) custom-call(s32[14]{0:T(128)} %concatenate.9.sc, bf16[192,1024]{1,0:T(8,128)(2,1)} %get-tuple-element.99.q_ref, s32[8,1024]{1,0:T(8,128)} %add_add_fusion.span_ref, ...), custom_call_target="tpu_custom_call" | custom-call | flops 2264924160 | bytes 3145728 | tf_op jit(solution)/shard_map/pallas_call | solution.py:940
  163.8 9.1 %shard_map.275 = bf16[2,2,4,432,384]{4,3,2,1,0:T(8,128)(2,1)} custom-call(s32[14]{0:T(128)} %concatenate.9.sc, bf16[256,768]{1,0:T(8,128)(2,1)} %get-tuple-element.154.refs_0_, bf16[256,768]{1,0:T(8,128)(2,1)} %get-tuple-element.155.refs_1_, bf16[256,768]{1,0:T(8,128)(2,1)} %get-tuple-element.156.refs_2_, bf16[256,1536]{1,0:T(8,128)(2,1)} %get-tuple-element.157.refs_3_, ...), custom_call_target="tpu_custom_call" | custom-call | flops 2415919104 | bytes 9437184 | tf_op jit(solution)/shard_map/pallas_call | solution.py:964
  172.9 9.0 %collective-permute-done.30.c_ref = bf16[384,1024]{1,0:T(8,128)(2,1)S(1)} collective-permute-done((bf16[384,1024]{1,0:T(8,128)(2,1)S(1)}, bf16[384,1024]{1,0:T(8,128)(2,1)S(1)}, u32[]{:S(2)}, u32[]{:S(2)}) %collective-permute-start.30) | collective-permute-done | bytes 786464 | tf_op jit(solution)/shard_map/ppermute | solution.py:970
  182.8 4.4 %shard_map.269 = (bf16[4,384,256]{2,1,0:T(8,128)(2,1)}, bf16[256,768]{1,0:T(8,128)(2,1)}, bf16[256,768]{1,0:T(8,128)(2,1)}, bf16[256,768]{1,0:T(8,128)(2,1)}, bf16[256,768]{1,0:T(8,128)(2,1)}) custom-call(s32[14]{0:T(128)} %concatenate.9.sc, bf16[384,1024]{1,0:T(8,128)(2,1)} %get-tuple-element.135.a_ref, bf16[384,1024]{1,0:T(8,128)(2,1)} %copy-done.11, ...), custom_call_target="tpu_custom_call" | custom-call | flops 905969664 | bytes 6291456 | tf_op jit(solution)/shard_map/pallas_call | solution.py:971
  187.2 9.4 %collective-permute-start.31 = (bf16[256,768]{1,0:T(8,128)(2,1)}, bf16[256,768]{1,0:T(8,128)(2,1)S(1)}, u32[]{:S(2)}, u32[]{:S(2)}) collective-permute-start(bf16[256,768]{1,0:T(8,128)(2,1)} %get-tuple-element.145), channel_id=1, source_target_pairs={{0,1},{1,0},{2,3},{3,2},{4,5},{5,4},{6,7},{7,6},{8,9},{9,8},{10,11... | collective-permute-start | bytes 1179656 | tf_op jit(solution)/shard_map/ppermute | solution.py:743
  196.6 4.2 %shard_map.271 = bf16[2,2,304,384]{3,2,1,0:T(8,128)(2,1)} custom-call(s32[14]{0:T(128)} %concatenate.9.sc, bf16[4,192,256]{2,1,0:T(8,128)(2,1)} %get-tuple-element.139.dq_ref, bf16[4,384,256]{2,1,0:T(8,128)(2,1)} %get-tuple-element.141.kv_ref, bf16[1024,768]{1,0:T(8,128)(2,1)} %bitcast.43, bf16[4,272,768]{2,1,0:T(8,128)(2,1)} %bitcast.37), custom_call_target="tpu_custom_call" | custom-call | flops 905969664 | bytes 3145728 | tf_op jit(solution)/shard_map/pallas_call | solution.py:983
  202.1 3.8 %collective-permute-done.31.b_ref = bf16[256,768]{1,0:T(8,128)(2,1)S(1)} collective-permute-done((bf16[256,768]{1,0:T(8,128)(2,1)}, bf16[256,768]{1,0:T(8,128)(2,1)S(1)}, u32[]{:S(2)}, u32[]{:S(2)}) %collective-permute-start.31) | collective-permute-done | bytes 393248 | tf_op jit(solution)/shard_map/ppermute | solution.py:743
  212.3 10.1 %collective-permute-done.32.b_ref = bf16[256,768]{1,0:T(8,128)(2,1)S(1)} collective-permute-done((bf16[256,768]{1,0:T(8,128)(2,1)}, bf16[256,768]{1,0:T(8,128)(2,1)S(1)}, u32[]{:S(2)}, u32[]{:S(2)}) %collective-permute-start.32) | collective-permute-done | bytes 393248 | tf_op jit(solution)/shard_map/ppermute | solution.py:743
  222.4 6.6 %collective-permute-done.33.c_ref = bf16[256,768]{1,0:T(8,128)(2,1)S(1)} collective-permute-done((bf16[256,768]{1,0:T(8,128)(2,1)}, bf16[256,768]{1,0:T(8,128)(2,1)S(1)}, u32[]{:S(2)}, u32[]{:S(2)}) %collective-permute-start.33) | collective-permute-done | bytes 393248 | tf_op jit(solution)/shard_map/ppermute | solution.py:743
  234.8 15.5 %collective-permute-done.36.refs_2_ = bf16[256,768]{1,0:T(8,128)(2,1)S(1)} collective-permute-done((bf16[256,768]{1,0:T(8,128)(2,1)}, bf16[256,768]{1,0:T(8,128)(2,1)S(1)}, u32[]{:S(2)}, u32[]{:S(2)}) %collective-permute-start.36) | collective-permute-done | bytes 393248 | tf_op jit(solution)/shard_map/ppermute | solution.py:743
  256.8 5.8 %collective-permute-done.48 = bf16[432,384]{1,0:T(8,128)(2,1)S(1)} collective-permute-done((bf16[432,384]{1,0:T(8,128)(2,1)S(1)}, bf16[432,384]{1,0:T(8,128)(2,1)S(1)}, u32[]{:S(2)}, u32[]{:S(2)}) %collective-permute-start.48) | collective-permute-done | bytes 331808 | tf_op jit(solution)/shard_map/ppermute | solution.py:743
  267.7 16.4 %collective-permute-done.47 = bf16[432,384]{1,0:T(8,128)(2,1)S(1)} collective-permute-done((bf16[432,384]{1,0:T(8,128)(2,1)S(1)}, bf16[432,384]{1,0:T(8,128)(2,1)S(1)}, u32[]{:S(2)}, u32[]{:S(2)}) %collective-permute-start.47) | collective-permute-done | bytes 331808 | tf_op jit(solution)/shard_map/ppermute | solution.py:743
  287.5 3.2 %shard_map.273 = f32[1024,768]{1,0:T(8,128)} custom-call(s32[14]{0:T(128)} %concatenate.9.sc, bf16[256,768]{1,0:T(8,128)(2,1)} %shard_map.272.refs_0_, bf16[256,768]{1,0:T(8,128)(2,1)} %copy-done.19, bf16[256,768]{1,0:T(8,128)(2,1)} %copy-done.18, bf16[256,768]{1,0:T(8,128)(2,1)} %copy-done.20), custom_call_target="tpu_custom_call" | custom-call | flops 786432 | bytes 4718592 | tf_op jit(solution)/shard_map/pallas_call | solution.py:1011
  (237 shorter events, 89.3 us)
Async XLA Ops:
  7.2 86.6 %all-gather.4.cloned.1.call-start = ((), (), s32[]{:S(2)}) async-start(), calls=%async_computation.1 | async-start | bytes 3538944 | tf_op jit(solution)/shard_map/all_gather | solution.py:833
  11.2 171.6 %all-gather.6.cloned.1.call-start = ((), (), s32[]{:S(2)}) async-start(), calls=%async_computation.3 | async-start | bytes 2088960 | tf_op jit(solution)/shard_map/all_gather | solution.py:938
  28.6 22.3 %collective-permute-start.3 = (bf16[384,1024]{1,0:T(8,128)(2,1)}, bf16[384,1024]{1,0:T(8,128)(2,1)S(1)}, u32[]{:S(2)}, u32[]{:S(2)}) collective-permute-start(bf16[384,1024]{1,0:T(8,128)(2,1)} %get-tuple-element.100.own), channel_id=1, source_target_pairs={{0,8},{1,9},{2,10},{3,11},{4,12},{5,13},{6,14},{7,15},{16,24},{17,... | collective-permute-start | bytes 2359304 | tf_op jit(solution)/shard_map/ppermute | solution.py:866
  32.4 19.1 %collective-permute-start.6 = (bf16[384,384]{1,0:T(8,128)(2,1)S(1)}, bf16[384,384]{1,0:T(8,128)(2,1)S(1)}, u32[]{:S(2)}, u32[]{:S(2)}) collective-permute-start(bf16[384,384]{1,0:T(8,128)(2,1)S(1)} %constant_dynamic-update-slice_fusion.refs_8_), channel_id=1, source_target_pairs={{0,2},{1,3},{2,0},{3,1},{4,6},{5,7},{6,4},{7,5},{8,10},{9,11},{10,... | collective-permute-start | bytes 884744 | tf_op jit(solution)/shard_map/ppermute | solution.py:743
  35.0 16.4 %collective-permute-start.5 = (bf16[384,384]{1,0:T(8,128)(2,1)S(1)}, bf16[384,384]{1,0:T(8,128)(2,1)S(1)}, u32[]{:S(2)}, u32[]{:S(2)}) collective-permute-start(bf16[384,384]{1,0:T(8,128)(2,1)S(1)} %constant_dynamic-update-slice_fusion.refs_8_), channel_id=1, source_target_pairs={{0,1},{1,0},{2,3},{3,2},{4,5},{5,4},{6,7},{7,6},{8,9},{9,8},{10,11... | collective-permute-start | bytes 884744 | tf_op jit(solution)/shard_map/ppermute | solution.py:743
  54.4 24.7 %collective-permute-start.11 = (bf16[384,384]{1,0:T(8,128)(2,1)S(1)}, bf16[384,384]{1,0:T(8,128)(2,1)S(1)}, u32[]{:S(2)}, u32[]{:S(2)}) collective-permute-start(bf16[384,384]{1,0:T(8,128)(2,1)S(1)} %collective-permute-done.6.refs_10_), channel_id=1, source_target_pairs={{0,1},{1,0},{2,3},{3,2},{4,5},{5,4},{6,7},{7,6},{8,9},{9,8},{10,11... | collective-permute-start | bytes 884744 | tf_op jit(solution)/shard_map/ppermute | solution.py:743
  54.5 24.7 %collective-permute-start.8 = (bf16[384,384]{1,0:T(8,128)(2,1)S(1)}, bf16[384,384]{1,0:T(8,128)(2,1)S(1)}, u32[]{:S(2)}, u32[]{:S(2)}) collective-permute-start(bf16[384,384]{1,0:T(8,128)(2,1)S(1)} %constant_dynamic-update-slice_fusion.refs_8_), channel_id=1, source_target_pairs={{0,8},{8,0},{1,9},{9,1},{2,10},{10,2},{3,11},{11,3},{4,12},{12,4},... | collective-permute-start | bytes 884744 | tf_op jit(solution)/shard_map/ppermute | solution.py:743
  54.5 24.7 %collective-permute-start.9 = (bf16[384,384]{1,0:T(8,128)(2,1)S(1)}, bf16[384,384]{1,0:T(8,128)(2,1)S(1)}, u32[]{:S(2)}, u32[]{:S(2)}) collective-permute-start(bf16[384,384]{1,0:T(8,128)(2,1)S(1)} %collective-permute-done.5.refs_9_), channel_id=1, source_target_pairs={{0,8},{8,0},{1,9},{9,1},{2,10},{10,2},{3,11},{11,3},{4,12},{12,4},... | collective-permute-start | bytes 884744 | tf_op jit(solution)/shard_map/ppermute | solution.py:743
  56.5 22.7 %collective-permute-start.10 = (bf16[384,384]{1,0:T(8,128)(2,1)S(1)}, bf16[384,384]{1,0:T(8,128)(2,1)S(1)}, u32[]{:S(2)}, u32[]{:S(2)}) collective-permute-start(bf16[384,384]{1,0:T(8,128)(2,1)S(1)} %collective-permute-done.6.refs_10_), channel_id=1, source_target_pairs={{0,8},{8,0},{1,9},{9,1},{2,10},{10,2},{3,11},{11,3},{4,12},{12,4},... | collective-permute-start | bytes 884744 | tf_op jit(solution)/shard_map/ppermute | solution.py:743
  79.2 14.6 %collective-permute-start.15 = (bf16[384,384]{1,0:T(8,128)(2,1)S(1)}, bf16[384,384]{1,0:T(8,128)(2,1)S(1)}, u32[]{:S(2)}, u32[]{:S(2)}) collective-permute-start(bf16[384,384]{1,0:T(8,128)(2,1)S(1)} %collective-permute-done.11.refs_11_), channel_id=1, source_target_pairs={{0,8},{8,0},{1,9},{9,1},{2,10},{10,2},{3,11},{11,3},{4,12},{12,4},... | collective-permute-start | bytes 884744 | tf_op jit(solution)/shard_map/ppermute | solution.py:743
  122.2 128.5 %reduce-scatter.2.cloned.1.call-start = ((), (), s32[]{:S(2)}) async-start(), calls=%async_computation.2 | async-start | bytes 6635520 | tf_op jit(solution)/shard_map/reduce_scatter | solution.py:1065
  123.2 16.2 %collective-permute-start.26 = (bf16[192,256]{1,0:T(8,128)(2,1)}, bf16[192,256]{1,0:T(8,128)(2,1)S(1)}, u32[]{:S(2)}, u32[]{:S(2)}) collective-permute-start(bf16[192,256]{1,0:T(8,128)(2,1)} %get-tuple-element.132), channel_id=1, source_target_pairs={{0,2},{1,3},{2,0},{3,1},{4,6},{5,7},{6,4},{7,5},{8,10},{9,11},{10,... | collective-permute-start | bytes 294920 | tf_op jit(solution)/shard_map/ppermute | solution.py:743
  123.7 15.7 %collective-permute-start.27 = (bf16[192,256]{1,0:T(8,128)(2,1)}, bf16[192,256]{1,0:T(8,128)(2,1)S(1)}, u32[]{:S(2)}, u32[]{:S(2)}) collective-permute-start(bf16[192,256]{1,0:T(8,128)(2,1)} %get-tuple-element.133), channel_id=1, source_target_pairs={{0,3},{1,2},{2,1},{3,0},{4,7},{5,6},{6,5},{7,4},{8,11},{9,10},{10,... | collective-permute-start | bytes 294920 | tf_op jit(solution)/shard_map/ppermute | solution.py:743
  158.9 23.0 %collective-permute-start.30 = (bf16[384,1024]{1,0:T(8,128)(2,1)S(1)}, bf16[384,1024]{1,0:T(8,128)(2,1)S(1)}, u32[]{:S(2)}, u32[]{:S(2)}) collective-permute-start(bf16[384,1024]{1,0:T(8,128)(2,1)S(1)} %add_convert_fusion), channel_id=1, source_target_pairs={{8,0},{9,1},{10,2},{11,3},{12,4},{13,5},{14,6},{15,7},{24,16},{25,... | collective-permute-start | bytes 2359304 | tf_op jit(solution)/shard_map/ppermute | solution.py:970
  187.2 18.7 %collective-permute-start.31 = (bf16[256,768]{1,0:T(8,128)(2,1)}, bf16[256,768]{1,0:T(8,128)(2,1)S(1)}, u32[]{:S(2)}, u32[]{:S(2)}) collective-permute-start(bf16[256,768]{1,0:T(8,128)(2,1)} %get-tuple-element.145), channel_id=1, source_target_pairs={{0,1},{1,0},{2,3},{3,2},{4,5},{5,4},{6,7},{7,6},{8,9},{9,8},{10,11... | collective-permute-start | bytes 1179656 | tf_op jit(solution)/shard_map/ppermute | solution.py:743
  205.9 16.4 %collective-permute-start.32 = (bf16[256,768]{1,0:T(8,128)(2,1)}, bf16[256,768]{1,0:T(8,128)(2,1)S(1)}, u32[]{:S(2)}, u32[]{:S(2)}) collective-permute-start(bf16[256,768]{1,0:T(8,128)(2,1)} %get-tuple-element.146), channel_id=1, source_target_pairs={{0,1},{1,0},{2,3},{3,2},{4,5},{5,4},{6,7},{7,6},{8,9},{9,8},{10,11... | collective-permute-start | bytes 1179656 | tf_op jit(solution)/shard_map/ppermute | solution.py:743
  209.6 19.4 %collective-permute-start.33 = (bf16[256,768]{1,0:T(8,128)(2,1)}, bf16[256,768]{1,0:T(8,128)(2,1)S(1)}, u32[]{:S(2)}, u32[]{:S(2)}) collective-permute-start(bf16[256,768]{1,0:T(8,128)(2,1)} %shard_map.270), channel_id=1, source_target_pairs={{0,2},{1,3},{2,0},{3,1},{4,6},{5,7},{6,4},{7,5},{8,10},{9,11},{10,... | collective-permute-start | bytes 1179656 | tf_op jit(solution)/shard_map/ppermute | solution.py:743
  232.1 18.1 %collective-permute-start.36 = (bf16[256,768]{1,0:T(8,128)(2,1)}, bf16[256,768]{1,0:T(8,128)(2,1)S(1)}, u32[]{:S(2)}, u32[]{:S(2)}) collective-permute-start(bf16[256,768]{1,0:T(8,128)(2,1)} %shard_map.272.refs_0_), channel_id=1, source_target_pairs={{0,2},{1,3},{2,0},{3,1},{4,6},{5,7},{6,4},{7,5},{8,10},{9,11},{10,... | collective-permute-start | bytes 1179656 | tf_op jit(solution)/shard_map/ppermute | solution.py:743
  232.1 18.3 %collective-permute-start.35 = (bf16[256,768]{1,0:T(8,128)(2,1)}, bf16[256,768]{1,0:T(8,128)(2,1)S(1)}, u32[]{:S(2)}, u32[]{:S(2)}) collective-permute-start(bf16[256,768]{1,0:T(8,128)(2,1)} %shard_map.272.refs_0_), channel_id=1, source_target_pairs={{0,1},{1,0},{2,3},{3,2},{4,5},{5,4},{6,7},{7,6},{8,9},{9,8},{10,11... | collective-permute-start | bytes 1179656 | tf_op jit(solution)/shard_map/ppermute | solution.py:743
  253.4 12.7 %collective-permute-start.38 = (bf16[2,304,384]{2,1,0:T(8,128)(2,1)S(1)}, bf16[2,304,384]{2,1,0:T(8,128)(2,1)S(1)}, u32[]{:S(2)}, u32[]{:S(2)}) collective-permute-start(bf16[2,304,384]{2,1,0:T(8,128)(2,1)S(1)} %fusion), channel_id=1, source_target_pairs={{0,8},{8,0},{1,9},{9,1},{2,10},{10,2},{3,11},{11,3},{4,12},{12,4},... | collective-permute-start | bytes 1400840 | tf_op jit(solution)/shard_map/ppermute | solution.py:743
  254.7 32.0 %collective-permute-start.37 = (bf16[256,768]{1,0:T(8,128)(2,1)S(1)}, bf16[256,768]{1,0:T(8,128)(2,1)S(1)}, u32[]{:S(2)}, u32[]{:S(2)}) collective-permute-start(bf16[256,768]{1,0:T(8,128)(2,1)S(1)} %collective-permute-done.36.refs_2_), channel_id=1, source_target_pairs={{0,1},{1,0},{2,3},{3,2},{4,5},{5,4},{6,7},{7,6},{8,9},{9,8},{10,11... | collective-permute-start | bytes 1179656 | tf_op jit(solution)/shard_map/ppermute | solution.py:743
  255.3 28.8 %collective-permute-start.47 = (bf16[432,384]{1,0:T(8,128)(2,1)S(1)}, bf16[432,384]{1,0:T(8,128)(2,1)S(1)}, u32[]{:S(2)}, u32[]{:S(2)}) collective-permute-start(bf16[432,384]{1,0:T(8,128)(2,1)S(1)} %get-tuple-element.178), channel_id=1, source_target_pairs={{0,1},{1,0},{2,3},{3,2},{4,5},{5,4},{6,7},{7,6},{8,9},{9,8},{10,11... | collective-permute-start | bytes 995336 | tf_op jit(solution)/shard_map/ppermute | solution.py:743
  263.7 20.4 %collective-permute-start.49 = (bf16[432,384]{1,0:T(8,128)(2,1)S(1)}, bf16[432,384]{1,0:T(8,128)(2,1)S(1)}, u32[]{:S(2)}, u32[]{:S(2)}) collective-permute-start(bf16[432,384]{1,0:T(8,128)(2,1)S(1)} %add_convert_fusion.3), channel_id=1, source_target_pairs={{0,2},{1,3},{2,0},{3,1},{4,6},{5,7},{6,4},{7,5},{8,10},{9,11},{10,... | collective-permute-start | bytes 995336 | tf_op jit(solution)/shard_map/ppermute | solution.py:743
  266.3 20.3 %collective-permute-start.39 = (bf16[304,384]{1,0:T(8,128)(2,1)S(1)}, bf16[304,384]{1,0:T(8,128)(2,1)S(1)}, u32[]{:S(2)}, u32[]{:S(2)}) collective-permute-start(bf16[304,384]{1,0:T(8,128)(2,1)S(1)} %slice_bitcast_fusion.2), channel_id=1, source_target_pairs={{0,16},{16,0},{1,17},{17,1},{2,18},{18,2},{3,19},{19,3},{4,20},{20... | collective-permute-start | bytes 700424 | tf_op jit(solution)/shard_map/ppermute | solution.py:743
  (86 other events, 644.8 us)
Sparse Core Ops, SparseCore 0:
  11.3 78.6 all-gather.3
  122.3 40.1 all-gather.5
  182.0 68.6 reduce-scatter.1
